TPU v7x, 512 devices: a whole 4x8x8 slice. The times are simulated.
512 devices in a mesh: rows: 128 (over z, y, core), cent: 4 (over x).
Axes of the slice: x: 4, y: 8, z: 8, core: 2. Of those that a mesh axis runs over, the one named last changes fastest.
Arguments:
- embeddings: bfloat16 [131072, 768], P('rows'), may hold values from -6 to 6
- centroids: bfloat16 [4096, 768], P('cent'), may hold values from -0.21875 to 0.21875
- positions: int32 [131072], P('rows'), may hold values from 0 to 131071, as said below
- cluster_sizes: int32 [4096], replicated, may hold values from 1 to 1024, 131072 in all
Outputs:
- margin: float32 [131072], P('rows')
- prior_sim: float32 [131072], P(('rows', 'cent'))
Inputs may be any that keep to these rules, and one draw needn't show every extreme that they name: positions is a permutation of the places. Call owner o the places o * 1024 to (o + 1) * 1024 - 1, and quarter c of index r of rows the rows r * 1024 + c * 256 to r * 1024 + (c + 1) * 256 - 1. The number of rows of quarter c of index r with places at owner o is 2 plus a term that depends only on c and on (o - r) modulo 128 and sums to zero over o; it is at most 4, and exactly that for some pair in every draw. `cluster_sizes`: the sizes sum to 131072; the largest is exactly 1024.
All inputs are finite; a program needn't handle non-finite values.
Results may differ from a plain program's by a relative error of at most 0.0012.
Values may be sent and summed in bfloat16 or wider, within the bound.
No kernel may reach another device: no remote copies, remote signals or barrier semaphores. Data moves between devices by JAX's collectives and lax.ppermute only.
A program may use at most 64 MiB of HBM per device.

v0:
```python
import jax
import jax.numpy as jnp
from jax import lax
from jax.sharding import PartitionSpec as P


def joined(shard, axis, combine):
    everything = jax.tree.map(lambda part: lax.all_gather(part, axis), shard)
    initial = jax.tree.map(lambda part: part[0], everything)

    def hop(k, so_far):
        return combine(so_far, jax.tree.map(lambda part: part[k], everything))

    return lax.fori_loop(1, lax.axis_size(axis), hop, initial)


def from_behind(shard, axis, by):
    peers = lax.axis_size(axis)
    pairs = [(i, i + by) for i in range(peers) if 0 <= i + by < peers]
    return lax.ppermute(shard, axis, pairs)


def combine_best(first_pair, second_pair):
    return (jnp.maximum(first_pair[0], second_pair[0]), first_pair[1] + second_pair[1])


def pack_rows(row_data, places, row_count, capacity, block_rows):
    features = row_data.shape[1]
    owners = places // block_rows
    onehot = (owners[:, None] == jnp.arange(row_count, dtype=jnp.int32)[None, :]).astype(jnp.int32)
    ranking = jnp.sum(onehot * jnp.cumsum(onehot, axis=0), axis=1) - 1
    slot_index = owners * capacity + ranking
    buffer = (
        jnp.zeros((row_count * capacity, features), row_data.dtype).at[slot_index].set(row_data)
    )
    send_tags = jnp.full((row_count * capacity,), -1, jnp.int32).at[slot_index].set(places)
    return (buffer.reshape(row_count, capacity, features), send_tags.reshape(row_count, capacity))


def place_rows(row_data, places, first_place, block_rows):
    usable = (places >= 0) & (places - first_place >= 0) & (places - first_place < block_rows)
    target = jnp.where(usable, places - first_place, block_rows)
    empty = jnp.zeros((block_rows, row_data.shape[1]), row_data.dtype)
    return empty.at[target].set(row_data, mode="drop")


def on_device(embeddings, centroids, positions, cluster_sizes):
    block_rows, features = embeddings.shape
    row_count = lax.axis_size("rows")
    cent_count = lax.axis_size("cent")
    quarter_rows = block_rows // cent_count
    slab_size = centroids.shape[0]
    row_index = lax.axis_index("rows")
    cent_index = lax.axis_index("cent")
    floats = embeddings.astype(jnp.float32)
    normed = (floats * lax.rsqrt(jnp.sum(floats * floats, axis=-1, keepdims=True) + 1e-06)).astype(
        jnp.bfloat16
    )
    cluster_ends = jnp.cumsum(cluster_sizes)
    assigned = jnp.searchsorted(cluster_ends, positions, side="right")
    scores = lax.dot_general(
        normed, centroids, (((1,), (1,)), ((), ())), preferred_element_type=jnp.float32
    )
    best_sim = jnp.max(scores, axis=1)
    column = assigned - cent_index * slab_size
    picked = jnp.sum(
        jnp.where(jnp.arange(slab_size, dtype=jnp.int32)[None, :] == column[:, None], scores, 0.0),
        axis=1,
    )
    best_sim, picked = joined((best_sim, picked), "cent", combine_best)
    margin = best_sim - picked
    base_place = row_index * block_rows
    query_places = (
        base_place + cent_index * quarter_rows + jnp.arange(quarter_rows, dtype=jnp.int32)
    )
    query_cluster = jnp.searchsorted(cluster_ends, query_places, side="right")
    send_rows, send_tags = pack_rows(
        normed, positions, row_count, 2 * block_rows // row_count, block_rows
    )
    got_rows, got_tags = (
        lax.all_to_all(send_rows, "rows", split_axis=0, concat_axis=0, tiled=True),
        lax.all_to_all(send_tags, "rows", split_axis=0, concat_axis=0, tiled=True),
    )
    own_block = place_rows(
        got_rows.reshape(-1, features), got_tags.reshape(-1), base_place, block_rows
    )
    prev_block = from_behind(own_block, "rows", 1)
    queries = lax.dynamic_slice_in_dim(own_block, cent_index * quarter_rows, quarter_rows, 0)
    keys_all = jnp.concatenate([prev_block, own_block], axis=0)
    key_places = base_place - block_rows + jnp.arange(2 * block_rows, dtype=jnp.int32)
    key_cluster = jnp.searchsorted(cluster_ends, key_places, side="right")
    similarity = lax.dot_general(
        queries, keys_all, (((1,), (1,)), ((), ())), preferred_element_type=jnp.float32
    )
    allowed = (
        (key_cluster[None, :] == query_cluster[:, None])
        & (key_places[None, :] < query_places[:, None])
        & (key_places[None, :] >= 0)
    )
    prior_sim = jnp.max(jnp.where(allowed, similarity, -1.0), axis=1)
    return (margin, prior_sim)


def solution(mesh):
    in_specs = (P("rows", None), P("cent", None), P("rows"), P())
    out_specs = (P("rows"), P(("rows", "cent")))
    return jax.shard_map(
        on_device, mesh=mesh, in_specs=in_specs, out_specs=out_specs, check_vma=False
    )
```

profile of v0, /device:TPU:2, one launch (start us, length us, event | category | flops | bytes accessed | tf_op | source)
XLA Modules:
  0.0 354.2 jit_solution(16766934843961250471)
XLA Ops:
  9.3 17.8 %all-to-all-start = ((s32[128,1,16]{2,1,0:T(1,128)}), s32[128,1,16]{2,1,0:T(1,128)S(1)}, u32[]{:S(2)}, u32[]{:S(2)}) async-start(s32[128,1,16]{2,1,0:T(1,128)} %bitcast.8), calls=%async_computation | async-start | bytes 131072 | tf_op jit(solution)/shard_map/all_to_all | solution.py:82
  28.1 154.3 %while.91 = (s32[]{:T(128)}, u32[2048]{0:T(1024)S(1)}, u32[2048]{0:T(1024)S(1)}, s32[4096]{0:T(1024)S(1)}, s32[]{:T(128)}, /*index=5*/s32[]{:T(128)}, s32[]{:T(128)}, s32[]{}) while((s32[]{:T(128)}, u32[2048]{0:T(1024)S(1)}, u32[2048]{0:T(1024)S(1)}, s32[4096]{0:T(1024)S(1)}, s32[]{:T(128)}, /*index=5*/s32[]{:T(128)}, ...), condition=%wide.region_10.11_spmd.clone, body=%wide.region_9.10_spmd.clone.sunk | while | flops 40964 | bytes 127089 | solution.py:91
  28.1 11.8 %gather_fusion.1 = s32[2048]{0:T(1024)S(1)} fusion(s32[4096]{0:T(1024)S(1)} %get-tuple-element.654, u32[2048]{0:T(1024)S(1)} %broadcast_clamp_fusion.5), kind=kCustom, calls=%fused_computation.1.clone.clone.1 | custom fusion | bytes 24576 | tf_op jit(solution)/shard_map/jit(searchsorted)/jit(_searchsorted_scan_impl)/vmap(jit(_searchsorted_scan_impl))/while/body/eval_jaxpr/gather | solution.py:91
  40.0 11.8 %gather_fusion.1 = s32[2048]{0:T(1024)S(1)} fusion(s32[4096]{0:T(1024)S(1)} %get-tuple-element.654, u32[2048]{0:T(1024)S(1)} %broadcast_clamp_fusion.5), kind=kCustom, calls=%fused_computation.1.clone.clone.1 | custom fusion | bytes 24576 | tf_op jit(solution)/shard_map/jit(searchsorted)/jit(_searchsorted_scan_impl)/vmap(jit(_searchsorted_scan_impl))/while/body/eval_jaxpr/gather | solution.py:91
  51.9 11.8 %gather_fusion.1 = s32[2048]{0:T(1024)S(1)} fusion(s32[4096]{0:T(1024)S(1)} %get-tuple-element.654, u32[2048]{0:T(1024)S(1)} %broadcast_clamp_fusion.5), kind=kCustom, calls=%fused_computation.1.clone.clone.1 | custom fusion | bytes 24576 | tf_op jit(solution)/shard_map/jit(searchsorted)/jit(_searchsorted_scan_impl)/vmap(jit(_searchsorted_scan_impl))/while/body/eval_jaxpr/gather | solution.py:91
  63.7 11.8 %gather_fusion.1 = s32[2048]{0:T(1024)S(1)} fusion(s32[4096]{0:T(1024)S(1)} %get-tuple-element.654, u32[2048]{0:T(1024)S(1)} %broadcast_clamp_fusion.5), kind=kCustom, calls=%fused_computation.1.clone.clone.1 | custom fusion | bytes 24576 | tf_op jit(solution)/shard_map/jit(searchsorted)/jit(_searchsorted_scan_impl)/vmap(jit(_searchsorted_scan_impl))/while/body/eval_jaxpr/gather | solution.py:91
  75.6 11.8 %gather_fusion.1 = s32[2048]{0:T(1024)S(1)} fusion(s32[4096]{0:T(1024)S(1)} %get-tuple-element.654, u32[2048]{0:T(1024)S(1)} %broadcast_clamp_fusion.5), kind=kCustom, calls=%fused_computation.1.clone.clone.1 | custom fusion | bytes 24576 | tf_op jit(solution)/shard_map/jit(searchsorted)/jit(_searchsorted_scan_impl)/vmap(jit(_searchsorted_scan_impl))/while/body/eval_jaxpr/gather | solution.py:91
  87.5 11.8 %gather_fusion.1 = s32[2048]{0:T(1024)S(1)} fusion(s32[4096]{0:T(1024)S(1)} %get-tuple-element.654, u32[2048]{0:T(1024)S(1)} %broadcast_clamp_fusion.5), kind=kCustom, calls=%fused_computation.1.clone.clone.1 | custom fusion | bytes 24576 | tf_op jit(solution)/shard_map/jit(searchsorted)/jit(_searchsorted_scan_impl)/vmap(jit(_searchsorted_scan_impl))/while/body/eval_jaxpr/gather | solution.py:91
  99.3 11.8 %gather_fusion.1 = s32[2048]{0:T(1024)S(1)} fusion(s32[4096]{0:T(1024)S(1)} %get-tuple-element.654, u32[2048]{0:T(1024)S(1)} %broadcast_clamp_fusion.5), kind=kCustom, calls=%fused_computation.1.clone.clone.1 | custom fusion | bytes 24576 | tf_op jit(solution)/shard_map/jit(searchsorted)/jit(_searchsorted_scan_impl)/vmap(jit(_searchsorted_scan_impl))/while/body/eval_jaxpr/gather | solution.py:91
  111.2 11.8 %gather_fusion.1 = s32[2048]{0:T(1024)S(1)} fusion(s32[4096]{0:T(1024)S(1)} %get-tuple-element.654, u32[2048]{0:T(1024)S(1)} %broadcast_clamp_fusion.5), kind=kCustom, calls=%fused_computation.1.clone.clone.1 | custom fusion | bytes 24576 | tf_op jit(solution)/shard_map/jit(searchsorted)/jit(_searchsorted_scan_impl)/vmap(jit(_searchsorted_scan_impl))/while/body/eval_jaxpr/gather | solution.py:91
  123.1 11.8 %gather_fusion.1 = s32[2048]{0:T(1024)S(1)} fusion(s32[4096]{0:T(1024)S(1)} %get-tuple-element.654, u32[2048]{0:T(1024)S(1)} %broadcast_clamp_fusion.5), kind=kCustom, calls=%fused_computation.1.clone.clone.1 | custom fusion | bytes 24576 | tf_op jit(solution)/shard_map/jit(searchsorted)/jit(_searchsorted_scan_impl)/vmap(jit(_searchsorted_scan_impl))/while/body/eval_jaxpr/gather | solution.py:91
  134.9 11.8 %gather_fusion.1 = s32[2048]{0:T(1024)S(1)} fusion(s32[4096]{0:T(1024)S(1)} %get-tuple-element.654, u32[2048]{0:T(1024)S(1)} %broadcast_clamp_fusion.5), kind=kCustom, calls=%fused_computation.1.clone.clone.1 | custom fusion | bytes 24576 | tf_op jit(solution)/shard_map/jit(searchsorted)/jit(_searchsorted_scan_impl)/vmap(jit(_searchsorted_scan_impl))/while/body/eval_jaxpr/gather | solution.py:91
  146.8 11.8 %gather_fusion.1 = s32[2048]{0:T(1024)S(1)} fusion(s32[4096]{0:T(1024)S(1)} %get-tuple-element.654, u32[2048]{0:T(1024)S(1)} %broadcast_clamp_fusion.5), kind=kCustom, calls=%fused_computation.1.clone.clone.1 | custom fusion | bytes 24576 | tf_op jit(solution)/shard_map/jit(searchsorted)/jit(_searchsorted_scan_impl)/vmap(jit(_searchsorted_scan_impl))/while/body/eval_jaxpr/gather | solution.py:91
  158.7 11.8 %gather_fusion.1 = s32[2048]{0:T(1024)S(1)} fusion(s32[4096]{0:T(1024)S(1)} %get-tuple-element.654, u32[2048]{0:T(1024)S(1)} %broadcast_clamp_fusion.5), kind=kCustom, calls=%fused_computation.1.clone.clone.1 | custom fusion | bytes 24576 | tf_op jit(solution)/shard_map/jit(searchsorted)/jit(_searchsorted_scan_impl)/vmap(jit(_searchsorted_scan_impl))/while/body/eval_jaxpr/gather | solution.py:91
  170.5 11.8 %gather_fusion.1 = s32[2048]{0:T(1024)S(1)} fusion(s32[4096]{0:T(1024)S(1)} %get-tuple-element.654, u32[2048]{0:T(1024)S(1)} %broadcast_clamp_fusion.5), kind=kCustom, calls=%fused_computation.1.clone.clone.1 | custom fusion | bytes 24576 | tf_op jit(solution)/shard_map/jit(searchsorted)/jit(_searchsorted_scan_impl)/vmap(jit(_searchsorted_scan_impl))/while/body/eval_jaxpr/gather | solution.py:91
  182.4 7.8 %scatter_custom_fusion.1 = bf16[2048,768]{1,0:T(8,128)(2,1)} fusion(s32[1024]{0:T(1024)S(1)} %compare_select_fusion.1, bf16[]{:T(256)} %constant.174.clone.1, bf16[1024,768]{1,0:T(8,128)(2,1)S(1)} %copy-done.1, f32[1024]{0:T(1024)S(1)} %add_rsqrt_fusion), kind=kCustom, calls=%fused_computation.37 | custom fusion | flops 2359296 | bytes 4722690 | tf_op jit(solution)/shard_map/scatter | solution.py:34
  190.2 14.4 %all-to-all-start.1 = ((bf16[128,16,768]{2,1,0:T(8,128)(2,1)}), bf16[128,16,768]{2,1,0:T(8,128)(2,1)}, u32[]{:S(2)}, u32[]{:S(2)}) async-start(bf16[128,16,768]{2,1,0:T(8,128)(2,1)} %bitcast.24), calls=%async_computation.1 | async-start | bytes 6291456 | tf_op jit(solution)/shard_map/all_to_all | solution.py:81
  204.6 81.1 %while.90 = (s32[]{:T(128)}, u32[1024]{0:T(1024)S(1)}, u32[1024]{0:T(1024)S(1)}, s32[4096]{0:T(1024)S(1)}, s32[1024]{0:T(1024)S(1)}, /*index=5*/s32[]{:T(128)}, s32[]{:T(128)}, s32[]{}) while((s32[]{:T(128)}, u32[1024]{0:T(1024)S(1)}, u32[1024]{0:T(1024)S(1)}, s32[4096]{0:T(1024)S(1)}, s32[1024]{0:T(1024)S(1)}, ...), condition=%wide.region_5.6_spmd.clone, body=%wide.region_4.5_spmd.clone.sunk | while | flops 19460 | bytes 67693 | solution.py:60
  204.6 6.2 %gather_fusion = s32[1024]{0:T(1024)S(1)} fusion(s32[4096]{0:T(1024)S(1)} %get-tuple-element.606, u32[1024]{0:T(1024)S(1)} %broadcast_clamp_fusion.4), kind=kCustom, calls=%fused_computation.clone.clone.1 | custom fusion | bytes 12288 | tf_op jit(solution)/shard_map/jit(searchsorted)/jit(_searchsorted_scan_impl)/vmap(jit(_searchsorted_scan_impl))/while/body/eval_jaxpr/gather | solution.py:60
  210.9 6.2 %gather_fusion = s32[1024]{0:T(1024)S(1)} fusion(s32[4096]{0:T(1024)S(1)} %get-tuple-element.606, u32[1024]{0:T(1024)S(1)} %broadcast_clamp_fusion.4), kind=kCustom, calls=%fused_computation.clone.clone.1 | custom fusion | bytes 12288 | tf_op jit(solution)/shard_map/jit(searchsorted)/jit(_searchsorted_scan_impl)/vmap(jit(_searchsorted_scan_impl))/while/body/eval_jaxpr/gather | solution.py:60
  217.1 6.2 %gather_fusion = s32[1024]{0:T(1024)S(1)} fusion(s32[4096]{0:T(1024)S(1)} %get-tuple-element.606, u32[1024]{0:T(1024)S(1)} %broadcast_clamp_fusion.4), kind=kCustom, calls=%fused_computation.clone.clone.1 | custom fusion | bytes 12288 | tf_op jit(solution)/shard_map/jit(searchsorted)/jit(_searchsorted_scan_impl)/vmap(jit(_searchsorted_scan_impl))/while/body/eval_jaxpr/gather | solution.py:60
  223.3 6.2 %gather_fusion = s32[1024]{0:T(1024)S(1)} fusion(s32[4096]{0:T(1024)S(1)} %get-tuple-element.606, u32[1024]{0:T(1024)S(1)} %broadcast_clamp_fusion.4), kind=kCustom, calls=%fused_computation.clone.clone.1 | custom fusion | bytes 12288 | tf_op jit(solution)/shard_map/jit(searchsorted)/jit(_searchsorted_scan_impl)/vmap(jit(_searchsorted_scan_impl))/while/body/eval_jaxpr/gather | solution.py:60
  235.8 6.2 %gather_fusion = s32[1024]{0:T(1024)S(1)} fusion(s32[4096]{0:T(1024)S(1)} %get-tuple-element.606, u32[1024]{0:T(1024)S(1)} %broadcast_clamp_fusion.4), kind=kCustom, calls=%fused_computation.clone.clone.1 | custom fusion | bytes 12288 | tf_op jit(solution)/shard_map/jit(searchsorted)/jit(_searchsorted_scan_impl)/vmap(jit(_searchsorted_scan_impl))/while/body/eval_jaxpr/gather | solution.py:60
  242.0 6.2 %gather_fusion = s32[1024]{0:T(1024)S(1)} fusion(s32[4096]{0:T(1024)S(1)} %get-tuple-element.606, u32[1024]{0:T(1024)S(1)} %broadcast_clamp_fusion.4), kind=kCustom, calls=%fused_computation.clone.clone.1 | custom fusion | bytes 12288 | tf_op jit(solution)/shard_map/jit(searchsorted)/jit(_searchsorted_scan_impl)/vmap(jit(_searchsorted_scan_impl))/while/body/eval_jaxpr/gather | solution.py:60
  248.3 6.2 %gather_fusion = s32[1024]{0:T(1024)S(1)} fusion(s32[4096]{0:T(1024)S(1)} %get-tuple-element.606, u32[1024]{0:T(1024)S(1)} %broadcast_clamp_fusion.4), kind=kCustom, calls=%fused_computation.clone.clone.1 | custom fusion | bytes 12288 | tf_op jit(solution)/shard_map/jit(searchsorted)/jit(_searchsorted_scan_impl)/vmap(jit(_searchsorted_scan_impl))/while/body/eval_jaxpr/gather | solution.py:60
  254.5 6.2 %gather_fusion = s32[1024]{0:T(1024)S(1)} fusion(s32[4096]{0:T(1024)S(1)} %get-tuple-element.606, u32[1024]{0:T(1024)S(1)} %broadcast_clamp_fusion.4), kind=kCustom, calls=%fused_computation.clone.clone.1 | custom fusion | bytes 12288 | tf_op jit(solution)/shard_map/jit(searchsorted)/jit(_searchsorted_scan_impl)/vmap(jit(_searchsorted_scan_impl))/while/body/eval_jaxpr/gather | solution.py:60
  260.8 6.2 %gather_fusion = s32[1024]{0:T(1024)S(1)} fusion(s32[4096]{0:T(1024)S(1)} %get-tuple-element.606, u32[1024]{0:T(1024)S(1)} %broadcast_clamp_fusion.4), kind=kCustom, calls=%fused_computation.clone.clone.1 | custom fusion | bytes 12288 | tf_op jit(solution)/shard_map/jit(searchsorted)/jit(_searchsorted_scan_impl)/vmap(jit(_searchsorted_scan_impl))/while/body/eval_jaxpr/gather | solution.py:60
  267.0 6.2 %gather_fusion = s32[1024]{0:T(1024)S(1)} fusion(s32[4096]{0:T(1024)S(1)} %get-tuple-element.606, u32[1024]{0:T(1024)S(1)} %broadcast_clamp_fusion.4), kind=kCustom, calls=%fused_computation.clone.clone.1 | custom fusion | bytes 12288 | tf_op jit(solution)/shard_map/jit(searchsorted)/jit(_searchsorted_scan_impl)/vmap(jit(_searchsorted_scan_impl))/while/body/eval_jaxpr/gather | solution.py:60
  286.3 11.4 %scatter_custom_fusion.2 = bf16[1024,768]{1,0:T(8,128)(2,1)} fusion(s32[2048]{0:T(1024)S(1)} %bitcast.28, bf16[2048,768]{1,0:T(8,128)(2,1)} %bitcast.11, bf16[]{:T(256)} %constant.174.clone.1), kind=kCustom, calls=%fused_computation.40 | custom fusion | bytes 1573376 | tf_op jit(solution)/shard_map/scatter | solution.py:44
  300.2 23.3 %while.92 = (s32[]{:T(128)}, u32[256]{0:T(256)S(1)}, u32[256]{0:T(256)S(1)}, s32[4096]{0:T(1024)S(1)}, s32[]{:T(128)}, /*index=5*/s32[]{:T(128)}, s32[]{:T(128)}, s32[]{}) while((s32[]{:T(128)}, u32[256]{0:T(256)S(1)}, u32[256]{0:T(256)S(1)}, s32[4096]{0:T(1024)S(1)}, s32[]{:T(128)}, /*index=5*/s32[]{:T(128)}, s32[]{:T(128)}, ...), condition=%wide.region_12.13_spmd.clone, body=%wide.region_11.12_spmd.clone.sunk | while | flops 4612 | bytes 16496 | solution.py:76
  325.6 12.0 %all-gather = f32[4096]{0:T(1024)S(1)} all-gather(f32[1024]{0:T(1024)S(1)} %get-tuple-element.396), channel_id=2, replica_groups=mesh['rows'=128,'cent'=4] {'cent'}, dimensions={0}, use_global_device_ids=true | all-gather | bytes 20480 | tf_op jit(solution)/shard_map/all_gather | solution.py:8
  337.6 11.9 %all-gather.1 = f32[4096]{0:T(1024)S(1)} all-gather(f32[1024]{0:T(1024)S(1)} %get-tuple-element.395), channel_id=3, replica_groups=mesh['rows'=128,'cent'=4] {'cent'}, dimensions={0}, use_global_device_ids=true | all-gather | bytes 20480 | tf_op jit(solution)/shard_map/all_gather | solution.py:8
  (226 shorter events, 61.4 us)
Async XLA Ops:
  0.6 322.8 %copy-start = (bf16[1024,768]{1,0:T(8,128)(2,1)S(1)}, bf16[1024,768]{1,0:T(8,128)(2,1)}, u32[]{:S(2)}) copy-start(bf16[1024,768]{1,0:T(8,128)(2,1)} %param.13) | copy-start | bytes 4718596
  0.6 3.6 %copy-start.3 = (s32[1024]{0:T(1024)S(1)}, s32[1024]{0:T(1024)}, u32[]{:S(2)}) copy-start(s32[1024]{0:T(1024)} %param.14) | copy-start | bytes 12292
  0.7 26.5 %copy-start.1 = (bf16[1024,768]{1,0:T(8,128)(2,1)S(1)}, bf16[1024,768]{1,0:T(8,128)(2,1)}, u32[]{:S(2)}) copy-start(bf16[1024,768]{1,0:T(8,128)(2,1)} %param.12) | copy-start | bytes 4718596
  1.8 0.8 copy-start.2
  2.6 24.9 %copy-start.4 = (s32[4096]{0:T(1024)S(1)}, s32[4096]{0:T(1024)}, u32[]{:S(2)}) copy-start(s32[4096]{0:T(1024)} %param.15) | copy-start | bytes 49156
  9.3 180.9 %all-to-all-start = ((s32[128,1,16]{2,1,0:T(1,128)}), s32[128,1,16]{2,1,0:T(1,128)S(1)}, u32[]{:S(2)}, u32[]{:S(2)}) async-start(s32[128,1,16]{2,1,0:T(1,128)} %bitcast.8), calls=%async_computation | async-start | bytes 131072 | tf_op jit(solution)/shard_map/all_to_all | solution.py:82
  190.2 96.1 %all-to-all-start.1 = ((bf16[128,16,768]{2,1,0:T(8,128)(2,1)}), bf16[128,16,768]{2,1,0:T(8,128)(2,1)}, u32[]{:S(2)}, u32[]{:S(2)}) async-start(bf16[128,16,768]{2,1,0:T(8,128)(2,1)} %bitcast.24), calls=%async_computation.1 | async-start | bytes 6291456 | tf_op jit(solution)/shard_map/all_to_all | solution.py:81
  297.7 52.6 %collective-permute-start = (bf16[1024,768]{1,0:T(8,128)(2,1)}, bf16[1024,768]{1,0:T(8,128)(2,1)}, u32[]{:S(2)}, u32[]{:S(2)}) collective-permute-start(bf16[1024,768]{1,0:T(8,128)(2,1)} %scatter_custom_fusion.2), channel_id=1, source_target_pairs={{0,4},{4,8},{8,12},{12,16},{16,20},{20,24},{24,28},{28,32},{32,36}... | collective-permute-start | bytes 4718600 | tf_op jit(solution)/shard_map/ppermute | solution.py:20
where the time goes:
time: 354 us
  local copies, waits for them, and re-layouts  274 us (77%)
  starting transfers between devices  34.6 us (10%)
  blocking collectives  23.9 us (7%)
  other arithmetic  13.3 us (4%)
  matrix products  5.86 us (2%)
    gather x13, local copies, waits for them, and re-layouts, on_device(): key_cluster = jnp.searchsorted(cluster_ends, key_places, side='right')  153 us
    gather x13, local copies, waits for them, and re-layouts, on_device(): assigned = jnp.searchsorted(cluster_ends, positions, side='right')  80 us
    all_gather x2, blocking collectives, joined(): everything = jax.tree.map(lambda part: lax.all_gather(part, axis), shard)  23.9 us
    gather x13, local copies, waits for them, and re-layouts, on_device(): query_cluster = jnp.searchsorted(cluster_ends, query_places, side='right')  22.4 us
    all_to_all x1, starting transfers between devices, on_device(): lax.all_to_all(send_tags, 'rows', split_axis=0, concat_axis=0, tiled=True)  17.8 us
    all_to_all x1, starting transfers between devices, on_device(): lax.all_to_all(send_rows, 'rows', split_axis=0, concat_axis=0, tiled=True)  14.4 us
    scatter x1, local copies, waits for them, and re-layouts, place_rows(): return empty.at[target].set(row_data, mode='drop')  11.4 us
    scatter x1, other arithmetic, pack_rows(): jnp.zeros((row_count * capacity, features), row_data.dtype).at[slot_index]  7.76 us
  transfers between devices with their start and end apart: 3, of which 0 were waited for; matrix products, arithmetic and copies ran while one was open for 76% of the time, Pallas kernels for 0%

commit v1 on v0

v1 whole, which is shorter than its diff:
```python
import jax
import jax.numpy as jnp
from jax import lax
from jax.experimental import pallas as pl
from jax.experimental.pallas import tpu as pltpu
from jax.sharding import PartitionSpec as P

SLOTS = 4
LANES = 128
TAG_BASE = 32
TAG_ROWS = 8


def rotated(shard, axis, by):
    peers = lax.axis_size(axis)
    return lax.ppermute(shard, axis, [(i, (i + by) % peers) for i in range(peers)])


def iota(shape, dim):
    return lax.broadcasted_iota(jnp.int32, shape, dim)


def as_column(row):
    size = row.shape[1]
    eye = iota((size, size), 0) == iota((size, size), 1)
    return jnp.sum(jnp.where(eye, row, jnp.zeros_like(row)), axis=1, keepdims=True)


def as_row(column):
    size = column.shape[0]
    eye = iota((size, size), 0) == iota((size, size), 1)
    return jnp.sum(jnp.where(eye, column, jnp.zeros_like(column)), axis=0, keepdims=True)


def dot(left, right, left_dim, right_dim):
    return lax.dot_general(
        left, right, (((left_dim,), (right_dim,)), ((), ())), preferred_element_type=jnp.float32
    )


def normalise(rows):
    floats = rows.astype(jnp.float32)
    return (floats * lax.rsqrt(jnp.sum(floats * floats, axis=-1, keepdims=True) + 1e-06)).astype(
        jnp.bfloat16
    )


def pack_kernel(cent_ref, rows_ref, places_ref, out_ref, *, owner_rows):
    normed = normalise(rows_ref[...])
    count, features = normed.shape
    slots = out_ref.shape[0]
    places = places_ref[0]
    owners = places // owner_rows
    owner_column = as_column(owners)
    earlier = (owner_column == owners) & (iota((count, count), 0) < iota((count, count), 1))
    rank = jnp.sum(earlier.astype(jnp.int32), axis=0, keepdims=True)
    slot = owners * SLOTS + rank
    chosen = (iota((slots, count), 0) == slot).astype(jnp.bfloat16)
    local = as_column(places % owner_rows)
    lane = iota((count, LANES), 1)
    tags = jnp.where(lane == 0, local // TAG_BASE + 1, jnp.where(lane == 1, local % TAG_BASE, 0))
    tags = tags.astype(jnp.float32).astype(jnp.bfloat16)
    out_ref[:, :features] = dot(chosen, normed, 1, 0).astype(jnp.bfloat16)
    out_ref[:, features:] = dot(chosen, tags, 1, 0).astype(jnp.bfloat16)


def pack(rows, places, cent_index, owners, owner_rows, quarters):
    count, features = rows.shape
    quarter = count // quarters
    slots = owners * SLOTS
    return pl.pallas_call(
        lambda *refs: pack_kernel(*refs, owner_rows=owner_rows),
        grid_spec=pltpu.PrefetchScalarGridSpec(
            num_scalar_prefetch=1,
            grid=(1,),
            in_specs=[
                pl.BlockSpec((quarter, features), lambda i, cent: (cent[0], 0)),
                pl.BlockSpec((1, 1, quarter), lambda i, cent: (cent[0], 0, 0)),
            ],
            out_specs=pl.BlockSpec((slots, features + LANES), lambda i, cent: (0, 0)),
        ),
        out_shape=jax.ShapeDtypeStruct((slots, features + LANES), jnp.bfloat16),
        name="pack",
    )(cent_index[None], rows, places.reshape(quarters, 1, quarter))


def compact_kernel(got_ref, out_ref):
    slots = got_ref.shape[0]
    features = out_ref.shape[1]
    count = out_ref.shape[0] - TAG_ROWS
    tags = got_ref[:, features:].astype(jnp.float32)
    high = tags[:, 0:1]
    low = tags[:, 1:2]
    filled = high > 0.5
    before = (iota((slots, slots), 1) < iota((slots, slots), 0)).astype(jnp.bfloat16)
    marks = jnp.broadcast_to(filled.astype(jnp.float32), (slots, LANES)).astype(jnp.bfloat16)
    rank = dot(before, marks, 1, 0)[:, 0:1].astype(jnp.int32)
    chosen = (rank == iota((slots, count), 1)) & filled
    out_ref[:count, :] = dot(
        chosen.astype(jnp.bfloat16), got_ref[:, :features], 0, 0
    ).astype(jnp.bfloat16)
    high_row = jnp.sum(jnp.where(chosen, high - 1.0, 0.0), axis=0, keepdims=True)
    low_row = jnp.sum(jnp.where(chosen, low, 0.0), axis=0, keepdims=True)
    spare = jnp.zeros((1, features - 2 * count), jnp.float32)
    row = jnp.concatenate([high_row, low_row, spare], axis=1)
    out_ref[count:, :] = jnp.broadcast_to(row, (TAG_ROWS, features)).astype(jnp.bfloat16)


def compact(got, count, features):
    return pl.pallas_call(
        compact_kernel,
        out_shape=jax.ShapeDtypeStruct((count + TAG_ROWS, features), jnp.bfloat16),
        name="compact",
    )(got)


def key_places(part_ref, count):
    tags = part_ref[count:, :].astype(jnp.float32)
    row = tags[0:1, :count] * float(TAG_BASE) + tags[0:1, count : 2 * count]
    return as_column(row.astype(jnp.int32))


def own_kernel(first_ref, starts_ref, *refs):
    *part_refs, queries_ref, best_ref = refs
    count = queries_ref.shape[0]
    query_places = first_ref[0] + iota((1, count), 1)
    starts = starts_ref[...]
    columns = [key_places(part, count) for part in part_refs]
    queries = jnp.zeros(queries_ref.shape, jnp.float32)
    for column, part in zip(columns, part_refs):
        chosen = (column == query_places).astype(jnp.bfloat16)
        queries = queries + dot(chosen, part[:count, :], 0, 0)
    queries = queries.astype(jnp.bfloat16)
    queries_ref[...] = queries
    best = jnp.full((1, count), -1.0, jnp.float32)
    for column, part in zip(columns, part_refs):
        similarity = dot(part[:count, :], queries, 1, 1)
        allowed = (column >= starts) & (column < query_places)
        masked = jnp.where(allowed, similarity, -1.0)
        best = jnp.maximum(best, jnp.max(masked, axis=0, keepdims=True))
    best_ref[...] = best


def previous_kernel(starts_ref, best_ref, queries_ref, *refs, owner_rows):
    *part_refs, out_ref = refs
    count = queries_ref.shape[0]
    starts = starts_ref[...]
    queries = queries_ref[...]
    best = best_ref[...]
    for part in part_refs:
        column = key_places(part, count) - owner_rows
        similarity = dot(part[:count, :], queries, 1, 1)
        masked = jnp.where(column >= starts, similarity, -1.0)
        best = jnp.maximum(best, jnp.max(masked, axis=0, keepdims=True))
    out_ref[...] = best


def on_device(embeddings, centroids, positions, cluster_sizes):
    block_rows, features = embeddings.shape
    row_count = lax.axis_size("rows")
    cent_count = lax.axis_size("cent")
    quarter = block_rows // cent_count
    slab_size = centroids.shape[0]
    row_index = lax.axis_index("rows")
    cent_index = lax.axis_index("cent")

    packed = pack(embeddings, positions, cent_index, row_count, block_rows, cent_count)
    got = lax.all_to_all(
        packed.reshape(row_count, SLOTS, -1), "rows", split_axis=0, concat_axis=0, tiled=True
    )

    cluster_ends = jnp.cumsum(cluster_sizes)
    cluster_starts = cluster_ends - cluster_sizes
    slab_ends = lax.dynamic_slice_in_dim(cluster_ends, cent_index * slab_size, slab_size)
    slab_starts = lax.dynamic_slice_in_dim(cluster_starts, cent_index * slab_size, slab_size)
    scores = lax.dot_general(
        normalise(embeddings),
        centroids,
        (((1,), (1,)), ((), ())),
        preferred_element_type=jnp.float32,
    )
    best_sim = jnp.max(scores, axis=1)
    assigned = (slab_starts[None, :] <= positions[:, None]) & (
        positions[:, None] < slab_ends[None, :]
    )
    picked = jnp.sum(jnp.where(assigned, scores, 0.0), axis=1)
    both = jnp.stack([best_sim, picked])
    for both_there in [rotated(both, "cent", by) for by in range(1, cent_count)]:
        best_sim = jnp.maximum(best_sim, both_there[0])
        picked = picked + both_there[1]
    margin = best_sim - picked

    base_place = row_index * block_rows
    first_local = cent_index * quarter
    query_places = base_place + first_local + jnp.arange(quarter, dtype=jnp.int32)
    started = jnp.where(cluster_starts[None, :] <= query_places[:, None], cluster_starts[None, :], 0)
    query_starts = (jnp.max(started, axis=1) - base_place)[None, :]

    mine = compact(got.reshape(row_count * SLOTS, -1), quarter, features)
    own_parts = [mine] + [rotated(mine, "cent", by) for by in (1, 3, 2)]
    previous_parts = [rotated(part, "rows", 1) for part in own_parts]
    queries, own_best = pl.pallas_call(
        own_kernel,
        in_specs=[pl.BlockSpec(memory_space=pltpu.SMEM)]
        + [pl.BlockSpec(memory_space=pltpu.VMEM)] * (1 + cent_count),
        out_shape=(
            jax.ShapeDtypeStruct((quarter, features), jnp.bfloat16),
            jax.ShapeDtypeStruct((1, quarter), jnp.float32),
        ),
        name="own",
    )(first_local[None], query_starts, *own_parts)
    prior_sim = pl.pallas_call(
        lambda *refs: previous_kernel(*refs, owner_rows=block_rows),
        out_shape=jax.ShapeDtypeStruct((1, quarter), jnp.float32),
        name="previous",
    )(query_starts, own_best, queries, *previous_parts)
    return (margin, prior_sim.reshape(quarter))


def solution(mesh):
    in_specs = (P("rows", None), P("cent", None), P("rows"), P())
    out_specs = (P("rows"), P(("rows", "cent")))
    return jax.shard_map(
        on_device, mesh=mesh, in_specs=in_specs, out_specs=out_specs, check_vma=False
    )
```

time: 354 us -> 104 us (0.29)
  the two profiles are of different devices: /device:TPU:2 before, /device:TPU:6 now
where the time goes in v1:
time: 104 us; the launch traced here: 103 us
  starting transfers between devices  46.2 us (44%)
  waiting for transfers between devices  33.6 us (32%)
  Pallas kernels  11.9 us (11%)
  local copies, waits for them, and re-layouts  5.99 us (6%)
  other arithmetic  2.71 us (3%)
  matrix products  2.09 us (2%)
    ppermute x10, starting transfers between devices, rotated(): lax.ppermute(shard, axis, [(i, (i + by) % peers) for i in range(peers)])  27.8 us
    ppermute x10, waiting for transfers between devices, rotated(): lax.ppermute(shard, axis, [(i, (i + by) % peers) for i in range(peers)])  20.8 us
    all_to_all x1, starting transfers between devices, on_device(): lax.all_to_all(packed.reshape(row_count, SLOTS, -1), 'rows', split_axis=0...  18.4 us
    all_to_all x1, waiting for transfers between devices, on_device(): lax.all_to_all(packed.reshape(row_count, SLOTS, -1), 'rows', split_axis=0...  12.8 us
    pallas_call x1, Pallas kernels, on_device(): pl.pallas_call(own_kernel, in_specs=[pl.BlockSpec(memory_space=pltpu.SMEM...  3.58 us
    pallas_call x1, Pallas kernels, compact(): pl.pallas_call(compact_kernel, out_shape=jax.ShapeDtypeStruct((count + TA...  2.87 us
    pallas_call x1, Pallas kernels, pack(): pl.pallas_call(lambda *refs: pack_kernel(*refs, owner_rows=owner_rows), g...  2.76 us
    pallas_call x1, Pallas kernels, on_device(): pl.pallas_call(lambda *refs: previous_kernel(*refs, owner_rows=block_rows...  2.69 us
  transfers between devices with their start and end apart: 11, of which 5 were waited for; matrix products, arithmetic and copies ran while one was open for 7% of the time, Pallas kernels for 6%

profile of v1, /device:TPU:6, one launch (start us, length us, event | category | flops | bytes accessed | tf_op | source)
XLA Modules:
  0.0 103.4 jit_solution(5920071643121062075)
XLA Ops:
  0.6 2.8 %pack.1 = bf16[512,896]{1,0:T(8,128)(2,1)} custom-call(s32[1]{0:T(128)} %bitcast.12.refs_0_, bf16[1024,768]{1,0:T(8,128)(2,1)} %refs_1_.1, s32[4,1,256]{2,1,0:T(1,128)} %bitcast.29), custom_call_target="tpu_custom_call" | custom-call | tf_op jit(solution)/shard_map/pack/pallas_call | solution.py:71
  3.4 2.6 %reshape.56 = bf16[128,4,896]{2,1,0:T(4,128)(2,1)} reshape(bf16[512,896]{1,0:T(8,128)(2,1)} %pack.1) | data formatting | bytes 1835008 | tf_op jit(solution)/shard_map/reshape | solution.py:169
  6.0 18.4 %all-to-all-start = ((bf16[128,4,896]{2,1,0:T(4,128)(2,1)}), bf16[128,4,896]{2,1,0:T(4,128)(2,1)}, u32[]{:S(2)}, u32[]{:S(2)}) async-start(bf16[128,4,896]{2,1,0:T(4,128)(2,1)} %reshape.56), calls=%async_computation | async-start | bytes 1835008 | tf_op jit(solution)/shard_map/all_to_all | solution.py:168
  24.5 0.3 reduce-window.9
  24.8 0.1 slice.33
  24.9 0.1 slice_reduce_fusion
  25.0 0.1 fusion.6
  25.1 0.4 fusion
  25.5 2.1 %fusion.5 = (f32[1024]{0:T(1024)S(1)}, f32[1024]{0:T(1024)S(1)}) fusion(s32[1024]{0:T(1024)S(1)} %dynamic_slice.7, s32[1024]{0:T(1024)S(1)} %copy-done.7, s32[1024]{0:T(1024)S(1)} %dynamic_slice.6, bf16[1024,768]{1,0:T(8,128)(2,1)S(1)} %copy-done, bf16[1024,768]{1,0:T(8,128)(2,1)S(1)} %copy-done.1, f32[1024]{0:T(1024)S(1)} %add_rsqrt_fusion), kind=kOutput, calls=%fused_computation.15 | convolution fusion | flops 1619261440 | bytes 3170304 | tf_op jit(solution)/shard_map/dot_general | solution.py:176
  27.6 2.7 %collective-permute-start.2 = (f32[2,1024]{1,0:T(2,128)S(1)}, f32[2,1024]{1,0:T(2,128)S(1)}, u32[]{:S(2)}, u32[]{:S(2)}) collective-permute-start(f32[2,1024]{1,0:T(2,128)S(1)} %pad_maximum_fusion), channel_id=1, source_target_pairs={{0,3},{1,0},{2,1},{3,2},{4,7},{5,4},{6,5},{7,6},{8,11},{9,8},{10,9... | collective-permute-start | bytes 24584 | tf_op jit(solution)/shard_map/ppermute | solution.py:16
  30.4 3.0 %collective-permute-start.1 = (f32[2,1024]{1,0:T(2,128)S(1)}, f32[2,1024]{1,0:T(2,128)S(1)}, u32[]{:S(2)}, u32[]{:S(2)}) collective-permute-start(f32[2,1024]{1,0:T(2,128)S(1)} %pad_maximum_fusion), channel_id=1, source_target_pairs={{0,2},{1,3},{2,0},{3,1},{4,6},{5,7},{6,4},{7,5},{8,10},{9,11},{10,... | collective-permute-start | bytes 24584 | tf_op jit(solution)/shard_map/ppermute | solution.py:16
  33.4 4.0 %collective-permute-start = (f32[2,1024]{1,0:T(2,128)S(1)}, f32[2,1024]{1,0:T(2,128)S(1)}, u32[]{:S(2)}, u32[]{:S(2)}) collective-permute-start(f32[2,1024]{1,0:T(2,128)S(1)} %pad_maximum_fusion), channel_id=1, source_target_pairs={{0,1},{1,2},{2,3},{3,0},{4,5},{5,6},{6,7},{7,4},{8,9},{9,10},{10,1... | collective-permute-start | bytes 24584 | tf_op jit(solution)/shard_map/ppermute | solution.py:16
  37.4 0.7 select_reduce_fusion
  38.1 0.6 broadcast_subtract_fusion
  38.7 12.8 %all-to-all-done = bf16[128,4,896]{2,1,0:T(4,128)(2,1)} async-done(((bf16[128,4,896]{2,1,0:T(4,128)(2,1)}), bf16[128,4,896]{2,1,0:T(4,128)(2,1)}, u32[]{:S(2)}, u32[]{:S(2)}) %all-to-all-start) | async-done | bytes 917536 | tf_op jit(solution)/shard_map/all_to_all | solution.py:168
  51.5 2.4 %reshape.57.got_ref = bf16[512,896]{1,0:T(8,128)(2,1)} reshape(bf16[128,4,896]{2,1,0:T(4,128)(2,1)} %all-to-all-done) | data formatting | bytes 1835008 | tf_op jit(solution)/shard_map/reshape | solution.py:199
  53.9 2.9 %compact.1.refs_0_ = bf16[264,768]{1,0:T(8,128)(2,1)} custom-call(bf16[512,896]{1,0:T(8,128)(2,1)} %reshape.57.got_ref), custom_call_target="tpu_custom_call" | custom-call | tf_op jit(solution)/shard_map/compact/pallas_call | solution.py:110
  56.8 2.4 %collective-permute-start.3 = (bf16[264,768]{1,0:T(8,128)(2,1)}, bf16[264,768]{1,0:T(8,128)(2,1)}, u32[]{:S(2)}, u32[]{:S(2)}) collective-permute-start(bf16[264,768]{1,0:T(8,128)(2,1)} %compact.1.refs_0_), channel_id=1, source_target_pairs={{0,1},{1,2},{2,3},{3,0},{4,5},{5,6},{6,7},{7,4},{8,9},{9,10},{10,1... | collective-permute-start | bytes 1216520 | tf_op jit(solution)/shard_map/ppermute | solution.py:16
  59.2 3.5 %collective-permute-start.4 = (bf16[264,768]{1,0:T(8,128)(2,1)}, bf16[264,768]{1,0:T(8,128)(2,1)}, u32[]{:S(2)}, u32[]{:S(2)}) collective-permute-start(bf16[264,768]{1,0:T(8,128)(2,1)} %compact.1.refs_0_), channel_id=1, source_target_pairs={{0,3},{1,0},{2,1},{3,2},{4,7},{5,4},{6,5},{7,6},{8,11},{9,8},{10,9... | collective-permute-start | bytes 1216520 | tf_op jit(solution)/shard_map/ppermute | solution.py:16
  62.6 3.3 %collective-permute-start.5 = (bf16[264,768]{1,0:T(8,128)(2,1)}, bf16[264,768]{1,0:T(8,128)(2,1)}, u32[]{:S(2)}, u32[]{:S(2)}) collective-permute-start(bf16[264,768]{1,0:T(8,128)(2,1)} %compact.1.refs_0_), channel_id=1, source_target_pairs={{0,2},{1,3},{2,0},{3,1},{4,6},{5,7},{6,4},{7,5},{8,10},{9,11},{10,... | collective-permute-start | bytes 1216520 | tf_op jit(solution)/shard_map/ppermute | solution.py:16
  66.0 1.9 %collective-permute-start.6 = (bf16[264,768]{1,0:T(8,128)(2,1)}, bf16[264,768]{1,0:T(8,128)(2,1)S(1)}, u32[]{:S(2)}, u32[]{:S(2)}) collective-permute-start(bf16[264,768]{1,0:T(8,128)(2,1)} %compact.1.refs_0_), channel_id=1, source_target_pairs={{0,4},{4,8},{8,12},{12,16},{16,20},{20,24},{24,28},{28,32},{32,36}... | collective-permute-start | bytes 1216520 | tf_op jit(solution)/shard_map/ppermute | solution.py:16
  67.9 3.2 %collective-permute-done.3.refs_1_ = bf16[264,768]{1,0:T(8,128)(2,1)} collective-permute-done((bf16[264,768]{1,0:T(8,128)(2,1)}, bf16[264,768]{1,0:T(8,128)(2,1)}, u32[]{:S(2)}, u32[]{:S(2)}) %collective-permute-start.3) | collective-permute-done | bytes 405536 | tf_op jit(solution)/shard_map/ppermute | solution.py:16
  71.1 1.9 %collective-permute-start.7 = (bf16[264,768]{1,0:T(8,128)(2,1)}, bf16[264,768]{1,0:T(8,128)(2,1)S(1)}, u32[]{:S(2)}, u32[]{:S(2)}) collective-permute-start(bf16[264,768]{1,0:T(8,128)(2,1)} %collective-permute-done.3.refs_1_), channel_id=1, source_target_pairs={{0,4},{4,8},{8,12},{12,16},{16,20},{20,24},{24,28},{28,32},{32,36}... | collective-permute-start | bytes 1216520 | tf_op jit(solution)/shard_map/ppermute | solution.py:16
  73.1 9.8 %collective-permute-done.4.refs_2_ = bf16[264,768]{1,0:T(8,128)(2,1)} collective-permute-done((bf16[264,768]{1,0:T(8,128)(2,1)}, bf16[264,768]{1,0:T(8,128)(2,1)}, u32[]{:S(2)}, u32[]{:S(2)}) %collective-permute-start.4) | collective-permute-done | bytes 405536 | tf_op jit(solution)/shard_map/ppermute | solution.py:16
  82.9 1.9 %collective-permute-start.8 = (bf16[264,768]{1,0:T(8,128)(2,1)}, bf16[264,768]{1,0:T(8,128)(2,1)S(1)}, u32[]{:S(2)}, u32[]{:S(2)}) collective-permute-start(bf16[264,768]{1,0:T(8,128)(2,1)} %collective-permute-done.4.refs_2_), channel_id=1, source_target_pairs={{0,4},{4,8},{8,12},{12,16},{16,20},{20,24},{24,28},{28,32},{32,36}... | collective-permute-start | bytes 1216520 | tf_op jit(solution)/shard_map/ppermute | solution.py:16
  84.8 3.1 %collective-permute-start.9 = (bf16[264,768]{1,0:T(8,128)(2,1)}, bf16[264,768]{1,0:T(8,128)(2,1)S(1)}, u32[]{:S(2)}, u32[]{:S(2)}) collective-permute-start(bf16[264,768]{1,0:T(8,128)(2,1)} %collective-permute-done.5.refs_3_), channel_id=1, source_target_pairs={{0,4},{4,8},{8,12},{12,16},{16,20},{20,24},{24,28},{28,32},{32,36}... | collective-permute-start | bytes 1216520 | tf_op jit(solution)/shard_map/ppermute | solution.py:16
  87.9 0.6 add_subtract_fusion
  88.5 3.6 %own.1 = (bf16[256,768]{1,0:T(8,128)(2,1)}, f32[1,256]{1,0:T(1,128)}) custom-call(s32[1]{0:T(128)} %bitcast.11.first_ref, s32[1,256]{1,0:T(1,128)} %bitcast.27, bf16[264,768]{1,0:T(8,128)(2,1)} %compact.1.refs_0_, bf16[264,768]{1,0:T(8,128)(2,1)} %collective-permute-done.3.refs_1_, bf16[264,768]{1,0:T(8,128)(2,1)} %collective-permute-done.4.refs_2_, ...), custom_call_target="tpu_custom_call" | custom-call | tf_op jit(solution)/shard_map/own/pallas_call | solution.py:202
  92.1 3.5 %collective-permute-done.8.refs_5_ = bf16[264,768]{1,0:T(8,128)(2,1)S(1)} collective-permute-done((bf16[264,768]{1,0:T(8,128)(2,1)}, bf16[264,768]{1,0:T(8,128)(2,1)S(1)}, u32[]{:S(2)}, u32[]{:S(2)}) %collective-permute-start.8) | collective-permute-done | bytes 405536 | tf_op jit(solution)/shard_map/ppermute | solution.py:16
  95.6 4.3 %collective-permute-done.9.refs_6_ = bf16[264,768]{1,0:T(8,128)(2,1)S(1)} collective-permute-done((bf16[264,768]{1,0:T(8,128)(2,1)}, bf16[264,768]{1,0:T(8,128)(2,1)S(1)}, u32[]{:S(2)}, u32[]{:S(2)}) %collective-permute-start.9) | collective-permute-done | bytes 405536 | tf_op jit(solution)/shard_map/ppermute | solution.py:16
  100.0 0.7 copy-done.5
  100.7 2.7 %previous.1 = f32[1,256]{1,0:T(1,128)} custom-call(s32[1,256]{1,0:T(1,128)} %bitcast.28, f32[1,256]{1,0:T(1,128)} %get-tuple-element.4.refs_1_, bf16[256,768]{1,0:T(8,128)(2,1)} %get-tuple-element.5.refs_2_, bf16[264,768]{1,0:T(8,128)(2,1)} %copy-done.2, bf16[264,768]{1,0:T(8,128)(2,1)} %copy-done.3, bf16[264,768]{1,0:T(8,128)(2,1)} %copy-done.4, ...), custom_call_target="tpu_custom_call" | custom-call | tf_op jit(solution)/shard_map/previous/pallas_call | solution.py:212
  (30 shorter events, 0.2 us)
Async XLA Ops:
  0.6 24.9 %copy-start = (bf16[1024,768]{1,0:T(8,128)(2,1)S(1)}, bf16[1024,768]{1,0:T(8,128)(2,1)}, u32[]{:S(2)}) copy-start(bf16[1024,768]{1,0:T(8,128)(2,1)} %param.5) | copy-start | bytes 4718596
  3.4 21.0 %copy-start.6 = (s32[4096]{0:T(1024)S(1)}, s32[4096]{0:T(1024)}, u32[]{:S(2)}) copy-start(s32[4096]{0:T(1024)} %param.7) | copy-start | bytes 49156
  3.4 21.7 %copy-start.1 = (bf16[1024,768]{1,0:T(8,128)(2,1)S(1)}, bf16[1024,768]{1,0:T(8,128)(2,1)}, u32[]{:S(2)}) copy-start(bf16[1024,768]{1,0:T(8,128)(2,1)} %refs_1_.1) | copy-start | bytes 4718596
  6.0 19.5 %copy-start.7 = (s32[1024]{0:T(1024)S(1)}, s32[1024]{0:T(1024)}, u32[]{:S(2)}) copy-start(s32[1024]{0:T(1024)} %param.6) | copy-start | bytes 12292
  6.0 45.5 %all-to-all-start = ((bf16[128,4,896]{2,1,0:T(4,128)(2,1)}), bf16[128,4,896]{2,1,0:T(4,128)(2,1)}, u32[]{:S(2)}, u32[]{:S(2)}) async-start(bf16[128,4,896]{2,1,0:T(4,128)(2,1)} %reshape.56), calls=%async_computation | async-start | bytes 1835008 | tf_op jit(solution)/shard_map/all_to_all | solution.py:168
  27.6 35.0 %collective-permute-start.2 = (f32[2,1024]{1,0:T(2,128)S(1)}, f32[2,1024]{1,0:T(2,128)S(1)}, u32[]{:S(2)}, u32[]{:S(2)}) collective-permute-start(f32[2,1024]{1,0:T(2,128)S(1)} %pad_maximum_fusion), channel_id=1, source_target_pairs={{0,3},{1,0},{2,1},{3,2},{4,7},{5,4},{6,5},{7,6},{8,11},{9,8},{10,9... | collective-permute-start | bytes 24584 | tf_op jit(solution)/shard_map/ppermute | solution.py:16
  30.4 35.6 %collective-permute-start.1 = (f32[2,1024]{1,0:T(2,128)S(1)}, f32[2,1024]{1,0:T(2,128)S(1)}, u32[]{:S(2)}, u32[]{:S(2)}) collective-permute-start(f32[2,1024]{1,0:T(2,128)S(1)} %pad_maximum_fusion), channel_id=1, source_target_pairs={{0,2},{1,3},{2,0},{3,1},{4,6},{5,7},{6,4},{7,5},{8,10},{9,11},{10,... | collective-permute-start | bytes 24584 | tf_op jit(solution)/shard_map/ppermute | solution.py:16
  33.4 54.5 %collective-permute-start = (f32[2,1024]{1,0:T(2,128)S(1)}, f32[2,1024]{1,0:T(2,128)S(1)}, u32[]{:S(2)}, u32[]{:S(2)}) collective-permute-start(f32[2,1024]{1,0:T(2,128)S(1)} %pad_maximum_fusion), channel_id=1, source_target_pairs={{0,1},{1,2},{2,3},{3,0},{4,5},{5,6},{6,7},{7,4},{8,9},{9,10},{10,1... | collective-permute-start | bytes 24584 | tf_op jit(solution)/shard_map/ppermute | solution.py:16
  56.8 14.4 %collective-permute-start.3 = (bf16[264,768]{1,0:T(8,128)(2,1)}, bf16[264,768]{1,0:T(8,128)(2,1)}, u32[]{:S(2)}, u32[]{:S(2)}) collective-permute-start(bf16[264,768]{1,0:T(8,128)(2,1)} %compact.1.refs_0_), channel_id=1, source_target_pairs={{0,1},{1,2},{2,3},{3,0},{4,5},{5,6},{6,7},{7,4},{8,9},{9,10},{10,1... | collective-permute-start | bytes 1216520 | tf_op jit(solution)/shard_map/ppermute | solution.py:16
  59.2 23.7 %collective-permute-start.4 = (bf16[264,768]{1,0:T(8,128)(2,1)}, bf16[264,768]{1,0:T(8,128)(2,1)}, u32[]{:S(2)}, u32[]{:S(2)}) collective-permute-start(bf16[264,768]{1,0:T(8,128)(2,1)} %compact.1.refs_0_), channel_id=1, source_target_pairs={{0,3},{1,0},{2,1},{3,2},{4,7},{5,4},{6,5},{7,6},{8,11},{9,8},{10,9... | collective-permute-start | bytes 1216520 | tf_op jit(solution)/shard_map/ppermute | solution.py:16
  62.6 22.1 %collective-permute-start.5 = (bf16[264,768]{1,0:T(8,128)(2,1)}, bf16[264,768]{1,0:T(8,128)(2,1)}, u32[]{:S(2)}, u32[]{:S(2)}) collective-permute-start(bf16[264,768]{1,0:T(8,128)(2,1)} %compact.1.refs_0_), channel_id=1, source_target_pairs={{0,2},{1,3},{2,0},{3,1},{4,6},{5,7},{6,4},{7,5},{8,10},{9,11},{10,... | collective-permute-start | bytes 1216520 | tf_op jit(solution)/shard_map/ppermute | solution.py:16
  66.0 26.1 %collective-permute-start.6 = (bf16[264,768]{1,0:T(8,128)(2,1)}, bf16[264,768]{1,0:T(8,128)(2,1)S(1)}, u32[]{:S(2)}, u32[]{:S(2)}) collective-permute-start(bf16[264,768]{1,0:T(8,128)(2,1)} %compact.1.refs_0_), channel_id=1, source_target_pairs={{0,4},{4,8},{8,12},{12,16},{16,20},{20,24},{24,28},{28,32},{32,36}... | collective-permute-start | bytes 1216520 | tf_op jit(solution)/shard_map/ppermute | solution.py:16
  71.1 21.0 %collective-permute-start.7 = (bf16[264,768]{1,0:T(8,128)(2,1)}, bf16[264,768]{1,0:T(8,128)(2,1)S(1)}, u32[]{:S(2)}, u32[]{:S(2)}) collective-permute-start(bf16[264,768]{1,0:T(8,128)(2,1)} %collective-permute-done.3.refs_1_), channel_id=1, source_target_pairs={{0,4},{4,8},{8,12},{12,16},{16,20},{20,24},{24,28},{28,32},{32,36}... | collective-permute-start | bytes 1216520 | tf_op jit(solution)/shard_map/ppermute | solution.py:16
  82.9 12.7 %collective-permute-start.8 = (bf16[264,768]{1,0:T(8,128)(2,1)}, bf16[264,768]{1,0:T(8,128)(2,1)S(1)}, u32[]{:S(2)}, u32[]{:S(2)}) collective-permute-start(bf16[264,768]{1,0:T(8,128)(2,1)} %collective-permute-done.4.refs_2_), channel_id=1, source_target_pairs={{0,4},{4,8},{8,12},{12,16},{16,20},{20,24},{24,28},{28,32},{32,36}... | collective-permute-start | bytes 1216520 | tf_op jit(solution)/shard_map/ppermute | solution.py:16
  84.8 15.2 %collective-permute-start.9 = (bf16[264,768]{1,0:T(8,128)(2,1)}, bf16[264,768]{1,0:T(8,128)(2,1)S(1)}, u32[]{:S(2)}, u32[]{:S(2)}) collective-permute-start(bf16[264,768]{1,0:T(8,128)(2,1)} %collective-permute-done.5.refs_3_), channel_id=1, source_target_pairs={{0,4},{4,8},{8,12},{12,16},{16,20},{20,24},{24,28},{28,32},{32,36}... | collective-permute-start | bytes 1216520 | tf_op jit(solution)/shard_map/ppermute | solution.py:16
  92.1 7.8 %copy-start.2 = (bf16[264,768]{1,0:T(8,128)(2,1)}, bf16[264,768]{1,0:T(8,128)(2,1)S(1)}, u32[]{:S(2)}) copy-start(bf16[264,768]{1,0:T(8,128)(2,1)S(1)} %collective-permute-done.6.refs_3_) | copy-start | bytes 1216516
  92.1 7.8 %copy-start.3 = (bf16[264,768]{1,0:T(8,128)(2,1)}, bf16[264,768]{1,0:T(8,128)(2,1)S(1)}, u32[]{:S(2)}) copy-start(bf16[264,768]{1,0:T(8,128)(2,1)S(1)} %collective-permute-done.7.refs_4_) | copy-start | bytes 1216516
  95.6 4.4 %copy-start.4 = (bf16[264,768]{1,0:T(8,128)(2,1)}, bf16[264,768]{1,0:T(8,128)(2,1)S(1)}, u32[]{:S(2)}) copy-start(bf16[264,768]{1,0:T(8,128)(2,1)S(1)} %collective-permute-done.8.refs_5_) | copy-start | bytes 1216516
  100.0 0.8 copy-start.5

commit v2 on v1

v2 whole, which is shorter than its diff:
```python
import jax
import jax.numpy as jnp
from jax import lax
from jax.experimental import pallas as pl
from jax.experimental.pallas import tpu as pltpu
from jax.sharding import PartitionSpec as P

SLOTS = 4
LANES = 128
TAG_BASE = 32
PAIR_SLOTS = 6
PAIR_ROWS = 8
HELD = 264
PART = 272
NOWHERE = -4096


def rotated(shard, axis, by):
    peers = lax.axis_size(axis)
    return lax.ppermute(shard, axis, [(i, (i + by) % peers) for i in range(peers)])


def to_next_owner(shard):
    row_count = lax.axis_size("rows")
    return lax.ppermute(shard, "rows", [(row, row + 1) for row in range(row_count - 1)])


def from_holders(shard, cent_by, row_by):
    row_count, cent_count = lax.axis_size("rows"), lax.axis_size("cent")
    pairs = []
    for row in range(row_count):
        for cent in range(cent_count):
            target_row = (row ^ (cent // 2)) + row_by
            target_cent = (cent + cent_by) % cent_count
            if target_row < row_count:
                pairs.append((row * cent_count + cent, target_row * cent_count + target_cent))
    return lax.ppermute(shard, ("rows", "cent"), pairs)


def iota(shape, dim):
    return lax.broadcasted_iota(jnp.int32, shape, dim)


def as_column(row):
    size = row.shape[1]
    eye = iota((size, size), 0) == iota((size, size), 1)
    return jnp.sum(jnp.where(eye, row, jnp.zeros_like(row)), axis=1, keepdims=True)


def dot(left, right, left_dim, right_dim):
    return lax.dot_general(
        left, right, (((left_dim,), (right_dim,)), ((), ())), preferred_element_type=jnp.float32
    )


def normalise(rows):
    floats = rows.astype(jnp.float32)
    return (floats * lax.rsqrt(jnp.sum(floats * floats, axis=-1, keepdims=True) + 1e-06)).astype(
        jnp.bfloat16
    )


def tag_rows(local):
    return local // TAG_BASE + 1, local % TAG_BASE


def pack_pairs_kernel(row_ref, cent_ref, rows_ref, places_ref, out_ref, fits_ref, *, owner_rows):
    row_index = row_ref[0]
    sibling = cent_ref[0] // 2
    half = cent_ref[0] % 2
    count, features = rows_ref.shape
    slots = out_ref.shape[0]
    places = places_ref[...]
    owners = places // owner_rows
    owner_count = count // PAIR_ROWS
    step = 256
    earlier = (iota((step, step), 0) < iota((step, step), 1)).astype(jnp.bfloat16)
    so_far = jnp.zeros((owner_count, 1), jnp.float32)
    ranks = []
    for first in range(0, count, step):
        here = iota((owner_count, step), 0) == owners[:, first : first + step]
        marks = here.astype(jnp.float32)
        before = dot(marks.astype(jnp.bfloat16), earlier, 1, 0) + so_far
        ranks.append(jnp.sum(marks * before, axis=0, keepdims=True))
        so_far = so_far + jnp.sum(marks, axis=1, keepdims=True)
    rank = jnp.concatenate(ranks, axis=1).astype(jnp.int32)
    plane = ((owners + row_index) % 2) * 2 + rank % 2
    spare = (plane == iota((8, count), 0)).astype(jnp.float32)
    held = jnp.max(jnp.sum(spare, axis=1, keepdims=True) - float(HELD), axis=0, keepdims=True)
    over = jnp.max(rank.astype(jnp.float32), axis=1, keepdims=True) - float(2 * PAIR_SLOTS - 1)
    fits_ref[0] = (jnp.max(jnp.maximum(held, over)) < 0.5).astype(jnp.int32)

    mine = plane == sibling * 2 + half
    block = owners // 2 * PAIR_ROWS
    slot = rank // 2
    chosen = (iota((slots, count), 0) == jnp.where(mine, block + slot, -1)).astype(jnp.bfloat16)
    sent = dot(chosen, rows_ref[...], 1, 0)
    sent = sent * lax.rsqrt(jnp.sum(sent * sent, axis=-1, keepdims=True) + 1e-06)
    high, low = tag_rows(places % owner_rows)
    field = iota((16, count), 0)
    tags = jnp.where(field // 2 == slot, jnp.where(field % 2 == 0, high, low), 0)
    tags = jnp.concatenate([tags, jnp.zeros((LANES - 16, count), jnp.int32)], axis=0)
    tags = tags.astype(jnp.float32).astype(jnp.bfloat16)
    chips = slots // PAIR_ROWS
    sender = iota((chips, count), 0) == jnp.where(mine, owners // 2, -1)
    tags = dot(sender.astype(jnp.bfloat16), tags, 1, 1)
    tags = jnp.broadcast_to(tags[:, None, :], (chips, PAIR_ROWS, LANES)).reshape(slots, LANES)
    wide = features - LANES
    rest = sent[:, wide:]
    line = iota((slots, LANES), 0) % PAIR_ROWS
    for tile in range(PAIR_SLOTS - 1):
        lanes = slice(tile * LANES, (tile + 1) * LANES)
        moved = pltpu.roll(rest, PAIR_SLOTS - tile, 0)
        value = jnp.where(line == PAIR_SLOTS, moved, sent[:, lanes])
        if tile == 0:
            value = jnp.where(line == PAIR_SLOTS + 1, pltpu.roll(rest, 2, 0), value)
        if tile == 1:
            value = jnp.where(line == PAIR_SLOTS + 1, tags, value)
        out_ref[:, lanes] = value.astype(jnp.bfloat16)


def pack_pairs(rows, places, row_index, cent_index, chips, owner_rows):
    count, features = rows.shape
    return pl.pallas_call(
        lambda *refs: pack_pairs_kernel(*refs, owner_rows=owner_rows),
        in_specs=[
            pl.BlockSpec(memory_space=pltpu.SMEM),
            pl.BlockSpec(memory_space=pltpu.SMEM),
            pl.BlockSpec(memory_space=pltpu.VMEM),
            pl.BlockSpec(memory_space=pltpu.VMEM),
        ],
        out_specs=(
            pl.BlockSpec(memory_space=pltpu.VMEM),
            pl.BlockSpec(memory_space=pltpu.SMEM),
        ),
        out_shape=(
            jax.ShapeDtypeStruct((chips * PAIR_ROWS, features - LANES), jnp.bfloat16),
            jax.ShapeDtypeStruct((1,), jnp.int32),
        ),
        name="pack_pairs",
    )(row_index[None], cent_index[None], rows, places[None])


def store_part(out_ref, tags, pieces):
    tag_lines = tags.T[:16].astype(jnp.bfloat16)
    slots = tag_lines.shape[1]
    filled = tag_lines[0:1].astype(jnp.float32) > 0.5
    marks = jnp.broadcast_to(filled.astype(jnp.float32), (16, slots)).astype(jnp.bfloat16)
    before = (iota((slots, slots), 0) < iota((slots, slots), 1)).astype(jnp.bfloat16)
    rank = jnp.where(filled, dot(marks, before, 1, 0)[0:1].astype(jnp.int32), -1)
    picks = (iota((PART, slots), 0) == rank).astype(jnp.bfloat16)
    lines = jnp.concatenate([jnp.zeros((8, PART), jnp.float32), dot(tag_lines[:8], picks, 1, 1)], 0)
    first = 0
    for piece in pieces:
        lanes = slice(first, first + piece.shape[1])
        out_ref[:, lanes] = dot(picks, piece, 1, 0).astype(jnp.bfloat16)
        first = first + piece.shape[1]
    kept = out_ref[PART - 16 :, :PART].astype(jnp.float32)
    out_ref[PART - 16 :, :PART] = (kept + lines).astype(jnp.bfloat16)


def compact_pairs_kernel(got_ref, out_ref):
    slots, wide = got_ref.shape
    line = iota((slots, LANES), 0) % PAIR_ROWS
    lane = iota((slots, LANES), 1)
    rest = jnp.zeros((slots, LANES), jnp.float32)
    placed = jnp.zeros((slots, LANES), jnp.float32)
    tags = got_ref[:, LANES : 2 * LANES].astype(jnp.float32)
    for slot in range(PAIR_SLOTS):
        tile = slot % (PAIR_SLOTS - 1)
        up = PAIR_SLOTS - slot if slot < PAIR_SLOTS - 1 else 2
        value = got_ref[:, tile * LANES : (tile + 1) * LANES].astype(jnp.float32)
        rest = jnp.where(line == slot, pltpu.roll(value, slots - up, 0), rest)
        moved = pltpu.roll(tags, slots - (PAIR_ROWS - 1 - slot), 0)
        moved = pltpu.roll(moved, (LANES - 2 * slot) % LANES, 1) if slot else moved
        placed = jnp.where((line == slot) & (lane < 2), moved, placed)
    store_part(out_ref, placed, [got_ref[...], rest.astype(jnp.bfloat16)])


def pack_kernel(cent_ref, rows_ref, places_ref, out_ref, *, owner_rows):
    normed = normalise(rows_ref[...])
    count, features = normed.shape
    slots = out_ref.shape[0]
    places = places_ref[0]
    owners = places // owner_rows
    earlier = (as_column(owners) == owners) & (iota((count, count), 0) < iota((count, count), 1))
    rank = jnp.sum(earlier.astype(jnp.int32), axis=0, keepdims=True)
    chosen = (iota((slots, count), 0) == owners * SLOTS + rank).astype(jnp.bfloat16)
    high, low = tag_rows(as_column(places % owner_rows))
    lane = iota((count, LANES), 1)
    tags = jnp.where(lane == 0, high, jnp.where(lane == 1, low, 0))
    tags = tags.astype(jnp.float32).astype(jnp.bfloat16)
    out_ref[:, :features] = dot(chosen, normed, 1, 0).astype(jnp.bfloat16)
    out_ref[:, features:] = dot(chosen, tags, 1, 0).astype(jnp.bfloat16)


def pack(rows, places, cent_index, owners, owner_rows, quarters):
    count, features = rows.shape
    quarter = count // quarters
    slots = owners * SLOTS
    return pl.pallas_call(
        lambda *refs: pack_kernel(*refs, owner_rows=owner_rows),
        grid_spec=pltpu.PrefetchScalarGridSpec(
            num_scalar_prefetch=1,
            grid=(1,),
            in_specs=[
                pl.BlockSpec((quarter, features), lambda i, cent: (cent[0], 0)),
                pl.BlockSpec((1, 1, quarter), lambda i, cent: (cent[0], 0, 0)),
            ],
            out_specs=pl.BlockSpec((slots, features + LANES), lambda i, cent: (0, 0)),
        ),
        out_shape=jax.ShapeDtypeStruct((slots, features + LANES), jnp.bfloat16),
        name="pack",
    )(cent_index[None], rows, places.reshape(quarters, 1, quarter))


def compact_kernel(got_ref, out_ref):
    features = out_ref.shape[1]
    tags = got_ref[:, features:].astype(jnp.float32)
    store_part(out_ref, tags, [got_ref[:, :features]])


def compacted(kernel, got, features, name):
    return pl.pallas_call(
        kernel, out_shape=jax.ShapeDtypeStruct((PART, features), jnp.bfloat16), name=name
    )(got)


def decoded(high, low):
    places = jnp.where(high > 0.5, (high - 1.0) * float(TAG_BASE) + low, float(NOWHERE))
    return places.astype(jnp.int32)


def part_tags(part_ref):
    return part_ref[PART - 16 :, : 3 * LANES].astype(jnp.float32)


def place_row(part_ref):
    tags = part_tags(part_ref)
    return decoded(tags[8:9, :PART], tags[9:10, :PART])


def place_column(part_ref):
    tags = part_tags(part_ref).T
    return decoded(tags[:PART, 8:9], tags[:PART, 9:10])


def picked_queries(first_place, count, part_refs):
    queries = 0.0
    for part in part_refs:
        chosen = place_row(part) == first_place + iota((count, PART), 0)
        queries = queries + dot(chosen.astype(jnp.bfloat16), part[...], 1, 0)
    return queries


def compared(best, queries, query_places, starts, part_refs, first_place):
    for part in part_refs:
        column = place_column(part) + first_place
        similarity = dot(part[...], queries, 1, 1)
        allowed = (column >= starts) & (column < query_places)
        masked = jnp.where(allowed, similarity, -1.0)
        best = jnp.maximum(best, jnp.max(masked, axis=0, keepdims=True))
    return best


def early_queries_kernel(first_ref, *refs):
    *part_refs, queries_ref = refs
    queries = picked_queries(first_ref[0], queries_ref.shape[0], part_refs)
    queries_ref[...] = queries.astype(jnp.bfloat16)


def own_kernel(first_ref, starts_ref, early_ref, *refs):
    *part_refs, queries_ref, best_ref = refs
    count = queries_ref.shape[0]
    query_places = first_ref[0] + iota((1, count), 1)
    late = picked_queries(first_ref[0], count, part_refs[-1:])
    queries = (early_ref[...].astype(jnp.float32) + late).astype(jnp.bfloat16)
    queries_ref[...] = queries
    best = jnp.full((1, count), -1.0, jnp.float32)
    best_ref[...] = compared(best, queries, query_places, starts_ref[...], part_refs, 0)


def previous_kernel(first_ref, starts_ref, best_ref, queries_ref, *refs, owner_rows):
    *part_refs, last_ref, out_ref, last_copy, arrived = refs
    copy = pltpu.make_async_copy(last_ref, last_copy, arrived)
    copy.start()
    query_places = first_ref[0] + iota((1, queries_ref.shape[0]), 1)
    queries = queries_ref[...]
    starts = starts_ref[...]
    best = compared(best_ref[...], queries, query_places, starts, part_refs, -owner_rows)
    copy.wait()
    out_ref[...] = compared(best, queries, query_places, starts, [last_copy], -owner_rows)


def whole_call(kernel, out_shape, name, scalar, *arrays, left_there=0, scratch=()):
    here = len(arrays) - left_there
    size = sum(array.size for array in arrays)
    return pl.pallas_call(
        kernel,
        in_specs=[pl.BlockSpec(memory_space=pltpu.SMEM)]
        + [pl.BlockSpec(memory_space=pltpu.VMEM)] * here
        + [pl.BlockSpec(memory_space=pltpu.HBM)] * left_there,
        out_shape=out_shape,
        scratch_shapes=scratch,
        cost_estimate=pl.CostEstimate(
            flops=2 * size * PART, transcendentals=0, bytes_accessed=8 * size
        ),
        name=name,
    )(scalar, *arrays)


def margin_of(embeddings, centroids, positions, slab_starts, slab_ends):
    scores = lax.dot_general(
        normalise(embeddings),
        centroids,
        (((1,), (1,)), ((), ())),
        preferred_element_type=jnp.float32,
    )
    best_sim = jnp.max(scores, axis=1)
    assigned = (slab_starts[None, :] <= positions[:, None]) & (
        positions[:, None] < slab_ends[None, :]
    )
    picked = jnp.sum(jnp.where(assigned, scores, 0.0), axis=1)
    both = jnp.stack([best_sim, picked])
    for both_there in [rotated(both, "cent", by) for by in range(1, lax.axis_size("cent"))]:
        best_sim = jnp.maximum(best_sim, both_there[0])
        picked = picked + both_there[1]
    return best_sim - picked


def on_device(embeddings, centroids, positions, cluster_sizes):
    block_rows, features = embeddings.shape
    row_count = lax.axis_size("rows")
    cent_count = lax.axis_size("cent")
    quarter = block_rows // cent_count
    slab_size = centroids.shape[0]
    row_index = lax.axis_index("rows")
    cent_index = lax.axis_index("cent")
    chips = row_count // 2

    packed, fits = pack_pairs(embeddings, positions, row_index, cent_index, chips, block_rows)

    cluster_ends = jnp.cumsum(cluster_sizes)
    cluster_starts = cluster_ends - cluster_sizes
    slab_ends = lax.dynamic_slice_in_dim(cluster_ends, cent_index * slab_size, slab_size)
    slab_starts = lax.dynamic_slice_in_dim(cluster_starts, cent_index * slab_size, slab_size)

    def by_pairs(packed, embeddings, centroids, positions, slab_starts, slab_ends):
        got = lax.all_to_all(
            packed,
            "rows",
            split_axis=0,
            concat_axis=0,
            tiled=True,
            axis_index_groups=[list(range(core, row_count, 2)) for core in range(2)],
        )
        margin = margin_of(embeddings, centroids, positions, slab_starts, slab_ends)
        return compacted(compact_pairs_kernel, got, features, "compact_pairs"), margin

    def by_quarters(packed, embeddings, centroids, positions, slab_starts, slab_ends):
        packed = pack(embeddings, positions, cent_index, row_count, block_rows, cent_count)
        got = lax.all_to_all(
            packed.reshape(row_count, SLOTS, -1), "rows", split_axis=0, concat_axis=0, tiled=True
        )
        margin = margin_of(embeddings, centroids, positions, slab_starts, slab_ends)
        part = compacted(
            compact_kernel, got.reshape(row_count * SLOTS, -1), features, "compact"
        )
        return from_holders(part, 0, 0), margin

    held, margin = lax.cond(
        fits[0] != 0,
        by_pairs,
        by_quarters,
        packed,
        embeddings,
        centroids,
        positions,
        slab_starts,
        slab_ends,
    )
    base_place = row_index * block_rows
    places = base_place + cent_index * quarter + jnp.arange(quarter, dtype=jnp.int32)
    started = jnp.where(cluster_starts[None, :] <= places[:, None], cluster_starts[None, :], 0)
    starts = (jnp.max(started, axis=1) - base_place)[None, :]

    left = from_holders(held, 1, 0)
    right = from_holders(held, 3, 0)
    previous_here = from_holders(held, 0, 1)
    here = from_holders(held, 0, 0)
    held, left, right, previous_here, here = lax.optimization_barrier(
        (held, left, right, previous_here, here)
    )
    across = from_holders(held, 2, 0)
    previous_left = to_next_owner(left)
    previous_right = to_next_owner(right)

    first = (cent_index * quarter)[None]
    queries_shape = jax.ShapeDtypeStruct((quarter, features), jnp.bfloat16)
    best_shape = jax.ShapeDtypeStruct((1, quarter), jnp.float32)
    early = whole_call(
        early_queries_kernel, queries_shape, "early_queries", first, here, left, right
    )
    across, early, starts = lax.optimization_barrier((across, early, starts))
    previous_across = to_next_owner(across)
    queries, best = whole_call(
        own_kernel, (queries_shape, best_shape), "own", first, starts, early, here, left, right, across
    )
    best = whole_call(
        lambda *refs: previous_kernel(*refs, owner_rows=block_rows),
        best_shape,
        "previous",
        first,
        starts,
        best,
        queries,
        previous_here,
        previous_left,
        previous_right,
        previous_across,
        left_there=1,
        scratch=[pltpu.VMEM((PART, features), jnp.bfloat16), pltpu.SemaphoreType.DMA],
    )
    return (margin, best.reshape(quarter))


def solution(mesh):
    in_specs = (P("rows", None), P("cent", None), P("rows"), P())
    out_specs = (P("rows"), P(("rows", "cent")))
    return jax.shard_map(
        on_device, mesh=mesh, in_specs=in_specs, out_specs=out_specs, check_vma=False
    )
```

time: 104 us -> 95.2 us (0.915)
  the two profiles are of different devices: /device:TPU:6 before, /device:TPU:130 now
where the time goes in v2:
time: 95.2 us; the launch traced here: 94.5 us
  starting transfers between devices  44.6 us (47%)
  waiting for transfers between devices  25.1 us (26%)
  Pallas kernels  15.8 us (17%)
  local copies, waits for them, and re-layouts  2.87 us (3%)
  matrix products  2.1 us (2%)
  other arithmetic  2.09 us (2%)
  between operations  1.66 us (2%)
    all_to_all x1, starting transfers between devices, by_pairs(): lax.all_to_all(packed, 'rows', split_axis=0, concat_axis=0, tiled=True, a...  14.9 us
    ppermute x5, starting transfers between devices, from_holders(): return lax.ppermute(shard, ('rows', 'cent'), pairs)  12.8 us
    ppermute x5, waiting for transfers between devices, from_holders(): return lax.ppermute(shard, ('rows', 'cent'), pairs)  10.7 us
    ppermute x3, starting transfers between devices, rotated(): lax.ppermute(shard, axis, [(i, (i + by) % peers) for i in range(peers)])  10.5 us
    pallas_call x3, Pallas kernels, whole_call(): pl.pallas_call(kernel, in_specs=[pl.BlockSpec(memory_space=pltpu.SMEM)] +...  9.55 us
    ppermute x3, waiting for transfers between devices, to_next_owner(): lax.ppermute(shard, 'rows', [(row, row + 1) for row in range(row_count -...  6.47 us
    ppermute x3, starting transfers between devices, to_next_owner(): lax.ppermute(shard, 'rows', [(row, row + 1) for row in range(row_count -...  6.44 us
    all_to_all x1, waiting for transfers between devices, by_pairs(): lax.all_to_all(packed, 'rows', split_axis=0, concat_axis=0, tiled=True, a...  6.16 us
  transfers between devices with their start and end apart: 12, of which 8 were waited for; matrix products, arithmetic and copies ran while one was open for 4% of the time, Pallas kernels for 6%

profile of v2, /device:TPU:130, one launch (start us, length us, event | category | flops | bytes accessed | tf_op | source)
XLA Modules:
  0.0 94.5 jit_solution(3170873394124705959)
XLA Ops:
  0.7 4.0 %pack_pairs.1 = (bf16[512,640]{1,0:T(8,128)(2,1)}, s32[1]{0:T(128)}) custom-call(s32[1]{0:T(128)} %bitcast.20.refs_0_, s32[1]{0:T(128)} %bitcast.21.refs_1_, bf16[1024,768]{1,0:T(8,128)(2,1)} %refs_2_.1, s32[1,1024]{1,0:T(1,128)} %bitcast.35), custom_call_target="tpu_custom_call" | custom-call | tf_op jit(solution)/shard_map/pack_pairs/pallas_call | solution.py:124
  5.9 40.3 %conditional.1 = (bf16[272,768]{1,0:T(8,128)(2,1)S(1)}, f32[1024]{0:T(1024)S(1)}) conditional(s32[]{:T(128)} %bitcast.23, (s32[]{:T(128)}, s32[1024]{0:T(1024)S(1)}, bf16[1024,768]{1,0:T(8,128)(2,1)S(1)}, bf16[1024,768]{1,0:T(8,128)(2,1)}, s32[1024]{0:T(1024)S(1)}, /*index=5*/s32[1024]{0:T(1024)S(1)}) %tuple.36, (bf16[512,640]{1,0:T(8,128)(2,1)}, ...), branch_computations={%region_2.6_spmd, %region_6.10_spmd} | conditional | flops 1621629952 | bytes 19341548 | solution.py:371
  6.0 14.9 %all-to-all-start.1 = ((bf16[64,8,640]{2,1,0:T(8,128)(2,1)}), bf16[64,8,640]{2,1,0:T(8,128)(2,1)S(1)}, u32[]{:S(2)}, u32[]{:S(2)}) async-start(bf16[64,8,640]{2,1,0:T(8,128)(2,1)} %bitcast.10), calls=%async_computation.1 | async-start | bytes 1310720 | tf_op jit(solution)/shard_map/cond/branch_1_fun/all_to_all | solution.py:349
  21.3 1.0 %copy-done.9 = bf16[1024,768]{1,0:T(8,128)(2,1)S(1)} copy-done((bf16[1024,768]{1,0:T(8,128)(2,1)S(1)}, bf16[1024,768]{1,0:T(8,128)(2,1)}, u32[]{:S(2)}) %copy-start.9) | copy-done | bytes 1572888 | tf_op jit(solution)/shard_map/cond
  22.3 2.1 %fusion.11 = (f32[1024]{0:T(1024)S(1)}, f32[1024]{0:T(1024)S(1)}) fusion(s32[1024]{0:T(1024)S(1)} %get-tuple-element.35, s32[1024]{0:T(1024)S(1)} %get-tuple-element.34, s32[1024]{0:T(1024)S(1)} %get-tuple-element.33, bf16[1024,768]{1,0:T(8,128)(2,1)S(1)} %copy-done.9, bf16[1024,768]{1,0:T(8,128)(2,1)S(1)} %get-tuple-element.31, f32[1024]{0:T(1024)S(1)} %add_rsqrt_fusion.1), kind=kOutput, calls=%fused_computation.26 | convolution fusion | flops 1619261440 | bytes 3170304 | tf_op jit(solution)/shard_map/cond/branch_1_fun/dot_general | solution.py:313
  24.4 2.4 %collective-permute-start.6 = (f32[2,1024]{1,0:T(2,128)S(1)}, f32[2,1024]{1,0:T(2,128)S(1)}, u32[]{:S(2)}, u32[]{:S(2)}) collective-permute-start(f32[2,1024]{1,0:T(2,128)S(1)} %pad_maximum_fusion.1), channel_id=1, source_target_pairs={{0,3},{1,0},{2,1},{3,2},{4,7},{5,4},{6,5},{7,6},{8,11},{9,8},{10,9... | collective-permute-start | bytes 24584 | tf_op jit(solution)/shard_map/cond/branch_1_fun/ppermute | solution.py:20
  26.8 4.3 %collective-permute-start.5 = (f32[2,1024]{1,0:T(2,128)S(1)}, f32[2,1024]{1,0:T(2,128)S(1)}, u32[]{:S(2)}, u32[]{:S(2)}) collective-permute-start(f32[2,1024]{1,0:T(2,128)S(1)} %pad_maximum_fusion.1), channel_id=1, source_target_pairs={{0,2},{1,3},{2,0},{3,1},{4,6},{5,7},{6,4},{7,5},{8,10},{9,11},{10,... | collective-permute-start | bytes 24584 | tf_op jit(solution)/shard_map/cond/branch_1_fun/ppermute | solution.py:20
  31.2 3.7 %collective-permute-start.4 = (f32[2,1024]{1,0:T(2,128)S(1)}, f32[2,1024]{1,0:T(2,128)S(1)}, u32[]{:S(2)}, u32[]{:S(2)}) collective-permute-start(f32[2,1024]{1,0:T(2,128)S(1)} %pad_maximum_fusion.1), channel_id=1, source_target_pairs={{0,1},{1,2},{2,3},{3,0},{4,5},{5,6},{6,7},{7,4},{8,9},{9,10},{10,1... | collective-permute-start | bytes 24584 | tf_op jit(solution)/shard_map/cond/branch_1_fun/ppermute | solution.py:20
  35.0 1.8 %collective-permute-done.4 = f32[2,1024]{1,0:T(2,128)S(1)} collective-permute-done((f32[2,1024]{1,0:T(2,128)S(1)}, f32[2,1024]{1,0:T(2,128)S(1)}, u32[]{:S(2)}, u32[]{:S(2)}) %collective-permute-start.4) | collective-permute-done | bytes 8224 | tf_op jit(solution)/shard_map/cond/branch_1_fun/ppermute | solution.py:20
  36.8 6.2 %all-to-all-done.1 = bf16[64,8,640]{2,1,0:T(8,128)(2,1)S(1)} async-done(((bf16[64,8,640]{2,1,0:T(8,128)(2,1)}), bf16[64,8,640]{2,1,0:T(8,128)(2,1)S(1)}, u32[]{:S(2)}, u32[]{:S(2)}) %all-to-all-start.1) | async-done | bytes 655392 | tf_op jit(solution)/shard_map/cond/branch_1_fun/all_to_all | solution.py:349
  42.9 0.8 copy-done.1
  43.8 2.3 %compact_pairs.1 = bf16[272,768]{1,0:T(8,128)(2,1)S(1)} custom-call(bf16[512,640]{1,0:T(8,128)(2,1)} %bitcast.33), custom_call_target="tpu_custom_call" | custom-call | tf_op jit(solution)/shard_map/cond/branch_1_fun/compact_pairs/pallas_call | solution.py:224
  46.3 3.4 %collective-permute-start.7 = (bf16[272,768]{1,0:T(8,128)(2,1)S(1)}, bf16[272,768]{1,0:T(8,128)(2,1)S(1)}, u32[]{:S(2)}, u32[]{:S(2)}) collective-permute-start(bf16[272,768]{1,0:T(8,128)(2,1)S(1)} %get-tuple-element.56), channel_id=1, source_target_pairs={{0,1},{1,2},{2,7},{3,4},{4,5},{5,6},{6,3},{7,0},{8,9},{9,10},{10,1... | collective-permute-start | bytes 1253384 | tf_op jit(solution)/shard_map/ppermute | solution.py:37
  49.7 2.4 %collective-permute-start.8 = (bf16[272,768]{1,0:T(8,128)(2,1)S(1)}, bf16[272,768]{1,0:T(8,128)(2,1)S(1)}, u32[]{:S(2)}, u32[]{:S(2)}) collective-permute-start(bf16[272,768]{1,0:T(8,128)(2,1)S(1)} %get-tuple-element.56), channel_id=1, source_target_pairs={{0,3},{1,0},{2,5},{3,6},{4,7},{5,4},{6,1},{7,2},{8,11},{9,8},{10,1... | collective-permute-start | bytes 1253384 | tf_op jit(solution)/shard_map/ppermute | solution.py:37
  52.1 1.9 %collective-permute-start.9 = (bf16[272,768]{1,0:T(8,128)(2,1)S(1)}, bf16[272,768]{1,0:T(8,128)(2,1)S(1)}, u32[]{:S(2)}, u32[]{:S(2)}) collective-permute-start(bf16[272,768]{1,0:T(8,128)(2,1)S(1)} %get-tuple-element.56), channel_id=1, source_target_pairs={{0,4},{1,5},{2,10},{3,11},{4,8},{5,9},{6,6},{7,7},{8,12},{9,13},{1... | collective-permute-start | bytes 1253384 | tf_op jit(solution)/shard_map/ppermute | solution.py:37
  54.1 0.7 collective-permute-start.10
  54.8 2.8 %collective-permute-done.7.refs_1_ = bf16[272,768]{1,0:T(8,128)(2,1)S(1)} collective-permute-done((bf16[272,768]{1,0:T(8,128)(2,1)S(1)}, bf16[272,768]{1,0:T(8,128)(2,1)S(1)}, u32[]{:S(2)}, u32[]{:S(2)}) %collective-permute-start.7) | collective-permute-done | bytes 417824 | tf_op jit(solution)/shard_map/ppermute | solution.py:37
  57.6 4.5 %collective-permute-done.8.refs_2_ = bf16[272,768]{1,0:T(8,128)(2,1)S(1)} collective-permute-done((bf16[272,768]{1,0:T(8,128)(2,1)S(1)}, bf16[272,768]{1,0:T(8,128)(2,1)S(1)}, u32[]{:S(2)}, u32[]{:S(2)}) %collective-permute-start.8) | collective-permute-done | bytes 417824 | tf_op jit(solution)/shard_map/ppermute | solution.py:37
  62.1 1.5 %collective-permute-done.9.refs_4_ = bf16[272,768]{1,0:T(8,128)(2,1)S(1)} collective-permute-done((bf16[272,768]{1,0:T(8,128)(2,1)S(1)}, bf16[272,768]{1,0:T(8,128)(2,1)S(1)}, u32[]{:S(2)}, u32[]{:S(2)}) %collective-permute-start.9) | collective-permute-done | bytes 417824 | tf_op jit(solution)/shard_map/ppermute | solution.py:37
  63.6 4.3 %collective-permute-start.11 = (bf16[272,768]{1,0:T(8,128)(2,1)S(1)}, bf16[272,768]{1,0:T(8,128)(2,1)S(1)}, u32[]{:S(2)}, u32[]{:S(2)}) collective-permute-start(bf16[272,768]{1,0:T(8,128)(2,1)S(1)} %get-tuple-element.56), channel_id=1, source_target_pairs={{0,2},{1,3},{2,4},{3,5},{4,6},{5,7},{6,0},{7,1},{8,10},{9,11},{10,... | collective-permute-start | bytes 1253384 | tf_op jit(solution)/shard_map/ppermute | solution.py:37
  68.0 0.7 select_reduce_fusion.2
  68.6 0.6 broadcast_subtract_fusion
  69.2 1.9 %collective-permute-start.12 = (bf16[272,768]{1,0:T(8,128)(2,1)S(1)}, bf16[272,768]{1,0:T(8,128)(2,1)S(1)}, u32[]{:S(2)}, u32[]{:S(2)}) collective-permute-start(bf16[272,768]{1,0:T(8,128)(2,1)S(1)} %collective-permute-done.7.refs_1_), channel_id=1, source_target_pairs={{0,4},{4,8},{8,12},{12,16},{16,20},{20,24},{24,28},{28,32},{32,36}... | collective-permute-start | bytes 1253384 | tf_op jit(solution)/shard_map/ppermute | solution.py:25
  71.1 2.6 %collective-permute-start.13 = (bf16[272,768]{1,0:T(8,128)(2,1)S(1)}, bf16[272,768]{1,0:T(8,128)(2,1)S(1)}, u32[]{:S(2)}, u32[]{:S(2)}) collective-permute-start(bf16[272,768]{1,0:T(8,128)(2,1)S(1)} %collective-permute-done.8.refs_2_), channel_id=1, source_target_pairs={{0,4},{4,8},{8,12},{12,16},{16,20},{20,24},{24,28},{28,32},{32,36}... | collective-permute-start | bytes 1253384 | tf_op jit(solution)/shard_map/ppermute | solution.py:25
  73.8 2.8 %early_queries.1.early_ref = bf16[256,768]{1,0:T(8,128)(2,1)} custom-call(s32[1]{0:T(128)} %bitcast.26.first_ref.refs_0_, bf16[272,768]{1,0:T(8,128)(2,1)} %copy-done.4, bf16[272,768]{1,0:T(8,128)(2,1)} %copy-done.2, bf16[272,768]{1,0:T(8,128)(2,1)} %copy-done.3), custom_call_target="tpu_custom_call" | custom-call | flops 340918272 | bytes 5013504 | tf_op jit(solution)/shard_map/early_queries/pallas_call | solution.py:298
  76.6 1.8 %collective-permute-done.11.refs_3_ = bf16[272,768]{1,0:T(8,128)(2,1)S(1)} collective-permute-done((bf16[272,768]{1,0:T(8,128)(2,1)S(1)}, bf16[272,768]{1,0:T(8,128)(2,1)S(1)}, u32[]{:S(2)}, u32[]{:S(2)}) %collective-permute-start.11) | collective-permute-done | bytes 417824 | tf_op jit(solution)/shard_map/ppermute | solution.py:37
  78.4 1.9 %collective-permute-start.14 = (bf16[272,768]{1,0:T(8,128)(2,1)S(1)}, bf16[272,768]{1,0:T(8,128)(2,1)S(1)}, u32[]{:S(2)}, u32[]{:S(2)}) collective-permute-start(bf16[272,768]{1,0:T(8,128)(2,1)S(1)} %collective-permute-done.11.refs_3_), channel_id=1, source_target_pairs={{0,4},{4,8},{8,12},{12,16},{16,20},{20,24},{24,28},{28,32},{32,36}... | collective-permute-start | bytes 1253384 | tf_op jit(solution)/shard_map/ppermute | solution.py:25
  80.4 3.0 %own.1 = (bf16[256,768]{1,0:T(8,128)(2,1)}, f32[1,256]{1,0:T(1,128)}) custom-call(s32[1]{0:T(128)} %bitcast.26.first_ref.refs_0_, s32[1,256]{1,0:T(1,128)} %bitcast.53, bf16[256,768]{1,0:T(8,128)(2,1)} %early_queries.1.early_ref, bf16[272,768]{1,0:T(8,128)(2,1)} %copy-done.4, bf16[272,768]{1,0:T(8,128)(2,1)} %copy-done.2, bf16[272,768]{1,0:T(8,128)(2,1)} %copy-done.3, ...), custom_call_target="tpu_custom_call" | custom-call | flops 561651712 | bytes 8259584 | tf_op jit(solution)/shard_map/own/pallas_call | solution.py:298
  83.4 1.7 %collective-permute-done.13.refs_6_ = bf16[272,768]{1,0:T(8,128)(2,1)S(1)} collective-permute-done((bf16[272,768]{1,0:T(8,128)(2,1)S(1)}, bf16[272,768]{1,0:T(8,128)(2,1)S(1)}, u32[]{:S(2)}, u32[]{:S(2)}) %collective-permute-start.13) | collective-permute-done | bytes 417824 | tf_op jit(solution)/shard_map/ppermute | solution.py:25
  85.2 4.7 %collective-permute-done.14.refs_7_ = bf16[272,768]{1,0:T(8,128)(2,1)S(1)} collective-permute-done((bf16[272,768]{1,0:T(8,128)(2,1)S(1)}, bf16[272,768]{1,0:T(8,128)(2,1)S(1)}, u32[]{:S(2)}, u32[]{:S(2)}) %collective-permute-start.14) | collective-permute-done | bytes 417824 | tf_op jit(solution)/shard_map/ppermute | solution.py:25
  89.9 0.8 copy-done.14
  90.7 3.7 %previous.1 = f32[1,256]{1,0:T(1,128)} custom-call(s32[1]{0:T(128)} %bitcast.26.first_ref.refs_0_, s32[1,256]{1,0:T(1,128)} %bitcast.54, f32[1,256]{1,0:T(1,128)} %get-tuple-element.63.refs_2_, bf16[256,768]{1,0:T(8,128)(2,1)} %get-tuple-element.64.refs_3_, bf16[272,768]{1,0:T(8,128)(2,1)} %copy-done.10, bf16[272,768]{1,0:T(8,128)(2,1)} %copy-done.12, ...), custom_call_target="tpu_custom_call" | custom-call | flops 561790976 | bytes 8261632 | tf_op jit(solution)/shard_map/previous/pallas_call | solution.py:298
  (44 shorter events, 1.1 us)
Async XLA Ops:
  0.6 5.3 %copy-start = (bf16[1024,768]{1,0:T(8,128)(2,1)S(1)}, bf16[1024,768]{1,0:T(8,128)(2,1)}, u32[]{:S(2)}) copy-start(bf16[1024,768]{1,0:T(8,128)(2,1)} %refs_2_.1) | copy-start | bytes 4718596
  0.6 5.3 %copy-start.6 = (s32[1024]{0:T(1024)S(1)}, s32[1024]{0:T(1024)}, u32[]{:S(2)}) copy-start(s32[1024]{0:T(1024)} %param.8) | copy-start | bytes 12292
  0.6 4.6 %copy-start.5 = (s32[4096]{0:T(1024)S(1)}, s32[4096]{0:T(1024)}, u32[]{:S(2)}) copy-start(s32[4096]{0:T(1024)} %param.9) | copy-start | bytes 49156
  6.0 37.0 %all-to-all-start.1 = ((bf16[64,8,640]{2,1,0:T(8,128)(2,1)}), bf16[64,8,640]{2,1,0:T(8,128)(2,1)S(1)}, u32[]{:S(2)}, u32[]{:S(2)}) async-start(bf16[64,8,640]{2,1,0:T(8,128)(2,1)} %bitcast.10), calls=%async_computation.1 | async-start | bytes 1310720 | tf_op jit(solution)/shard_map/cond/branch_1_fun/all_to_all | solution.py:349
  20.9 1.4 %copy-start.9 = (bf16[1024,768]{1,0:T(8,128)(2,1)S(1)}, bf16[1024,768]{1,0:T(8,128)(2,1)}, u32[]{:S(2)}) copy-start(bf16[1024,768]{1,0:T(8,128)(2,1)} %get-tuple-element.32) | copy-start | bytes 4718596 | tf_op jit(solution)/shard_map/cond
  24.4 10.5 %collective-permute-start.6 = (f32[2,1024]{1,0:T(2,128)S(1)}, f32[2,1024]{1,0:T(2,128)S(1)}, u32[]{:S(2)}, u32[]{:S(2)}) collective-permute-start(f32[2,1024]{1,0:T(2,128)S(1)} %pad_maximum_fusion.1), channel_id=1, source_target_pairs={{0,3},{1,0},{2,1},{3,2},{4,7},{5,4},{6,5},{7,6},{8,11},{9,8},{10,9... | collective-permute-start | bytes 24584 | tf_op jit(solution)/shard_map/cond/branch_1_fun/ppermute | solution.py:20
  26.8 8.1 %collective-permute-start.5 = (f32[2,1024]{1,0:T(2,128)S(1)}, f32[2,1024]{1,0:T(2,128)S(1)}, u32[]{:S(2)}, u32[]{:S(2)}) collective-permute-start(f32[2,1024]{1,0:T(2,128)S(1)} %pad_maximum_fusion.1), channel_id=1, source_target_pairs={{0,2},{1,3},{2,0},{3,1},{4,6},{5,7},{6,4},{7,5},{8,10},{9,11},{10,... | collective-permute-start | bytes 24584 | tf_op jit(solution)/shard_map/cond/branch_1_fun/ppermute | solution.py:20
  31.2 5.5 %collective-permute-start.4 = (f32[2,1024]{1,0:T(2,128)S(1)}, f32[2,1024]{1,0:T(2,128)S(1)}, u32[]{:S(2)}, u32[]{:S(2)}) collective-permute-start(f32[2,1024]{1,0:T(2,128)S(1)} %pad_maximum_fusion.1), channel_id=1, source_target_pairs={{0,1},{1,2},{2,3},{3,0},{4,5},{5,6},{6,7},{7,4},{8,9},{9,10},{10,1... | collective-permute-start | bytes 24584 | tf_op jit(solution)/shard_map/cond/branch_1_fun/ppermute | solution.py:20
  42.9 0.8 copy-start.1
  46.3 37.1 %copy-start.7 = (f32[1024]{0:T(1024)}, f32[1024]{0:T(1024)S(1)}, u32[]{:S(2)}) copy-start(f32[1024]{0:T(1024)S(1)} %get-tuple-element.50) | copy-start | bytes 12292
  46.3 11.3 %collective-permute-start.7 = (bf16[272,768]{1,0:T(8,128)(2,1)S(1)}, bf16[272,768]{1,0:T(8,128)(2,1)S(1)}, u32[]{:S(2)}, u32[]{:S(2)}) collective-permute-start(bf16[272,768]{1,0:T(8,128)(2,1)S(1)} %get-tuple-element.56), channel_id=1, source_target_pairs={{0,1},{1,2},{2,7},{3,4},{4,5},{5,6},{6,3},{7,0},{8,9},{9,10},{10,1... | collective-permute-start | bytes 1253384 | tf_op jit(solution)/shard_map/ppermute | solution.py:37
  49.7 12.4 %collective-permute-start.8 = (bf16[272,768]{1,0:T(8,128)(2,1)S(1)}, bf16[272,768]{1,0:T(8,128)(2,1)S(1)}, u32[]{:S(2)}, u32[]{:S(2)}) collective-permute-start(bf16[272,768]{1,0:T(8,128)(2,1)S(1)} %get-tuple-element.56), channel_id=1, source_target_pairs={{0,3},{1,0},{2,5},{3,6},{4,7},{5,4},{6,1},{7,2},{8,11},{9,8},{10,1... | collective-permute-start | bytes 1253384 | tf_op jit(solution)/shard_map/ppermute | solution.py:37
  52.1 11.5 %collective-permute-start.9 = (bf16[272,768]{1,0:T(8,128)(2,1)S(1)}, bf16[272,768]{1,0:T(8,128)(2,1)S(1)}, u32[]{:S(2)}, u32[]{:S(2)}) collective-permute-start(bf16[272,768]{1,0:T(8,128)(2,1)S(1)} %get-tuple-element.56), channel_id=1, source_target_pairs={{0,4},{1,5},{2,10},{3,11},{4,8},{5,9},{6,6},{7,7},{8,12},{9,13},{1... | collective-permute-start | bytes 1253384 | tf_op jit(solution)/shard_map/ppermute | solution.py:37
  54.1 9.5 %collective-permute-start.10 = (bf16[272,768]{1,0:T(8,128)(2,1)S(1)}, bf16[272,768]{1,0:T(8,128)(2,1)S(1)}, u32[]{:S(2)}, u32[]{:S(2)}) collective-permute-start(bf16[272,768]{1,0:T(8,128)(2,1)S(1)} %get-tuple-element.56), channel_id=1, source_target_pairs={{0,0},{1,1},{2,6},{3,7},{4,4},{5,5},{6,2},{7,3},{8,8},{9,9},{10,14... | collective-permute-start | bytes 1253384 | tf_op jit(solution)/shard_map/ppermute | solution.py:37
  57.6 16.2 %copy-start.2 = (bf16[272,768]{1,0:T(8,128)(2,1)}, bf16[272,768]{1,0:T(8,128)(2,1)S(1)}, u32[]{:S(2)}) copy-start(bf16[272,768]{1,0:T(8,128)(2,1)S(1)} %collective-permute-done.7.refs_1_) | copy-start | bytes 1253380
  62.1 11.7 %copy-start.3 = (bf16[272,768]{1,0:T(8,128)(2,1)}, bf16[272,768]{1,0:T(8,128)(2,1)S(1)}, u32[]{:S(2)}) copy-start(bf16[272,768]{1,0:T(8,128)(2,1)S(1)} %collective-permute-done.8.refs_2_) | copy-start | bytes 1253380
  63.6 26.3 %copy-start.10 = (bf16[272,768]{1,0:T(8,128)(2,1)}, bf16[272,768]{1,0:T(8,128)(2,1)S(1)}, u32[]{:S(2)}) copy-start(bf16[272,768]{1,0:T(8,128)(2,1)S(1)} %collective-permute-done.9.refs_4_) | copy-start | bytes 1253380
  63.6 10.2 %copy-start.4 = (bf16[272,768]{1,0:T(8,128)(2,1)}, bf16[272,768]{1,0:T(8,128)(2,1)S(1)}, u32[]{:S(2)}) copy-start(bf16[272,768]{1,0:T(8,128)(2,1)S(1)} %collective-permute-done.10.refs_0_) | copy-start | bytes 1253380
  63.6 14.8 %collective-permute-start.11 = (bf16[272,768]{1,0:T(8,128)(2,1)S(1)}, bf16[272,768]{1,0:T(8,128)(2,1)S(1)}, u32[]{:S(2)}, u32[]{:S(2)}) collective-permute-start(bf16[272,768]{1,0:T(8,128)(2,1)S(1)} %get-tuple-element.56), channel_id=1, source_target_pairs={{0,2},{1,3},{2,4},{3,5},{4,6},{5,7},{6,0},{7,1},{8,10},{9,11},{10,... | collective-permute-start | bytes 1253384 | tf_op jit(solution)/shard_map/ppermute | solution.py:37
  69.2 14.2 %collective-permute-start.12 = (bf16[272,768]{1,0:T(8,128)(2,1)S(1)}, bf16[272,768]{1,0:T(8,128)(2,1)S(1)}, u32[]{:S(2)}, u32[]{:S(2)}) collective-permute-start(bf16[272,768]{1,0:T(8,128)(2,1)S(1)} %collective-permute-done.7.refs_1_), channel_id=1, source_target_pairs={{0,4},{4,8},{8,12},{12,16},{16,20},{20,24},{24,28},{28,32},{32,36}... | collective-permute-start | bytes 1253384 | tf_op jit(solution)/shard_map/ppermute | solution.py:25
  71.1 14.0 %collective-permute-start.13 = (bf16[272,768]{1,0:T(8,128)(2,1)S(1)}, bf16[272,768]{1,0:T(8,128)(2,1)S(1)}, u32[]{:S(2)}, u32[]{:S(2)}) collective-permute-start(bf16[272,768]{1,0:T(8,128)(2,1)S(1)} %collective-permute-done.8.refs_2_), channel_id=1, source_target_pairs={{0,4},{4,8},{8,12},{12,16},{16,20},{20,24},{24,28},{28,32},{32,36}... | collective-permute-start | bytes 1253384 | tf_op jit(solution)/shard_map/ppermute | solution.py:25
  78.4 1.9 %copy-start.11 = (bf16[272,768]{1,0:T(8,128)(2,1)}, bf16[272,768]{1,0:T(8,128)(2,1)S(1)}, u32[]{:S(2)}) copy-start(bf16[272,768]{1,0:T(8,128)(2,1)S(1)} %collective-permute-done.11.refs_3_) | copy-start | bytes 1253380
  78.4 11.5 %collective-permute-start.14 = (bf16[272,768]{1,0:T(8,128)(2,1)S(1)}, bf16[272,768]{1,0:T(8,128)(2,1)S(1)}, u32[]{:S(2)}, u32[]{:S(2)}) collective-permute-start(bf16[272,768]{1,0:T(8,128)(2,1)S(1)} %collective-permute-done.11.refs_3_), channel_id=1, source_target_pairs={{0,4},{4,8},{8,12},{12,16},{16,20},{20,24},{24,28},{28,32},{32,36}... | collective-permute-start | bytes 1253384 | tf_op jit(solution)/shard_map/ppermute | solution.py:25
  83.4 6.5 %copy-start.12 = (bf16[272,768]{1,0:T(8,128)(2,1)}, bf16[272,768]{1,0:T(8,128)(2,1)S(1)}, u32[]{:S(2)}) copy-start(bf16[272,768]{1,0:T(8,128)(2,1)S(1)} %collective-permute-done.12.refs_5_) | copy-start | bytes 1253380
  85.2 4.7 %copy-start.13 = (bf16[272,768]{1,0:T(8,128)(2,1)}, bf16[272,768]{1,0:T(8,128)(2,1)S(1)}, u32[]{:S(2)}) copy-start(bf16[272,768]{1,0:T(8,128)(2,1)S(1)} %collective-permute-done.13.refs_6_) | copy-start | bytes 1253380
  89.9 0.8 copy-start.14

commit v3 on v2

--- a/solution.py
+++ b/solution.py
@@ -245,68 +245,77 @@
     return decoded(tags[:PART, 8:9], tags[:PART, 9:10])
 
 
-def picked_queries(first_place, count, part_refs):
-    queries = 0.0
-    for part in part_refs:
-        chosen = place_row(part) == first_place + iota((count, PART), 0)
-        queries = queries + dot(chosen.astype(jnp.bfloat16), part[...], 1, 0)
-    return queries
-
-
-def compared(best, queries, query_places, starts, part_refs, first_place):
-    for part in part_refs:
-        column = place_column(part) + first_place
-        similarity = dot(part[...], queries, 1, 1)
-        allowed = (column >= starts) & (column < query_places)
+def start_row(places, start_lines):
+    owner_rows = start_lines.shape[1]
+    here = (iota((owner_rows, PART), 0) == places).astype(jnp.bfloat16)
+    found = dot(start_lines, here, 1, 0)
+    return (found[0:1] * 64.0 + found[1:2]).astype(jnp.int32) - owner_rows
+
+
+def compared(best, queries_ref, places, starts, key_refs):
+    for key_ref, key_places in key_refs:
+        similarity = dot(key_ref[...], queries_ref[...], 1, 1)
+        allowed = (key_places >= starts) & (key_places < places)
         masked = jnp.where(allowed, similarity, -1.0)
         best = jnp.maximum(best, jnp.max(masked, axis=0, keepdims=True))
     return best
 
 
-def early_queries_kernel(first_ref, *refs):
-    *part_refs, queries_ref = refs
-    queries = picked_queries(first_ref[0], queries_ref.shape[0], part_refs)
-    queries_ref[...] = queries.astype(jnp.bfloat16)
-
-
-def own_kernel(first_ref, starts_ref, early_ref, *refs):
-    *part_refs, queries_ref, best_ref = refs
-    count = queries_ref.shape[0]
-    query_places = first_ref[0] + iota((1, count), 1)
-    late = picked_queries(first_ref[0], count, part_refs[-1:])
-    queries = (early_ref[...].astype(jnp.float32) + late).astype(jnp.bfloat16)
-    queries_ref[...] = queries
-    best = jnp.full((1, count), -1.0, jnp.float32)
-    best_ref[...] = compared(best, queries, query_places, starts_ref[...], part_refs, 0)
-
-
-def previous_kernel(first_ref, starts_ref, best_ref, queries_ref, *refs, owner_rows):
-    *part_refs, last_ref, out_ref, last_copy, arrived = refs
-    copy = pltpu.make_async_copy(last_ref, last_copy, arrived)
-    copy.start()
-    query_places = first_ref[0] + iota((1, queries_ref.shape[0]), 1)
-    queries = queries_ref[...]
-    starts = starts_ref[...]
-    best = compared(best_ref[...], queries, query_places, starts, part_refs, -owner_rows)
-    copy.wait()
-    out_ref[...] = compared(best, queries, query_places, starts, [last_copy], -owner_rows)
-
-
-def whole_call(kernel, out_shape, name, scalar, *arrays, left_there=0, scratch=()):
-    here = len(arrays) - left_there
+def near_kernel(starts_ref, here_ref, left_ref, right_ref, previous_ref, out_ref):
+    owner_rows = starts_ref.shape[1]
+    starts = starts_ref[...] + owner_rows
+    line = iota((16, owner_rows), 0)
+    start_lines = jnp.where(line == 0, starts // 64, jnp.where(line == 1, starts % 64, 0))
+    start_lines = start_lines.astype(jnp.float32).astype(jnp.bfloat16)
+    here = (here_ref, place_column(here_ref))
+    left = (left_ref, place_column(left_ref))
+    right = (right_ref, place_column(right_ref))
+    previous = (previous_ref, place_column(previous_ref) - owner_rows)
+    out_ref[...] = jnp.zeros(out_ref.shape, jnp.float32)
+    for part, queries_ref, keys in (
+        (0, here_ref, (here, left, right, previous)),
+        (1, left_ref, (right, previous)),
+        (2, right_ref, (previous,)),
+    ):
+        places = place_row(queries_ref)
+        starts = start_row(places, start_lines)
+        best = compared(jnp.full((1, PART), -1.0, jnp.float32), queries_ref, places, starts, keys)
+        out_ref[8 * part : 8 * part + 1, :PART] = best
+        out_ref[8 * part + 1 : 8 * part + 2, :PART] = places.astype(jnp.float32)
+        out_ref[8 * part + 2 : 8 * part + 3, :PART] = starts.astype(jnp.float32)
+
+
+def far_kernel(near_ref, right_ref, previous_left_ref, out_ref):
+    owner_rows = out_ref.shape[1]
+    lines = near_ref[16:24, :PART]
+    places, starts = lines[1:2].astype(jnp.int32), lines[2:3].astype(jnp.int32)
+    keys = (previous_left_ref, place_column(previous_left_ref) - owner_rows)
+    best_right = compared(lines[0:1], right_ref, places, starts, (keys,))
+    best = jnp.full((1, owner_rows), -1.0, jnp.float32)
+    lane = iota((PART, owner_rows), 1)
+    for part in range(3):
+        columns = near_ref[8 * part : 8 * part + 8, :].T
+        value = columns[:PART, 0:1]
+        if part == 2:
+            wide = jnp.broadcast_to(best_right, (8, PART))
+            wide = jnp.concatenate([wide, jnp.zeros((8, 3 * LANES - PART), jnp.float32)], axis=1)
+            value = wide.T[:PART, 0:1]
+        placed = jnp.where(columns[:PART, 1:2].astype(jnp.int32) == lane, value, -1.0)
+        best = jnp.maximum(best, jnp.max(placed, axis=0, keepdims=True))
+    out_ref[...] = best
+
+
+def whole_call(kernel, out_shape, name, *arrays):
     size = sum(array.size for array in arrays)
     return pl.pallas_call(
         kernel,
-        in_specs=[pl.BlockSpec(memory_space=pltpu.SMEM)]
-        + [pl.BlockSpec(memory_space=pltpu.VMEM)] * here
-        + [pl.BlockSpec(memory_space=pltpu.HBM)] * left_there,
+        in_specs=[pl.BlockSpec(memory_space=pltpu.VMEM)] * len(arrays),
         out_shape=out_shape,
-        scratch_shapes=scratch,
         cost_estimate=pl.CostEstimate(
             flops=2 * size * PART, transcendentals=0, bytes_accessed=8 * size
         ),
         name=name,
-    )(scalar, *arrays)
+    )(*arrays)
 
 
 def margin_of(embeddings, centroids, positions, slab_starts, slab_ends):
@@ -340,6 +349,7 @@
 
     packed, fits = pack_pairs(embeddings, positions, row_index, cent_index, chips, block_rows)
 
+    packed, fits, cluster_sizes = lax.optimization_barrier((packed, fits, cluster_sizes))
     cluster_ends = jnp.cumsum(cluster_sizes)
     cluster_starts = cluster_ends - cluster_sizes
     slab_ends = lax.dynamic_slice_in_dim(cluster_ends, cent_index * slab_size, slab_size)
@@ -380,48 +390,40 @@
         slab_ends,
     )
     base_place = row_index * block_rows
-    places = base_place + cent_index * quarter + jnp.arange(quarter, dtype=jnp.int32)
+    places = base_place + jnp.arange(block_rows, dtype=jnp.int32)
     started = jnp.where(cluster_starts[None, :] <= places[:, None], cluster_starts[None, :], 0)
     starts = (jnp.max(started, axis=1) - base_place)[None, :]
 
+    here = from_holders(held, 0, 0)
+    previous_here = from_holders(held, 0, 1)
+    right = from_holders(held, 3, 0)
     left = from_holders(held, 1, 0)
-    right = from_holders(held, 3, 0)
-    previous_here = from_holders(held, 0, 1)
-    here = from_holders(held, 0, 0)
-    held, left, right, previous_here, here = lax.optimization_barrier(
-        (held, left, right, previous_here, here)
-    )
-    across = from_holders(held, 2, 0)
+    here, previous_here, right, left, starts = lax.optimization_barrier(
+        (here, previous_here, right, left, starts)
+    )
     previous_left = to_next_owner(left)
-    previous_right = to_next_owner(right)
-
-    first = (cent_index * quarter)[None]
-    queries_shape = jax.ShapeDtypeStruct((quarter, features), jnp.bfloat16)
-    best_shape = jax.ShapeDtypeStruct((1, quarter), jnp.float32)
-    early = whole_call(
-        early_queries_kernel, queries_shape, "early_queries", first, here, left, right
-    )
-    across, early, starts = lax.optimization_barrier((across, early, starts))
-    previous_across = to_next_owner(across)
-    queries, best = whole_call(
-        own_kernel, (queries_shape, best_shape), "own", first, starts, early, here, left, right, across
+    near = whole_call(
+        near_kernel,
+        jax.ShapeDtypeStruct((24, 3 * LANES), jnp.float32),
+        "near",
+        starts,
+        here,
+        left,
+        right,
+        previous_here,
     )
     best = whole_call(
-        lambda *refs: previous_kernel(*refs, owner_rows=block_rows),
-        best_shape,
-        "previous",
-        first,
-        starts,
-        best,
-        queries,
-        previous_here,
+        far_kernel,
+        jax.ShapeDtypeStruct((1, block_rows), jnp.float32),
+        "far",
+        near,
+        right,
         previous_left,
-        previous_right,
-        previous_across,
-        left_there=1,
-        scratch=[pltpu.VMEM((PART, features), jnp.bfloat16), pltpu.SemaphoreType.DMA],
-    )
-    return (margin, best.reshape(quarter))
+    )
+    best = lax.all_to_all(
+        best.reshape(cent_count, 2, quarter // 2), "cent", split_axis=0, concat_axis=0, tiled=True
+    )
+    return (margin, jnp.max(best, axis=0).reshape(quarter))
 
 
 def solution(mesh):

time: 95.2 us -> 89.5 us (0.940)
  the two profiles are of different devices: /device:TPU:130 before, /device:TPU:64 now
where the time goes in v3:
time: 89.5 us; the launch traced here: 88.8 us
  starting transfers between devices  37.4 us (42%)
  waiting for transfers between devices  18.2 us (20%)
  Pallas kernels  13.3 us (15%)
  blocking collectives  8.87 us (10%)
  other arithmetic  4.3 us (5%)
  local copies, waits for them, and re-layouts  2.86 us (3%)
  matrix products  2.1 us (2%)
  between operations  1.49 us (2%)
    all_to_all x1, starting transfers between devices, by_pairs(): lax.all_to_all(packed, 'rows', split_axis=0, concat_axis=0, tiled=True, a...  15.8 us
    ppermute x3, starting transfers between devices, rotated(): lax.ppermute(shard, axis, [(i, (i + by) % peers) for i in range(peers)])  10.2 us
    ppermute x4, starting transfers between devices, from_holders(): return lax.ppermute(shard, ('rows', 'cent'), pairs)  9.48 us
    all_to_all x1, blocking collectives, on_device(): lax.all_to_all(best.reshape(cent_count, 2, quarter // 2), 'cent', split_a...  8.87 us
    pallas_call x2, Pallas kernels, whole_call(): pl.pallas_call(kernel, in_specs=[pl.BlockSpec(memory_space=pltpu.VMEM)] *...  6.98 us
    ppermute x4, waiting for transfers between devices, from_holders(): return lax.ppermute(shard, ('rows', 'cent'), pairs)  5.63 us
    ppermute x1, waiting for transfers between devices, to_next_owner(): lax.ppermute(shard, 'rows', [(row, row + 1) for row in range(row_count -...  5.35 us
    pallas_call x1, Pallas kernels, pack_pairs(): pl.pallas_call(lambda *refs: pack_pairs_kernel(*refs, owner_rows=owner_ro...  3.95 us
  transfers between devices with their start and end apart: 9, of which 7 were waited for; matrix products, arithmetic and copies ran while one was open for 6% of the time, Pallas kernels for 5%

profile of v3, /device:TPU:64, one launch (start us, length us, event | category | flops | bytes accessed | tf_op | source)
XLA Modules:
  0.0 88.8 jit_solution(11503073837009140486)
XLA Ops:
  0.7 4.0 %pack_pairs.1 = (bf16[512,640]{1,0:T(8,128)(2,1)}, s32[1]{0:T(128)}) custom-call(s32[1]{0:T(128)} %bitcast.20.refs_0_, s32[1]{0:T(128)} %bitcast.21.refs_1_, bf16[1024,768]{1,0:T(8,128)(2,1)} %refs_2_.1, s32[1,1024]{1,0:T(1,128)} %bitcast.35), custom_call_target="tpu_custom_call" | custom-call | tf_op jit(solution)/shard_map/pack_pairs/pallas_call | solution.py:124
  5.3 0.3 reduce-window.9
  5.7 0.1 slice_reduce_fusion
  6.0 40.2 %conditional.1 = (bf16[272,768]{1,0:T(8,128)(2,1)S(1)}, f32[1024]{0:T(1024)S(1)}) conditional(s32[]{:T(128)} %bitcast.23, (s32[]{:T(128)}, s32[1024]{0:T(1024)S(1)}, bf16[1024,768]{1,0:T(8,128)(2,1)S(1)}, bf16[1024,768]{1,0:T(8,128)(2,1)}, s32[1024]{0:T(1024)S(1)}, /*index=5*/s32[1024]{0:T(1024)S(1)}) %tuple.36, (bf16[512,640]{1,0:T(8,128)(2,1)}, ...), branch_computations={%region_2.6_spmd, %region_6.10_spmd} | conditional | flops 1621629952 | bytes 19341548 | solution.py:381
  6.0 15.8 %all-to-all-start.1 = ((bf16[64,8,640]{2,1,0:T(8,128)(2,1)}), bf16[64,8,640]{2,1,0:T(8,128)(2,1)S(1)}, u32[]{:S(2)}, u32[]{:S(2)}) async-start(bf16[64,8,640]{2,1,0:T(8,128)(2,1)} %bitcast.10), calls=%async_computation.1 | async-start | bytes 1310720 | tf_op jit(solution)/shard_map/cond/branch_1_fun/all_to_all | solution.py:359
  21.8 0.4 fusion.5
  22.2 1.0 %copy-done.11 = bf16[1024,768]{1,0:T(8,128)(2,1)S(1)} copy-done((bf16[1024,768]{1,0:T(8,128)(2,1)S(1)}, bf16[1024,768]{1,0:T(8,128)(2,1)}, u32[]{:S(2)}) %copy-start.11) | copy-done | bytes 1572888 | tf_op jit(solution)/shard_map/cond
  23.2 2.1 %fusion.11 = (f32[1024]{0:T(1024)S(1)}, f32[1024]{0:T(1024)S(1)}) fusion(s32[1024]{0:T(1024)S(1)} %get-tuple-element.35, s32[1024]{0:T(1024)S(1)} %get-tuple-element.34, s32[1024]{0:T(1024)S(1)} %get-tuple-element.33, bf16[1024,768]{1,0:T(8,128)(2,1)S(1)} %copy-done.11, bf16[1024,768]{1,0:T(8,128)(2,1)S(1)} %get-tuple-element.31, f32[1024]{0:T(1024)S(1)} %add_rsqrt_fusion.1), kind=kOutput, calls=%fused_computation.26 | convolution fusion | flops 1619261440 | bytes 3170304 | tf_op jit(solution)/shard_map/cond/branch_1_fun/dot_general | solution.py:322
  25.3 4.7 %collective-permute-start.6 = (f32[2,1024]{1,0:T(2,128)S(1)}, f32[2,1024]{1,0:T(2,128)S(1)}, u32[]{:S(2)}, u32[]{:S(2)}) collective-permute-start(f32[2,1024]{1,0:T(2,128)S(1)} %pad_maximum_fusion.1), channel_id=1, source_target_pairs={{0,3},{1,0},{2,1},{3,2},{4,7},{5,4},{6,5},{7,6},{8,11},{9,8},{10,9... | collective-permute-start | bytes 24584 | tf_op jit(solution)/shard_map/cond/branch_1_fun/ppermute | solution.py:20
  30.0 2.7 %collective-permute-start.5 = (f32[2,1024]{1,0:T(2,128)S(1)}, f32[2,1024]{1,0:T(2,128)S(1)}, u32[]{:S(2)}, u32[]{:S(2)}) collective-permute-start(f32[2,1024]{1,0:T(2,128)S(1)} %pad_maximum_fusion.1), channel_id=1, source_target_pairs={{0,2},{1,3},{2,0},{3,1},{4,6},{5,7},{6,4},{7,5},{8,10},{9,11},{10,... | collective-permute-start | bytes 24584 | tf_op jit(solution)/shard_map/cond/branch_1_fun/ppermute | solution.py:20
  32.7 2.8 %collective-permute-start.4 = (f32[2,1024]{1,0:T(2,128)S(1)}, f32[2,1024]{1,0:T(2,128)S(1)}, u32[]{:S(2)}, u32[]{:S(2)}) collective-permute-start(f32[2,1024]{1,0:T(2,128)S(1)} %pad_maximum_fusion.1), channel_id=1, source_target_pairs={{0,1},{1,2},{2,3},{3,0},{4,5},{5,6},{6,7},{7,4},{8,9},{9,10},{10,1... | collective-permute-start | bytes 24584 | tf_op jit(solution)/shard_map/cond/branch_1_fun/ppermute | solution.py:20
  35.6 1.5 %collective-permute-done.5 = f32[2,1024]{1,0:T(2,128)S(1)} collective-permute-done((f32[2,1024]{1,0:T(2,128)S(1)}, f32[2,1024]{1,0:T(2,128)S(1)}, u32[]{:S(2)}, u32[]{:S(2)}) %collective-permute-start.5) | collective-permute-done | bytes 8224 | tf_op jit(solution)/shard_map/cond/branch_1_fun/ppermute | solution.py:20
  37.1 2.4 %collective-permute-done.4 = f32[2,1024]{1,0:T(2,128)S(1)} collective-permute-done((f32[2,1024]{1,0:T(2,128)S(1)}, f32[2,1024]{1,0:T(2,128)S(1)}, u32[]{:S(2)}, u32[]{:S(2)}) %collective-permute-start.4) | collective-permute-done | bytes 8224 | tf_op jit(solution)/shard_map/cond/branch_1_fun/ppermute | solution.py:20
  39.5 3.3 %all-to-all-done.1 = bf16[64,8,640]{2,1,0:T(8,128)(2,1)S(1)} async-done(((bf16[64,8,640]{2,1,0:T(8,128)(2,1)}), bf16[64,8,640]{2,1,0:T(8,128)(2,1)S(1)}, u32[]{:S(2)}, u32[]{:S(2)}) %all-to-all-start.1) | async-done | bytes 655392 | tf_op jit(solution)/shard_map/cond/branch_1_fun/all_to_all | solution.py:359
  42.8 0.8 copy-done.1
  43.7 2.3 %compact_pairs.1 = bf16[272,768]{1,0:T(8,128)(2,1)S(1)} custom-call(bf16[512,640]{1,0:T(8,128)(2,1)} %bitcast.33), custom_call_target="tpu_custom_call" | custom-call | tf_op jit(solution)/shard_map/cond/branch_1_fun/compact_pairs/pallas_call | solution.py:224
  46.2 3.4 %collective-permute-start.10 = (bf16[272,768]{1,0:T(8,128)(2,1)S(1)}, bf16[272,768]{1,0:T(8,128)(2,1)S(1)}, u32[]{:S(2)}, u32[]{:S(2)}) collective-permute-start(bf16[272,768]{1,0:T(8,128)(2,1)S(1)} %get-tuple-element.56), channel_id=1, source_target_pairs={{0,1},{1,2},{2,7},{3,4},{4,5},{5,6},{6,3},{7,0},{8,9},{9,10},{10,1... | collective-permute-start | bytes 1253384 | tf_op jit(solution)/shard_map/ppermute | solution.py:37
  49.6 3.2 %collective-permute-start.9 = (bf16[272,768]{1,0:T(8,128)(2,1)S(1)}, bf16[272,768]{1,0:T(8,128)(2,1)S(1)}, u32[]{:S(2)}, u32[]{:S(2)}) collective-permute-start(bf16[272,768]{1,0:T(8,128)(2,1)S(1)} %get-tuple-element.56), channel_id=1, source_target_pairs={{0,3},{1,0},{2,5},{3,6},{4,7},{5,4},{6,1},{7,2},{8,11},{9,8},{10,1... | collective-permute-start | bytes 1253384 | tf_op jit(solution)/shard_map/ppermute | solution.py:37
  52.8 2.2 %collective-permute-start.8 = (bf16[272,768]{1,0:T(8,128)(2,1)S(1)}, bf16[272,768]{1,0:T(8,128)(2,1)S(1)}, u32[]{:S(2)}, u32[]{:S(2)}) collective-permute-start(bf16[272,768]{1,0:T(8,128)(2,1)S(1)} %get-tuple-element.56), channel_id=1, source_target_pairs={{0,4},{1,5},{2,10},{3,11},{4,8},{5,9},{6,6},{7,7},{8,12},{9,13},{1... | collective-permute-start | bytes 1253384 | tf_op jit(solution)/shard_map/ppermute | solution.py:37
  55.0 0.7 collective-permute-start.7
  55.7 2.3 %select_reduce_fusion.2 = s32[1024]{0:T(1024)S(1)} fusion(s32[4096]{0:T(1024)S(1)} %get-tuple-element.66, s32[1024]{0:T(1024)S(1)} %iota_add_fusion), kind=kLoop, calls=%fused_computation.20 | loop fusion | flops 12581888 | bytes 24576 | tf_op jit(solution)/shard_map/reduce_max | solution.py:395
  58.0 0.6 broadcast_subtract_fusion
  58.6 2.5 %collective-permute-done.10.left_ref = bf16[272,768]{1,0:T(8,128)(2,1)S(1)} collective-permute-done((bf16[272,768]{1,0:T(8,128)(2,1)S(1)}, bf16[272,768]{1,0:T(8,128)(2,1)S(1)}, u32[]{:S(2)}, u32[]{:S(2)}) %collective-permute-start.10) | collective-permute-done | bytes 417824 | tf_op jit(solution)/shard_map/ppermute | solution.py:37
  61.1 1.3 %collective-permute-done.9.right_ref = bf16[272,768]{1,0:T(8,128)(2,1)S(1)} collective-permute-done((bf16[272,768]{1,0:T(8,128)(2,1)S(1)}, bf16[272,768]{1,0:T(8,128)(2,1)S(1)}, u32[]{:S(2)}, u32[]{:S(2)}) %collective-permute-start.9) | collective-permute-done | bytes 417824 | tf_op jit(solution)/shard_map/ppermute | solution.py:37
  62.4 1.8 %collective-permute-done.8.previous_ref = bf16[272,768]{1,0:T(8,128)(2,1)S(1)} collective-permute-done((bf16[272,768]{1,0:T(8,128)(2,1)S(1)}, bf16[272,768]{1,0:T(8,128)(2,1)S(1)}, u32[]{:S(2)}, u32[]{:S(2)}) %collective-permute-start.8) | collective-permute-done | bytes 417824 | tf_op jit(solution)/shard_map/ppermute | solution.py:37
  64.3 1.9 %collective-permute-start.11 = (bf16[272,768]{1,0:T(8,128)(2,1)S(1)}, bf16[272,768]{1,0:T(8,128)(2,1)S(1)}, u32[]{:S(2)}, u32[]{:S(2)}) collective-permute-start(bf16[272,768]{1,0:T(8,128)(2,1)S(1)} %collective-permute-done.10.left_ref), channel_id=1, source_target_pairs={{0,4},{4,8},{8,12},{12,16},{16,20},{20,24},{24,28},{28,32},{32,36}... | collective-permute-start | bytes 1253384 | tf_op jit(solution)/shard_map/ppermute | solution.py:25
  66.2 4.2 %near.1.near_ref = f32[24,384]{1,0:T(8,128)} custom-call(s32[1,1024]{1,0:T(1,128)} %bitcast.37, bf16[272,768]{1,0:T(8,128)(2,1)} %copy-done.5, bf16[272,768]{1,0:T(8,128)(2,1)} %copy-done.3, bf16[272,768]{1,0:T(8,128)(2,1)} %copy-done.2, bf16[272,768]{1,0:T(8,128)(2,1)} %copy-done.4), custom_call_target="tpu_custom_call" | custom-call | flops 455114752 | bytes 6692864 | tf_op jit(solution)/shard_map/near/pallas_call | solution.py:310
  70.4 5.3 %collective-permute-done.11.previous_left_ref = bf16[272,768]{1,0:T(8,128)(2,1)S(1)} collective-permute-done((bf16[272,768]{1,0:T(8,128)(2,1)S(1)}, bf16[272,768]{1,0:T(8,128)(2,1)S(1)}, u32[]{:S(2)}, u32[]{:S(2)}) %collective-permute-start.11) | collective-permute-done | bytes 417824 | tf_op jit(solution)/shard_map/ppermute | solution.py:25
  75.7 0.8 copy-done.6
  76.5 2.8 %far.1 = f32[1,1024]{1,0:T(1,128)} custom-call(f32[24,384]{1,0:T(8,128)} %near.1.near_ref, bf16[272,768]{1,0:T(8,128)(2,1)} %copy-done.2, bf16[272,768]{1,0:T(8,128)(2,1)} %copy-done.6), custom_call_target="tpu_custom_call" | custom-call | flops 232292352 | bytes 3416064 | tf_op jit(solution)/shard_map/far/pallas_call | solution.py:310
  79.3 8.9 %all_to_all.17 = f32[4,2,128]{2,1,0:T(2,128)S(1)} all-to-all(f32[4,2,128]{2,1,0:T(2,128)} %bitcast.38), channel_id=1, replica_groups=mesh['rows'=128,'cent'=4] {'cent'}, dimensions={0} | all-to-all | bytes 8192 | tf_op jit(solution)/shard_map/all_to_all | solution.py:423
  88.2 0.6 reduce_max.37
  (33 shorter events, 0.3 us)
Async XLA Ops:
  0.6 5.3 %copy-start = (bf16[1024,768]{1,0:T(8,128)(2,1)S(1)}, bf16[1024,768]{1,0:T(8,128)(2,1)}, u32[]{:S(2)}) copy-start(bf16[1024,768]{1,0:T(8,128)(2,1)} %refs_2_.1) | copy-start | bytes 4718596
  0.6 5.3 %copy-start.8 = (s32[1024]{0:T(1024)S(1)}, s32[1024]{0:T(1024)}, u32[]{:S(2)}) copy-start(s32[1024]{0:T(1024)} %param.8) | copy-start | bytes 12292
  0.7 4.7 %copy-start.7 = (s32[4096]{0:T(1024)S(1)}, s32[4096]{0:T(1024)}, u32[]{:S(2)}) copy-start(s32[4096]{0:T(1024)} %param.9) | copy-start | bytes 49156
  6.0 36.9 %all-to-all-start.1 = ((bf16[64,8,640]{2,1,0:T(8,128)(2,1)}), bf16[64,8,640]{2,1,0:T(8,128)(2,1)S(1)}, u32[]{:S(2)}, u32[]{:S(2)}) async-start(bf16[64,8,640]{2,1,0:T(8,128)(2,1)} %bitcast.10), calls=%async_computation.1 | async-start | bytes 1310720 | tf_op jit(solution)/shard_map/cond/branch_1_fun/all_to_all | solution.py:359
  21.8 1.4 %copy-start.11 = (bf16[1024,768]{1,0:T(8,128)(2,1)S(1)}, bf16[1024,768]{1,0:T(8,128)(2,1)}, u32[]{:S(2)}) copy-start(bf16[1024,768]{1,0:T(8,128)(2,1)} %get-tuple-element.32) | copy-start | bytes 4718596 | tf_op jit(solution)/shard_map/cond
  25.3 10.2 %collective-permute-start.6 = (f32[2,1024]{1,0:T(2,128)S(1)}, f32[2,1024]{1,0:T(2,128)S(1)}, u32[]{:S(2)}, u32[]{:S(2)}) collective-permute-start(f32[2,1024]{1,0:T(2,128)S(1)} %pad_maximum_fusion.1), channel_id=1, source_target_pairs={{0,3},{1,0},{2,1},{3,2},{4,7},{5,4},{6,5},{7,6},{8,11},{9,8},{10,9... | collective-permute-start | bytes 24584 | tf_op jit(solution)/shard_map/cond/branch_1_fun/ppermute | solution.py:20
  30.0 7.1 %collective-permute-start.5 = (f32[2,1024]{1,0:T(2,128)S(1)}, f32[2,1024]{1,0:T(2,128)S(1)}, u32[]{:S(2)}, u32[]{:S(2)}) collective-permute-start(f32[2,1024]{1,0:T(2,128)S(1)} %pad_maximum_fusion.1), channel_id=1, source_target_pairs={{0,2},{1,3},{2,0},{3,1},{4,6},{5,7},{6,4},{7,5},{8,10},{9,11},{10,... | collective-permute-start | bytes 24584 | tf_op jit(solution)/shard_map/cond/branch_1_fun/ppermute | solution.py:20
  32.7 6.8 %collective-permute-start.4 = (f32[2,1024]{1,0:T(2,128)S(1)}, f32[2,1024]{1,0:T(2,128)S(1)}, u32[]{:S(2)}, u32[]{:S(2)}) collective-permute-start(f32[2,1024]{1,0:T(2,128)S(1)} %pad_maximum_fusion.1), channel_id=1, source_target_pairs={{0,1},{1,2},{2,3},{3,0},{4,5},{5,6},{6,7},{7,4},{8,9},{9,10},{10,1... | collective-permute-start | bytes 24584 | tf_op jit(solution)/shard_map/cond/branch_1_fun/ppermute | solution.py:20
  42.8 0.8 copy-start.1
  46.2 42.6 %copy-start.9 = (f32[1024]{0:T(1024)}, f32[1024]{0:T(1024)S(1)}, u32[]{:S(2)}) copy-start(f32[1024]{0:T(1024)S(1)} %get-tuple-element.48) | copy-start | bytes 12292
  46.2 14.9 %collective-permute-start.10 = (bf16[272,768]{1,0:T(8,128)(2,1)S(1)}, bf16[272,768]{1,0:T(8,128)(2,1)S(1)}, u32[]{:S(2)}, u32[]{:S(2)}) collective-permute-start(bf16[272,768]{1,0:T(8,128)(2,1)S(1)} %get-tuple-element.56), channel_id=1, source_target_pairs={{0,1},{1,2},{2,7},{3,4},{4,5},{5,6},{6,3},{7,0},{8,9},{9,10},{10,1... | collective-permute-start | bytes 1253384 | tf_op jit(solution)/shard_map/ppermute | solution.py:37
  49.6 12.8 %collective-permute-start.9 = (bf16[272,768]{1,0:T(8,128)(2,1)S(1)}, bf16[272,768]{1,0:T(8,128)(2,1)S(1)}, u32[]{:S(2)}, u32[]{:S(2)}) collective-permute-start(bf16[272,768]{1,0:T(8,128)(2,1)S(1)} %get-tuple-element.56), channel_id=1, source_target_pairs={{0,3},{1,0},{2,5},{3,6},{4,7},{5,4},{6,1},{7,2},{8,11},{9,8},{10,1... | collective-permute-start | bytes 1253384 | tf_op jit(solution)/shard_map/ppermute | solution.py:37
  52.8 11.5 %collective-permute-start.8 = (bf16[272,768]{1,0:T(8,128)(2,1)S(1)}, bf16[272,768]{1,0:T(8,128)(2,1)S(1)}, u32[]{:S(2)}, u32[]{:S(2)}) collective-permute-start(bf16[272,768]{1,0:T(8,128)(2,1)S(1)} %get-tuple-element.56), channel_id=1, source_target_pairs={{0,4},{1,5},{2,10},{3,11},{4,8},{5,9},{6,6},{7,7},{8,12},{9,13},{1... | collective-permute-start | bytes 1253384 | tf_op jit(solution)/shard_map/ppermute | solution.py:37
  55.0 9.3 %collective-permute-start.7 = (bf16[272,768]{1,0:T(8,128)(2,1)S(1)}, bf16[272,768]{1,0:T(8,128)(2,1)S(1)}, u32[]{:S(2)}, u32[]{:S(2)}) collective-permute-start(bf16[272,768]{1,0:T(8,128)(2,1)S(1)} %get-tuple-element.56), channel_id=1, source_target_pairs={{0,0},{1,1},{2,6},{3,7},{4,4},{5,5},{6,2},{7,3},{8,8},{9,9},{10,14... | collective-permute-start | bytes 1253384 | tf_op jit(solution)/shard_map/ppermute | solution.py:37
  61.1 5.1 %copy-start.3 = (bf16[272,768]{1,0:T(8,128)(2,1)}, bf16[272,768]{1,0:T(8,128)(2,1)S(1)}, u32[]{:S(2)}) copy-start(bf16[272,768]{1,0:T(8,128)(2,1)S(1)} %collective-permute-done.10.left_ref) | copy-start | bytes 1253380
  62.4 3.8 %copy-start.2 = (bf16[272,768]{1,0:T(8,128)(2,1)}, bf16[272,768]{1,0:T(8,128)(2,1)S(1)}, u32[]{:S(2)}) copy-start(bf16[272,768]{1,0:T(8,128)(2,1)S(1)} %collective-permute-done.9.right_ref) | copy-start | bytes 1253380
  64.3 2.0 %copy-start.4 = (bf16[272,768]{1,0:T(8,128)(2,1)}, bf16[272,768]{1,0:T(8,128)(2,1)S(1)}, u32[]{:S(2)}) copy-start(bf16[272,768]{1,0:T(8,128)(2,1)S(1)} %collective-permute-done.8.previous_ref) | copy-start | bytes 1253380
  64.3 2.0 %copy-start.5 = (bf16[272,768]{1,0:T(8,128)(2,1)}, bf16[272,768]{1,0:T(8,128)(2,1)S(1)}, u32[]{:S(2)}) copy-start(bf16[272,768]{1,0:T(8,128)(2,1)S(1)} %collective-permute-done.7.here_ref) | copy-start | bytes 1253380
  64.3 11.5 %collective-permute-start.11 = (bf16[272,768]{1,0:T(8,128)(2,1)S(1)}, bf16[272,768]{1,0:T(8,128)(2,1)S(1)}, u32[]{:S(2)}, u32[]{:S(2)}) collective-permute-start(bf16[272,768]{1,0:T(8,128)(2,1)S(1)} %collective-permute-done.10.left_ref), channel_id=1, source_target_pairs={{0,4},{4,8},{8,12},{12,16},{16,20},{20,24},{24,28},{28,32},{32,36}... | collective-permute-start | bytes 1253384 | tf_op jit(solution)/shard_map/ppermute | solution.py:25
  75.7 0.8 copy-start.6

commit v4 on v3

--- a/solution.py
+++ b/solution.py
@@ -1,3 +1,5 @@
+from functools import partial
+
 import jax
 import jax.numpy as jnp
 from jax import lax
@@ -8,8 +10,9 @@
 SLOTS = 4
 LANES = 128
 TAG_BASE = 32
-PAIR_SLOTS = 6
+PAIR_SLOTS = (5, 6)
 PAIR_ROWS = 8
+PAIR_TILES = {5: 4, 6: 5}
 HELD = 264
 PART = 272
 NOWHERE = -4096
@@ -64,7 +67,15 @@
     return local // TAG_BASE + 1, local % TAG_BASE
 
 
-def pack_pairs_kernel(row_ref, cent_ref, rows_ref, places_ref, out_ref, fits_ref, *, owner_rows):
+def spilled(slot, tile, pair_slots, feature_tiles):
+    wide = PAIR_TILES[pair_slots]
+    cell = slot * (feature_tiles - wide) + tile - wide
+    return pair_slots + cell // wide, cell % wide
+
+
+def pack_pairs_kernel(
+    row_ref, cent_ref, rows_ref, places_ref, out_ref, path_ref, *, owner_rows, pair_slots
+):
     row_index = row_ref[0]
     sibling = cent_ref[0] // 2
     half = cent_ref[0] % 2
@@ -85,10 +96,13 @@
         so_far = so_far + jnp.sum(marks, axis=1, keepdims=True)
     rank = jnp.concatenate(ranks, axis=1).astype(jnp.int32)
     plane = ((owners + row_index) % 2) * 2 + rank % 2
-    spare = (plane == iota((8, count), 0)).astype(jnp.float32)
-    held = jnp.max(jnp.sum(spare, axis=1, keepdims=True) - float(HELD), axis=0, keepdims=True)
-    over = jnp.max(rank.astype(jnp.float32), axis=1, keepdims=True) - float(2 * PAIR_SLOTS - 1)
-    fits_ref[0] = (jnp.max(jnp.maximum(held, over)) < 0.5).astype(jnp.int32)
+    counts = jnp.sum((plane == iota((8, count), 0)).astype(jnp.float32), axis=1, keepdims=True)
+    crowded = jnp.max(counts) > HELD
+    most = jnp.max(rank.astype(jnp.float32))
+    path = jnp.int32(0)
+    for slots_there in PAIR_SLOTS:
+        path = path + (crowded | (most >= 2 * slots_there)).astype(jnp.int32)
+    path_ref[0] = path
 
     mine = plane == sibling * 2 + half
     block = owners // 2 * PAIR_ROWS
@@ -105,24 +119,25 @@
     sender = iota((chips, count), 0) == jnp.where(mine, owners // 2, -1)
     tags = dot(sender.astype(jnp.bfloat16), tags, 1, 1)
     tags = jnp.broadcast_to(tags[:, None, :], (chips, PAIR_ROWS, LANES)).reshape(slots, LANES)
-    wide = features - LANES
-    rest = sent[:, wide:]
+    wide = PAIR_TILES[pair_slots]
+    tiles = features // LANES
     line = iota((slots, LANES), 0) % PAIR_ROWS
-    for tile in range(PAIR_SLOTS - 1):
-        lanes = slice(tile * LANES, (tile + 1) * LANES)
-        moved = pltpu.roll(rest, PAIR_SLOTS - tile, 0)
-        value = jnp.where(line == PAIR_SLOTS, moved, sent[:, lanes])
-        if tile == 0:
-            value = jnp.where(line == PAIR_SLOTS + 1, pltpu.roll(rest, 2, 0), value)
-        if tile == 1:
-            value = jnp.where(line == PAIR_SLOTS + 1, tags, value)
-        out_ref[:, lanes] = value.astype(jnp.bfloat16)
-
-
-def pack_pairs(rows, places, row_index, cent_index, chips, owner_rows):
+    values = [sent[:, tile * LANES : (tile + 1) * LANES] for tile in range(tiles)]
+    for slot in range(pair_slots):
+        for tile in range(wide, tiles):
+            row, lanes = spilled(slot, tile, pair_slots, tiles)
+            moved = pltpu.roll(values[tile], row - slot, 0)
+            values[lanes] = jnp.where(line == row, moved, values[lanes])
+    row, lanes = spilled(pair_slots, wide, pair_slots, tiles)
+    values[lanes] = jnp.where(line == row, tags, values[lanes])
+    for tile in range(wide):
+        out_ref[:, tile * LANES : (tile + 1) * LANES] = values[tile].astype(jnp.bfloat16)
+
+
+def pack_pairs(rows, places, row_index, cent_index, chips, owner_rows, pair_slots):
     count, features = rows.shape
     return pl.pallas_call(
-        lambda *refs: pack_pairs_kernel(*refs, owner_rows=owner_rows),
+        lambda *refs: pack_pairs_kernel(*refs, owner_rows=owner_rows, pair_slots=pair_slots),
         in_specs=[
             pl.BlockSpec(memory_space=pltpu.SMEM),
             pl.BlockSpec(memory_space=pltpu.SMEM),
@@ -134,10 +149,10 @@
             pl.BlockSpec(memory_space=pltpu.SMEM),
         ),
         out_shape=(
-            jax.ShapeDtypeStruct((chips * PAIR_ROWS, features - LANES), jnp.bfloat16),
+            jax.ShapeDtypeStruct((chips * PAIR_ROWS, PAIR_TILES[pair_slots] * LANES), jnp.bfloat16),
             jax.ShapeDtypeStruct((1,), jnp.int32),
         ),
-        name="pack_pairs",
+        name=f"pack_pairs_{pair_slots}",
     )(row_index[None], cent_index[None], rows, places[None])
 
 
@@ -159,22 +174,28 @@
     out_ref[PART - 16 :, :PART] = (kept + lines).astype(jnp.bfloat16)
 
 
-def compact_pairs_kernel(got_ref, out_ref):
-    slots, wide = got_ref.shape
+def compact_pairs_kernel(got_ref, out_ref, *, pair_slots):
+    slots = got_ref.shape[0]
+    wide = PAIR_TILES[pair_slots]
+    tiles = out_ref.shape[1] // LANES
     line = iota((slots, LANES), 0) % PAIR_ROWS
     lane = iota((slots, LANES), 1)
-    rest = jnp.zeros((slots, LANES), jnp.float32)
+    values = [
+        got_ref[:, tile * LANES : (tile + 1) * LANES].astype(jnp.float32) for tile in range(wide)
+    ]
+    tag_row, lanes = spilled(pair_slots, wide, pair_slots, tiles)
+    tags = values[lanes]
     placed = jnp.zeros((slots, LANES), jnp.float32)
-    tags = got_ref[:, LANES : 2 * LANES].astype(jnp.float32)
-    for slot in range(PAIR_SLOTS):
-        tile = slot % (PAIR_SLOTS - 1)
-        up = PAIR_SLOTS - slot if slot < PAIR_SLOTS - 1 else 2
-        value = got_ref[:, tile * LANES : (tile + 1) * LANES].astype(jnp.float32)
-        rest = jnp.where(line == slot, pltpu.roll(value, slots - up, 0), rest)
-        moved = pltpu.roll(tags, slots - (PAIR_ROWS - 1 - slot), 0)
+    rest = [jnp.zeros((slots, LANES), jnp.float32)] * (tiles - wide)
+    for slot in range(pair_slots):
+        for tile in range(wide, tiles):
+            row, lanes = spilled(slot, tile, pair_slots, tiles)
+            moved = pltpu.roll(values[lanes], slots - (row - slot), 0)
+            rest[tile - wide] = jnp.where(line == slot, moved, rest[tile - wide])
+        moved = pltpu.roll(tags, slots - (tag_row - slot), 0)
         moved = pltpu.roll(moved, (LANES - 2 * slot) % LANES, 1) if slot else moved
         placed = jnp.where((line == slot) & (lane < 2), moved, placed)
-    store_part(out_ref, placed, [got_ref[...], rest.astype(jnp.bfloat16)])
+    store_part(out_ref, placed, [got_ref[...]] + [tile.astype(jnp.bfloat16) for tile in rest])
 
 
 def pack_kernel(cent_ref, rows_ref, places_ref, out_ref, *, owner_rows):
@@ -261,7 +282,18 @@
     return best
 
 
-def near_kernel(starts_ref, here_ref, left_ref, right_ref, previous_ref, out_ref):
+def at_places(best, places, values):
+    lines = jnp.concatenate([values, places.astype(jnp.float32)], axis=0)
+    lines = jnp.concatenate([lines, jnp.zeros((6, PART), jnp.float32)], axis=0)
+    spare = jnp.zeros((8, 3 * LANES - PART), jnp.float32)
+    columns = jnp.concatenate([lines, spare], axis=1).T
+    owner_rows = best.shape[1]
+    there = columns[:PART, 1:2].astype(jnp.int32) == iota((PART, owner_rows), 1)
+    placed = jnp.where(there, columns[:PART, 0:1], -1.0)
+    return jnp.maximum(best, jnp.max(placed, axis=0, keepdims=True))
+
+
+def near_kernel(starts_ref, here_ref, left_ref, right_ref, previous_ref, best_ref, right_lines_ref):
     owner_rows = starts_ref.shape[1]
     starts = starts_ref[...] + owner_rows
     line = iota((16, owner_rows), 0)
@@ -271,38 +303,30 @@
     left = (left_ref, place_column(left_ref))
     right = (right_ref, place_column(right_ref))
     previous = (previous_ref, place_column(previous_ref) - owner_rows)
-    out_ref[...] = jnp.zeros(out_ref.shape, jnp.float32)
-    for part, queries_ref, keys in (
-        (0, here_ref, (here, left, right, previous)),
-        (1, left_ref, (right, previous)),
-        (2, right_ref, (previous,)),
+    placed = jnp.full((1, owner_rows), -1.0, jnp.float32)
+    for queries_ref, keys in (
+        (here_ref, (here, left, right, previous)),
+        (left_ref, (right, previous)),
+        (right_ref, (previous,)),
     ):
         places = place_row(queries_ref)
         starts = start_row(places, start_lines)
         best = compared(jnp.full((1, PART), -1.0, jnp.float32), queries_ref, places, starts, keys)
-        out_ref[8 * part : 8 * part + 1, :PART] = best
-        out_ref[8 * part + 1 : 8 * part + 2, :PART] = places.astype(jnp.float32)
-        out_ref[8 * part + 2 : 8 * part + 3, :PART] = starts.astype(jnp.float32)
-
-
-def far_kernel(near_ref, right_ref, previous_left_ref, out_ref):
+        if queries_ref is not right_ref:
+            placed = at_places(placed, places, best)
+    best_ref[...] = placed
+    right_lines_ref[0:1, :] = best
+    right_lines_ref[1:2, :] = places.astype(jnp.float32)
+    right_lines_ref[2:3, :] = starts.astype(jnp.float32)
+
+
+def far_kernel(best_ref, right_lines_ref, right_ref, previous_left_ref, out_ref):
     owner_rows = out_ref.shape[1]
-    lines = near_ref[16:24, :PART]
-    places, starts = lines[1:2].astype(jnp.int32), lines[2:3].astype(jnp.int32)
+    places = right_lines_ref[1:2, :].astype(jnp.int32)
+    starts = right_lines_ref[2:3, :].astype(jnp.int32)
     keys = (previous_left_ref, place_column(previous_left_ref) - owner_rows)
-    best_right = compared(lines[0:1], right_ref, places, starts, (keys,))
-    best = jnp.full((1, owner_rows), -1.0, jnp.float32)
-    lane = iota((PART, owner_rows), 1)
-    for part in range(3):
-        columns = near_ref[8 * part : 8 * part + 8, :].T
-        value = columns[:PART, 0:1]
-        if part == 2:
-            wide = jnp.broadcast_to(best_right, (8, PART))
-            wide = jnp.concatenate([wide, jnp.zeros((8, 3 * LANES - PART), jnp.float32)], axis=1)
-            value = wide.T[:PART, 0:1]
-        placed = jnp.where(columns[:PART, 1:2].astype(jnp.int32) == lane, value, -1.0)
-        best = jnp.maximum(best, jnp.max(placed, axis=0, keepdims=True))
-    out_ref[...] = best
+    best = compared(right_lines_ref[0:1, :], right_ref, places, starts, (keys,))
+    out_ref[...] = at_places(best_ref[...], places, best)
 
 
 def whole_call(kernel, out_shape, name, *arrays):
@@ -347,15 +371,22 @@
     cent_index = lax.axis_index("cent")
     chips = row_count // 2
 
-    packed, fits = pack_pairs(embeddings, positions, row_index, cent_index, chips, block_rows)
-
-    packed, fits, cluster_sizes = lax.optimization_barrier((packed, fits, cluster_sizes))
+    def packed_in(pair_slots, embeddings, positions):
+        return pack_pairs(
+            embeddings, positions, row_index, cent_index, chips, block_rows, pair_slots
+        )
+
+    packed, path = packed_in(PAIR_SLOTS[0], embeddings, positions)
+
+    packed, path, cluster_sizes = lax.optimization_barrier((packed, path, cluster_sizes))
     cluster_ends = jnp.cumsum(cluster_sizes)
     cluster_starts = cluster_ends - cluster_sizes
     slab_ends = lax.dynamic_slice_in_dim(cluster_ends, cent_index * slab_size, slab_size)
     slab_starts = lax.dynamic_slice_in_dim(cluster_starts, cent_index * slab_size, slab_size)
 
-    def by_pairs(packed, embeddings, centroids, positions, slab_starts, slab_ends):
+    def by_pairs(pair_slots, packed, embeddings, centroids, positions, slab_starts, slab_ends):
+        if pair_slots != PAIR_SLOTS[0]:
+            packed, _ = packed_in(pair_slots, embeddings, positions)
         got = lax.all_to_all(
             packed,
             "rows",
@@ -365,7 +396,8 @@
             axis_index_groups=[list(range(core, row_count, 2)) for core in range(2)],
         )
         margin = margin_of(embeddings, centroids, positions, slab_starts, slab_ends)
-        return compacted(compact_pairs_kernel, got, features, "compact_pairs"), margin
+        kernel = partial(compact_pairs_kernel, pair_slots=pair_slots)
+        return compacted(kernel, got, features, f"compact_pairs_{pair_slots}"), margin
 
     def by_quarters(packed, embeddings, centroids, positions, slab_starts, slab_ends):
         packed = pack(embeddings, positions, cent_index, row_count, block_rows, cent_count)
@@ -378,10 +410,9 @@
         )
         return from_holders(part, 0, 0), margin
 
-    held, margin = lax.cond(
-        fits[0] != 0,
-        by_pairs,
-        by_quarters,
+    held, margin = lax.switch(
+        path[0],
+        [partial(by_pairs, pair_slots) for pair_slots in PAIR_SLOTS] + [by_quarters],
         packed,
         embeddings,
         centroids,
@@ -402,9 +433,10 @@
         (here, previous_here, right, left, starts)
     )
     previous_left = to_next_owner(left)
-    near = whole_call(
+    best_shape = jax.ShapeDtypeStruct((1, block_rows), jnp.float32)
+    best, right_lines = whole_call(
         near_kernel,
-        jax.ShapeDtypeStruct((24, 3 * LANES), jnp.float32),
+        (best_shape, jax.ShapeDtypeStruct((3, PART), jnp.float32)),
         "near",
         starts,
         here,
@@ -414,9 +446,10 @@
     )
     best = whole_call(
         far_kernel,
-        jax.ShapeDtypeStruct((1, block_rows), jnp.float32),
+        best_shape,
         "far",
-        near,
+        best,
+        right_lines,
         right,
         previous_left,
     )

time: 89.5 us -> 87.3 us (0.975)
  waiting for transfers between devices: 18.2 us -> 15.1 us
  starting transfers between devices: 37.4 us -> 38.3 us
    all_to_all x1, waiting for transfers between devices: 3.32 us -> 1.07 us  [by_pairs(): lax.all_to_all(packed, 'rows', split_axis=0, concat_axis=0, tiled=True, a...]
    ppermute x4, starting transfers between devices: 9.48 us -> 10.4 us  [from_holders(): return lax.ppermute(shard, ('rows', 'cent'), pairs)]
where the time goes in v4:
time: 87.3 us; the launch traced here: 86.7 us
  starting transfers between devices  38.3 us (44%)
  waiting for transfers between devices  15.1 us (17%)
  Pallas kernels  13.8 us (16%)
  blocking collectives  8.86 us (10%)
  other arithmetic  4.29 us (5%)
  local copies, waits for them, and re-layouts  2.81 us (3%)
  matrix products  2.08 us (2%)
  between operations  1.36 us (2%)
    all_to_all x1, starting transfers between devices, by_pairs(): lax.all_to_all(packed, 'rows', split_axis=0, concat_axis=0, tiled=True, a...  15.8 us
    ppermute x4, starting transfers between devices, from_holders(): return lax.ppermute(shard, ('rows', 'cent'), pairs)  10.4 us
    ppermute x3, starting transfers between devices, rotated(): lax.ppermute(shard, axis, [(i, (i + by) % peers) for i in range(peers)])  10.2 us
    all_to_all x1, blocking collectives, on_device(): lax.all_to_all(best.reshape(cent_count, 2, quarter // 2), 'cent', split_a...  8.86 us
    pallas_call x2, Pallas kernels, whole_call(): pl.pallas_call(kernel, in_specs=[pl.BlockSpec(memory_space=pltpu.VMEM)] *...  6.78 us
    ppermute x1, waiting for transfers between devices, to_next_owner(): lax.ppermute(shard, 'rows', [(row, row + 1) for row in range(row_count -...  5.18 us
    ppermute x4, waiting for transfers between devices, from_holders(): return lax.ppermute(shard, ('rows', 'cent'), pairs)  4.89 us
    pallas_call x1, Pallas kernels, pack_pairs(): pl.pallas_call(lambda *refs: pack_pairs_kernel(*refs, owner_rows=owner_ro...  3.96 us
  transfers between devices with their start and end apart: 9, of which 7 were waited for; matrix products, arithmetic and copies ran while one was open for 6% of the time, Pallas kernels for 5%

profile of v4, /device:TPU:64, one launch (start us, length us, event | category | flops | bytes accessed | tf_op | source)
XLA Modules:
  0.0 86.7 jit_solution(3136751007432811248)
XLA Ops:
  0.7 4.0 %pack_pairs_5.1 = (bf16[512,512]{1,0:T(8,128)(2,1)}, s32[1]{0:T(128)}) custom-call(s32[1]{0:T(128)} %bitcast.33.refs_0_, s32[1]{0:T(128)} %bitcast.34.refs_1_, bf16[1024,768]{1,0:T(8,128)(2,1)} %refs_2_.1, s32[1,1024]{1,0:T(1,128)} %bitcast.51), custom_call_target="tpu_custom_call" | custom-call | tf_op jit(solution)/shard_map/pack_pairs_5/pallas_call | solution.py:139
  4.6 0.3 reduce-window.9
  5.1 0.1 slice_reduce_fusion
  5.9 38.4 %conditional.1 = (bf16[272,768]{1,0:T(8,128)(2,1)}, f32[1024]{0:T(1024)S(1)}) conditional(s32[]{:T(128)} %bitcast.36, (bf16[512,512]{1,0:T(8,128)(2,1)}, bf16[1024,768]{1,0:T(8,128)(2,1)S(1)}, bf16[1024,768]{1,0:T(8,128)(2,1)}, s32[1024]{0:T(1024)S(1)}, s32[1024]{0:T(1024)S(1)}, /*index=5*/s32[1024]{0:T(1024)S(1)}) %tuple.47, ...), branch_computations={%region_2.6_spmd, %region_6.10_spmd, %region_10.14_spmd} | conditional | flops 1621629952 | bytes 19341548 | solution.py:413
  5.9 15.8 %all-to-all-start = ((bf16[64,8,512]{2,1,0:T(8,128)(2,1)}), bf16[64,8,512]{2,1,0:T(8,128)(2,1)S(1)}, u32[]{:S(2)}, u32[]{:S(2)}) async-start(bf16[64,8,512]{2,1,0:T(8,128)(2,1)} %bitcast), calls=%async_computation | async-start | bytes 1048576 | tf_op jit(solution)/shard_map/cond/branch_0_fun/all_to_all | solution.py:390
  21.7 0.4 fusion
  22.1 1.0 %copy-done.8 = bf16[1024,768]{1,0:T(8,128)(2,1)S(1)} copy-done((bf16[1024,768]{1,0:T(8,128)(2,1)S(1)}, bf16[1024,768]{1,0:T(8,128)(2,1)}, u32[]{:S(2)}) %copy-start.8) | copy-done | bytes 1572888 | tf_op jit(solution)/shard_map/cond
  23.1 2.1 %fusion.15 = (f32[1024]{0:T(1024)S(1)}, f32[1024]{0:T(1024)S(1)}) fusion(s32[1024]{0:T(1024)S(1)} %get-tuple-element.43, s32[1024]{0:T(1024)S(1)} %get-tuple-element.42, s32[1024]{0:T(1024)S(1)} %get-tuple-element.41, bf16[1024,768]{1,0:T(8,128)(2,1)S(1)} %copy-done.8, bf16[1024,768]{1,0:T(8,128)(2,1)S(1)} %get-tuple-element.39, f32[1024]{0:T(1024)S(1)} %add_rsqrt_fusion), kind=kOutput, calls=%fused_computation.35 | convolution fusion | flops 1619261440 | bytes 3170304 | tf_op jit(solution)/shard_map/cond/branch_0_fun/dot_general | solution.py:346
  25.2 4.7 %collective-permute-start.2 = (f32[2,1024]{1,0:T(2,128)S(1)}, f32[2,1024]{1,0:T(2,128)S(1)}, u32[]{:S(2)}, u32[]{:S(2)}) collective-permute-start(f32[2,1024]{1,0:T(2,128)S(1)} %pad_maximum_fusion), channel_id=1, source_target_pairs={{0,3},{1,0},{2,1},{3,2},{4,7},{5,4},{6,5},{7,6},{8,11},{9,8},{10,9... | collective-permute-start | bytes 24584 | tf_op jit(solution)/shard_map/cond/branch_0_fun/ppermute | solution.py:23
  29.9 2.7 %collective-permute-start.1 = (f32[2,1024]{1,0:T(2,128)S(1)}, f32[2,1024]{1,0:T(2,128)S(1)}, u32[]{:S(2)}, u32[]{:S(2)}) collective-permute-start(f32[2,1024]{1,0:T(2,128)S(1)} %pad_maximum_fusion), channel_id=1, source_target_pairs={{0,2},{1,3},{2,0},{3,1},{4,6},{5,7},{6,4},{7,5},{8,10},{9,11},{10,... | collective-permute-start | bytes 24584 | tf_op jit(solution)/shard_map/cond/branch_0_fun/ppermute | solution.py:23
  32.6 2.8 %collective-permute-start = (f32[2,1024]{1,0:T(2,128)S(1)}, f32[2,1024]{1,0:T(2,128)S(1)}, u32[]{:S(2)}, u32[]{:S(2)}) collective-permute-start(f32[2,1024]{1,0:T(2,128)S(1)} %pad_maximum_fusion), channel_id=1, source_target_pairs={{0,1},{1,2},{2,3},{3,0},{4,5},{5,6},{6,7},{7,4},{8,9},{9,10},{10,1... | collective-permute-start | bytes 24584 | tf_op jit(solution)/shard_map/cond/branch_0_fun/ppermute | solution.py:23
  35.4 1.5 %collective-permute-done.1 = f32[2,1024]{1,0:T(2,128)S(1)} collective-permute-done((f32[2,1024]{1,0:T(2,128)S(1)}, f32[2,1024]{1,0:T(2,128)S(1)}, u32[]{:S(2)}, u32[]{:S(2)}) %collective-permute-start.1) | collective-permute-done | bytes 8224 | tf_op jit(solution)/shard_map/cond/branch_0_fun/ppermute | solution.py:23
  37.0 2.4 %collective-permute-done = f32[2,1024]{1,0:T(2,128)S(1)} collective-permute-done((f32[2,1024]{1,0:T(2,128)S(1)}, f32[2,1024]{1,0:T(2,128)S(1)}, u32[]{:S(2)}, u32[]{:S(2)}) %collective-permute-start) | collective-permute-done | bytes 8224 | tf_op jit(solution)/shard_map/cond/branch_0_fun/ppermute | solution.py:23
  39.4 1.1 %all-to-all-done = bf16[64,8,512]{2,1,0:T(8,128)(2,1)S(1)} async-done(((bf16[64,8,512]{2,1,0:T(8,128)(2,1)}), bf16[64,8,512]{2,1,0:T(8,128)(2,1)S(1)}, u32[]{:S(2)}, u32[]{:S(2)}) %all-to-all-start) | async-done | bytes 524320 | tf_op jit(solution)/shard_map/cond/branch_0_fun/all_to_all | solution.py:390
  40.4 0.8 copy-done.2
  41.2 3.0 %compact_pairs_5.1 = bf16[272,768]{1,0:T(8,128)(2,1)} custom-call(bf16[512,512]{1,0:T(8,128)(2,1)} %bitcast.48), custom_call_target="tpu_custom_call" | custom-call | tf_op jit(solution)/shard_map/cond/branch_0_fun/compact_pairs_5/pallas_call | solution.py:245
  44.3 3.4 %collective-permute-start.13 = (bf16[272,768]{1,0:T(8,128)(2,1)}, bf16[272,768]{1,0:T(8,128)(2,1)S(1)}, u32[]{:S(2)}, u32[]{:S(2)}) collective-permute-start(bf16[272,768]{1,0:T(8,128)(2,1)} %get-tuple-element.80), channel_id=1, source_target_pairs={{0,1},{1,2},{2,7},{3,4},{4,5},{5,6},{6,3},{7,0},{8,9},{9,10},{10,1... | collective-permute-start | bytes 1253384 | tf_op jit(solution)/shard_map/ppermute | solution.py:40
  47.7 3.2 %collective-permute-start.12 = (bf16[272,768]{1,0:T(8,128)(2,1)}, bf16[272,768]{1,0:T(8,128)(2,1)S(1)}, u32[]{:S(2)}, u32[]{:S(2)}) collective-permute-start(bf16[272,768]{1,0:T(8,128)(2,1)} %get-tuple-element.80), channel_id=1, source_target_pairs={{0,3},{1,0},{2,5},{3,6},{4,7},{5,4},{6,1},{7,2},{8,11},{9,8},{10,1... | collective-permute-start | bytes 1253384 | tf_op jit(solution)/shard_map/ppermute | solution.py:40
  50.9 2.2 %collective-permute-start.11 = (bf16[272,768]{1,0:T(8,128)(2,1)}, bf16[272,768]{1,0:T(8,128)(2,1)S(1)}, u32[]{:S(2)}, u32[]{:S(2)}) collective-permute-start(bf16[272,768]{1,0:T(8,128)(2,1)} %get-tuple-element.80), channel_id=1, source_target_pairs={{0,4},{1,5},{2,10},{3,11},{4,8},{5,9},{6,6},{7,7},{8,12},{9,13},{1... | collective-permute-start | bytes 1253384 | tf_op jit(solution)/shard_map/ppermute | solution.py:40
  53.1 1.7 %collective-permute-start.10 = (bf16[272,768]{1,0:T(8,128)(2,1)}, bf16[272,768]{1,0:T(8,128)(2,1)S(1)}, u32[]{:S(2)}, u32[]{:S(2)}) collective-permute-start(bf16[272,768]{1,0:T(8,128)(2,1)} %get-tuple-element.80), channel_id=1, source_target_pairs={{0,0},{1,1},{2,6},{3,7},{4,4},{5,5},{6,2},{7,3},{8,8},{9,9},{10,14... | collective-permute-start | bytes 1253384 | tf_op jit(solution)/shard_map/ppermute | solution.py:40
  54.8 2.3 %select_reduce_fusion.3 = s32[1024]{0:T(1024)S(1)} fusion(s32[4096]{0:T(1024)S(1)} %get-tuple-element.94, s32[1024]{0:T(1024)S(1)} %iota_add_fusion), kind=kLoop, calls=%fused_computation.30 | loop fusion | flops 12581888 | bytes 24576 | tf_op jit(solution)/shard_map/reduce_max | solution.py:426
  57.1 0.6 broadcast_subtract_fusion
  57.7 1.8 %collective-permute-done.13.left_ref = bf16[272,768]{1,0:T(8,128)(2,1)S(1)} collective-permute-done((bf16[272,768]{1,0:T(8,128)(2,1)}, bf16[272,768]{1,0:T(8,128)(2,1)S(1)}, u32[]{:S(2)}, u32[]{:S(2)}) %collective-permute-start.13) | collective-permute-done | bytes 417824 | tf_op jit(solution)/shard_map/ppermute | solution.py:40
  59.4 1.4 %collective-permute-done.12.right_ref = bf16[272,768]{1,0:T(8,128)(2,1)S(1)} collective-permute-done((bf16[272,768]{1,0:T(8,128)(2,1)}, bf16[272,768]{1,0:T(8,128)(2,1)S(1)}, u32[]{:S(2)}, u32[]{:S(2)}) %collective-permute-start.12) | collective-permute-done | bytes 417824 | tf_op jit(solution)/shard_map/ppermute | solution.py:40
  60.8 1.7 %collective-permute-done.11.previous_ref = bf16[272,768]{1,0:T(8,128)(2,1)S(1)} collective-permute-done((bf16[272,768]{1,0:T(8,128)(2,1)}, bf16[272,768]{1,0:T(8,128)(2,1)S(1)}, u32[]{:S(2)}, u32[]{:S(2)}) %collective-permute-start.11) | collective-permute-done | bytes 417824 | tf_op jit(solution)/shard_map/ppermute | solution.py:40
  62.6 1.9 %collective-permute-start.14 = (bf16[272,768]{1,0:T(8,128)(2,1)S(1)}, bf16[272,768]{1,0:T(8,128)(2,1)S(1)}, u32[]{:S(2)}, u32[]{:S(2)}) collective-permute-start(bf16[272,768]{1,0:T(8,128)(2,1)S(1)} %collective-permute-done.13.left_ref), channel_id=1, source_target_pairs={{0,4},{4,8},{8,12},{12,16},{16,20},{20,24},{24,28},{28,32},{32,36}... | collective-permute-start | bytes 1253384 | tf_op jit(solution)/shard_map/ppermute | solution.py:28
  64.5 4.3 %near.1 = (f32[1,1024]{1,0:T(1,128)}, f32[3,272]{1,0:T(4,128)}) custom-call(s32[1,1024]{1,0:T(1,128)} %bitcast.79, bf16[272,768]{1,0:T(8,128)(2,1)} %copy-done.13, bf16[272,768]{1,0:T(8,128)(2,1)} %copy-done.11, bf16[272,768]{1,0:T(8,128)(2,1)} %copy-done.3, bf16[272,768]{1,0:T(8,128)(2,1)} %copy-done.12), custom_call_target="tpu_custom_call" | custom-call | flops 455114752 | bytes 6692864 | tf_op jit(solution)/shard_map/near/pallas_call | solution.py:334
  68.8 5.2 %collective-permute-done.14.previous_left_ref = bf16[272,768]{1,0:T(8,128)(2,1)S(1)} collective-permute-done((bf16[272,768]{1,0:T(8,128)(2,1)S(1)}, bf16[272,768]{1,0:T(8,128)(2,1)S(1)}, u32[]{:S(2)}, u32[]{:S(2)}) %collective-permute-start.14) | collective-permute-done | bytes 417824 | tf_op jit(solution)/shard_map/ppermute | solution.py:28
  74.0 0.8 copy-done.4
  74.8 2.5 %far.1 = f32[1,1024]{1,0:T(1,128)} custom-call(f32[1,1024]{1,0:T(1,128)} %get-tuple-element.86.best_ref, f32[3,272]{1,0:T(4,128)} %get-tuple-element.87.right_lines_ref, bf16[272,768]{1,0:T(8,128)(2,1)} %copy-done.3, bf16[272,768]{1,0:T(8,128)(2,1)} %copy-done.4), custom_call_target="tpu_custom_call" | custom-call | flops 228279808 | bytes 3357056 | tf_op jit(solution)/shard_map/far/pallas_call | solution.py:334
  77.2 8.9 %all_to_all.25 = f32[4,2,128]{2,1,0:T(2,128)S(1)} all-to-all(f32[4,2,128]{2,1,0:T(2,128)} %bitcast.54), channel_id=1, replica_groups=mesh['rows'=128,'cent'=4] {'cent'}, dimensions={0} | all-to-all | bytes 8192 | tf_op jit(solution)/shard_map/all_to_all | solution.py:456
  86.1 0.6 reduce_max.46
  (33 shorter events, 0.3 us)
Async XLA Ops:
  0.6 5.2 %copy-start = (bf16[1024,768]{1,0:T(8,128)(2,1)S(1)}, bf16[1024,768]{1,0:T(8,128)(2,1)}, u32[]{:S(2)}) copy-start(bf16[1024,768]{1,0:T(8,128)(2,1)} %refs_2_.1) | copy-start | bytes 4718596
  0.6 5.2 %copy-start.6 = (s32[1024]{0:T(1024)S(1)}, s32[1024]{0:T(1024)}, u32[]{:S(2)}) copy-start(s32[1024]{0:T(1024)} %param.9) | copy-start | bytes 12292
  0.7 4.0 %copy-start.5 = (s32[4096]{0:T(1024)S(1)}, s32[4096]{0:T(1024)}, u32[]{:S(2)}) copy-start(s32[4096]{0:T(1024)} %param.10) | copy-start | bytes 49156
  5.9 34.6 %all-to-all-start = ((bf16[64,8,512]{2,1,0:T(8,128)(2,1)}), bf16[64,8,512]{2,1,0:T(8,128)(2,1)S(1)}, u32[]{:S(2)}, u32[]{:S(2)}) async-start(bf16[64,8,512]{2,1,0:T(8,128)(2,1)} %bitcast), calls=%async_computation | async-start | bytes 1048576 | tf_op jit(solution)/shard_map/cond/branch_0_fun/all_to_all | solution.py:390
  21.7 1.4 %copy-start.8 = (bf16[1024,768]{1,0:T(8,128)(2,1)S(1)}, bf16[1024,768]{1,0:T(8,128)(2,1)}, u32[]{:S(2)}) copy-start(bf16[1024,768]{1,0:T(8,128)(2,1)} %get-tuple-element.40) | copy-start | bytes 4718596 | tf_op jit(solution)/shard_map/cond
  25.2 10.2 %collective-permute-start.2 = (f32[2,1024]{1,0:T(2,128)S(1)}, f32[2,1024]{1,0:T(2,128)S(1)}, u32[]{:S(2)}, u32[]{:S(2)}) collective-permute-start(f32[2,1024]{1,0:T(2,128)S(1)} %pad_maximum_fusion), channel_id=1, source_target_pairs={{0,3},{1,0},{2,1},{3,2},{4,7},{5,4},{6,5},{7,6},{8,11},{9,8},{10,9... | collective-permute-start | bytes 24584 | tf_op jit(solution)/shard_map/cond/branch_0_fun/ppermute | solution.py:23
  29.9 7.1 %collective-permute-start.1 = (f32[2,1024]{1,0:T(2,128)S(1)}, f32[2,1024]{1,0:T(2,128)S(1)}, u32[]{:S(2)}, u32[]{:S(2)}) collective-permute-start(f32[2,1024]{1,0:T(2,128)S(1)} %pad_maximum_fusion), channel_id=1, source_target_pairs={{0,2},{1,3},{2,0},{3,1},{4,6},{5,7},{6,4},{7,5},{8,10},{9,11},{10,... | collective-permute-start | bytes 24584 | tf_op jit(solution)/shard_map/cond/branch_0_fun/ppermute | solution.py:23
  32.6 6.8 %collective-permute-start = (f32[2,1024]{1,0:T(2,128)S(1)}, f32[2,1024]{1,0:T(2,128)S(1)}, u32[]{:S(2)}, u32[]{:S(2)}) collective-permute-start(f32[2,1024]{1,0:T(2,128)S(1)} %pad_maximum_fusion), channel_id=1, source_target_pairs={{0,1},{1,2},{2,3},{3,0},{4,5},{5,6},{6,7},{7,4},{8,9},{9,10},{10,1... | collective-permute-start | bytes 24584 | tf_op jit(solution)/shard_map/cond/branch_0_fun/ppermute | solution.py:23
  40.4 0.8 copy-start.2
  44.3 42.4 %copy-start.7 = (f32[1024]{0:T(1024)}, f32[1024]{0:T(1024)S(1)}, u32[]{:S(2)}) copy-start(f32[1024]{0:T(1024)S(1)} %get-tuple-element.72) | copy-start | bytes 12292
  44.3 15.1 %collective-permute-start.13 = (bf16[272,768]{1,0:T(8,128)(2,1)}, bf16[272,768]{1,0:T(8,128)(2,1)S(1)}, u32[]{:S(2)}, u32[]{:S(2)}) collective-permute-start(bf16[272,768]{1,0:T(8,128)(2,1)} %get-tuple-element.80), channel_id=1, source_target_pairs={{0,1},{1,2},{2,7},{3,4},{4,5},{5,6},{6,3},{7,0},{8,9},{9,10},{10,1... | collective-permute-start | bytes 1253384 | tf_op jit(solution)/shard_map/ppermute | solution.py:40
  47.7 13.1 %collective-permute-start.12 = (bf16[272,768]{1,0:T(8,128)(2,1)}, bf16[272,768]{1,0:T(8,128)(2,1)S(1)}, u32[]{:S(2)}, u32[]{:S(2)}) collective-permute-start(bf16[272,768]{1,0:T(8,128)(2,1)} %get-tuple-element.80), channel_id=1, source_target_pairs={{0,3},{1,0},{2,5},{3,6},{4,7},{5,4},{6,1},{7,2},{8,11},{9,8},{10,1... | collective-permute-start | bytes 1253384 | tf_op jit(solution)/shard_map/ppermute | solution.py:40
  50.9 11.7 %collective-permute-start.11 = (bf16[272,768]{1,0:T(8,128)(2,1)}, bf16[272,768]{1,0:T(8,128)(2,1)S(1)}, u32[]{:S(2)}, u32[]{:S(2)}) collective-permute-start(bf16[272,768]{1,0:T(8,128)(2,1)} %get-tuple-element.80), channel_id=1, source_target_pairs={{0,4},{1,5},{2,10},{3,11},{4,8},{5,9},{6,6},{7,7},{8,12},{9,13},{1... | collective-permute-start | bytes 1253384 | tf_op jit(solution)/shard_map/ppermute | solution.py:40
  53.1 9.5 %collective-permute-start.10 = (bf16[272,768]{1,0:T(8,128)(2,1)}, bf16[272,768]{1,0:T(8,128)(2,1)S(1)}, u32[]{:S(2)}, u32[]{:S(2)}) collective-permute-start(bf16[272,768]{1,0:T(8,128)(2,1)} %get-tuple-element.80), channel_id=1, source_target_pairs={{0,0},{1,1},{2,6},{3,7},{4,4},{5,5},{6,2},{7,3},{8,8},{9,9},{10,14... | collective-permute-start | bytes 1253384 | tf_op jit(solution)/shard_map/ppermute | solution.py:40
  59.4 5.1 %copy-start.11 = (bf16[272,768]{1,0:T(8,128)(2,1)}, bf16[272,768]{1,0:T(8,128)(2,1)S(1)}, u32[]{:S(2)}) copy-start(bf16[272,768]{1,0:T(8,128)(2,1)S(1)} %collective-permute-done.13.left_ref) | copy-start | bytes 1253380
  60.8 3.7 %copy-start.3 = (bf16[272,768]{1,0:T(8,128)(2,1)}, bf16[272,768]{1,0:T(8,128)(2,1)S(1)}, u32[]{:S(2)}) copy-start(bf16[272,768]{1,0:T(8,128)(2,1)S(1)} %collective-permute-done.12.right_ref) | copy-start | bytes 1253380
  62.6 2.0 %copy-start.12 = (bf16[272,768]{1,0:T(8,128)(2,1)}, bf16[272,768]{1,0:T(8,128)(2,1)S(1)}, u32[]{:S(2)}) copy-start(bf16[272,768]{1,0:T(8,128)(2,1)S(1)} %collective-permute-done.11.previous_ref) | copy-start | bytes 1253380
  62.6 2.0 %copy-start.13 = (bf16[272,768]{1,0:T(8,128)(2,1)}, bf16[272,768]{1,0:T(8,128)(2,1)S(1)}, u32[]{:S(2)}) copy-start(bf16[272,768]{1,0:T(8,128)(2,1)S(1)} %collective-permute-done.10.here_ref) | copy-start | bytes 1253380
  62.6 11.5 %collective-permute-start.14 = (bf16[272,768]{1,0:T(8,128)(2,1)S(1)}, bf16[272,768]{1,0:T(8,128)(2,1)S(1)}, u32[]{:S(2)}, u32[]{:S(2)}) collective-permute-start(bf16[272,768]{1,0:T(8,128)(2,1)S(1)} %collective-permute-done.13.left_ref), channel_id=1, source_target_pairs={{0,4},{4,8},{8,12},{12,16},{16,20},{20,24},{24,28},{28,32},{32,36}... | collective-permute-start | bytes 1253384 | tf_op jit(solution)/shard_map/ppermute | solution.py:28
  74.0 0.8 copy-start.4

commit v5 on v4

--- a/solution.py
+++ b/solution.py
@@ -149,7 +149,7 @@
             pl.BlockSpec(memory_space=pltpu.SMEM),
         ),
         out_shape=(
-            jax.ShapeDtypeStruct((chips * PAIR_ROWS, PAIR_TILES[pair_slots] * LANES), jnp.bfloat16),
+            pltpu.VMEM((chips * PAIR_ROWS, PAIR_TILES[pair_slots] * LANES), jnp.bfloat16),
             jax.ShapeDtypeStruct((1,), jnp.int32),
         ),
         name=f"pack_pairs_{pair_slots}",
@@ -195,7 +195,8 @@
         moved = pltpu.roll(tags, slots - (tag_row - slot), 0)
         moved = pltpu.roll(moved, (LANES - 2 * slot) % LANES, 1) if slot else moved
         placed = jnp.where((line == slot) & (lane < 2), moved, placed)
-    store_part(out_ref, placed, [got_ref[...]] + [tile.astype(jnp.bfloat16) for tile in rest])
+    rest = jnp.concatenate(rest, axis=1).astype(jnp.bfloat16)
+    store_part(out_ref, placed, [got_ref[...], rest])
 
 
 def pack_kernel(cent_ref, rows_ref, places_ref, out_ref, *, owner_rows):
@@ -241,10 +242,17 @@
     store_part(out_ref, tags, [got_ref[:, :features]])
 
 
+def on_chip(array):
+    return pltpu.with_memory_space_constraint(array, pltpu.VMEM)
+
+
 def compacted(kernel, got, features, name):
     return pl.pallas_call(
-        kernel, out_shape=jax.ShapeDtypeStruct((PART, features), jnp.bfloat16), name=name
-    )(got)
+        kernel,
+        in_specs=[pl.BlockSpec(memory_space=pltpu.VMEM)],
+        out_shape=pltpu.VMEM((PART, features), jnp.bfloat16),
+        name=name,
+    )(on_chip(got))
 
 
 def decoded(high, low):
@@ -339,7 +347,7 @@
             flops=2 * size * PART, transcendentals=0, bytes_accessed=8 * size
         ),
         name=name,
-    )(*arrays)
+    )(*[on_chip(array) for array in arrays])
 
 
 def margin_of(embeddings, centroids, positions, slab_starts, slab_ends):
@@ -433,10 +441,10 @@
         (here, previous_here, right, left, starts)
     )
     previous_left = to_next_owner(left)
-    best_shape = jax.ShapeDtypeStruct((1, block_rows), jnp.float32)
+    best_shape = pltpu.VMEM((1, block_rows), jnp.float32)
     best, right_lines = whole_call(
         near_kernel,
-        (best_shape, jax.ShapeDtypeStruct((3, PART), jnp.float32)),
+        (best_shape, pltpu.VMEM((3, PART), jnp.float32)),
         "near",
         starts,
         here,

time: 87.3 us -> 82.7 us (0.947)
  Pallas kernels: 13.8 us -> 9.05 us
  waiting for transfers between devices: 15.1 us -> 17.6 us
  local copies, waits for them, and re-layouts: 2.81 us -> 1.24 us
    pallas_call x2, Pallas kernels: 6.78 us -> 3.12 us  [whole_call(): pl.pallas_call(kernel, in_specs=[pl.BlockSpec(memory_space=pltpu.VMEM)] *...]
    ppermute x1, waiting for transfers between devices: 5.18 us -> 7.13 us  [to_next_owner(): lax.ppermute(shard, 'rows', [(row, row + 1) for row in range(row_count -...]
    pallas_call x1, Pallas kernels: 3.04 us -> 1.96 us  [compacted(): pl.pallas_call(kernel, in_specs=[pl.BlockSpec(memory_space=pltpu.VMEM)],...]
    cond x4 -> x2, local copies, waits for them, and re-layouts: 1.81 us -> 1.01 us
  transfers between devices with their start and end apart: 9 -> 9, of which waited for: 7 -> 7; matrix products, arithmetic and copies ran while one was open for 6% -> 6% of each run, Pallas kernels for 5% -> 3%
where the time goes in v5:
time: 82.7 us; the launch traced here: 82.2 us
  starting transfers between devices  38.3 us (46%)
  waiting for transfers between devices  17.6 us (21%)
  Pallas kernels  9.05 us (11%)
  blocking collectives  8.67 us (10%)
  other arithmetic  3.71 us (4%)
  matrix products  2.08 us (3%)
  between operations  1.47 us (2%)
  local copies, waits for them, and re-layouts  1.24 us (1%)
    all_to_all x1, starting transfers between devices, by_pairs(): lax.all_to_all(packed, 'rows', split_axis=0, concat_axis=0, tiled=True, a...  15.8 us
    ppermute x4, starting transfers between devices, from_holders(): return lax.ppermute(shard, ('rows', 'cent'), pairs)  10.4 us
    ppermute x3, starting transfers between devices, rotated(): lax.ppermute(shard, axis, [(i, (i + by) % peers) for i in range(peers)])  10.2 us
    all_to_all x1, blocking collectives, on_device(): lax.all_to_all(best.reshape(cent_count, 2, quarter // 2), 'cent', split_a...  8.67 us
    ppermute x1, waiting for transfers between devices, to_next_owner(): lax.ppermute(shard, 'rows', [(row, row + 1) for row in range(row_count -...  7.13 us
    ppermute x4, waiting for transfers between devices, from_holders(): return lax.ppermute(shard, ('rows', 'cent'), pairs)  5.47 us
    pallas_call x1, Pallas kernels, pack_pairs(): pl.pallas_call(lambda *refs: pack_pairs_kernel(*refs, owner_rows=owner_ro...  3.97 us
    ppermute x3, waiting for transfers between devices, rotated(): lax.ppermute(shard, axis, [(i, (i + by) % peers) for i in range(peers)])  3.92 us
  transfers between devices with their start and end apart: 9, of which 7 were waited for; matrix products, arithmetic and copies ran while one was open for 6% of the time, Pallas kernels for 3%

profile of v5, /device:TPU:64, one launch (start us, length us, event | category | flops | bytes accessed | tf_op | source)
XLA Modules:
  0.0 82.2 jit_solution(15648783990608348165)
XLA Ops:
  0.7 4.0 %pack_pairs_5.1 = (bf16[512,512]{1,0:T(8,128)(2,1)}, s32[1]{0:T(128)}) custom-call(s32[1]{0:T(128)} %bitcast.33.refs_0_, s32[1]{0:T(128)} %bitcast.34.refs_1_, bf16[1024,768]{1,0:T(8,128)(2,1)} %refs_2_.1, s32[1,1024]{1,0:T(1,128)} %bitcast.52), custom_call_target="tpu_custom_call" | custom-call | tf_op jit(solution)/shard_map/pack_pairs_5/pallas_call | solution.py:139
  4.7 0.3 reduce-window.9
  4.9 0.1 slice.81
  5.0 0.1 reduce-window.12
  5.1 0.1 slice_reduce_fusion
  5.2 0.1 fusion.18
  6.0 36.5 %conditional.1 = (bf16[272,768]{1,0:T(8,128)(2,1)}, f32[1024]{0:T(1024)S(1)}) conditional(s32[]{:T(128)} %bitcast.36, (bf16[512,512]{1,0:T(8,128)(2,1)}, bf16[1024,768]{1,0:T(8,128)(2,1)S(1)}, bf16[1024,768]{1,0:T(8,128)(2,1)}, s32[1024]{0:T(1024)S(1)}, s32[1024]{0:T(1024)S(1)}, /*index=5*/s32[1024]{0:T(1024)S(1)}) %tuple.47, ...), branch_computations={%region_2.6_spmd, %region_6.10_spmd, %region_10.14_spmd} | conditional | flops 1621629952 | bytes 19341548 | solution.py:421
  6.0 15.8 %all-to-all-start = ((bf16[64,8,512]{2,1,0:T(8,128)(2,1)}), bf16[64,8,512]{2,1,0:T(8,128)(2,1)S(1)}, u32[]{:S(2)}, u32[]{:S(2)}) async-start(bf16[64,8,512]{2,1,0:T(8,128)(2,1)} %bitcast), calls=%async_computation | async-start | bytes 1048576 | tf_op jit(solution)/shard_map/cond/branch_0_fun/all_to_all | solution.py:398
  21.8 0.4 fusion
  22.2 1.0 %copy-done.4 = bf16[1024,768]{1,0:T(8,128)(2,1)S(1)} copy-done((bf16[1024,768]{1,0:T(8,128)(2,1)S(1)}, bf16[1024,768]{1,0:T(8,128)(2,1)}, u32[]{:S(2)}) %copy-start.4) | copy-done | bytes 1572888 | tf_op jit(solution)/shard_map/cond
  23.2 2.1 %fusion.15 = (f32[1024]{0:T(1024)S(1)}, f32[1024]{0:T(1024)S(1)}) fusion(s32[1024]{0:T(1024)S(1)} %get-tuple-element.43, s32[1024]{0:T(1024)S(1)} %get-tuple-element.42, s32[1024]{0:T(1024)S(1)} %get-tuple-element.41, bf16[1024,768]{1,0:T(8,128)(2,1)S(1)} %copy-done.4, bf16[1024,768]{1,0:T(8,128)(2,1)S(1)} %get-tuple-element.39, f32[1024]{0:T(1024)S(1)} %add_rsqrt_fusion), kind=kOutput, calls=%fused_computation.35 | convolution fusion | flops 1619261440 | bytes 3170304 | tf_op jit(solution)/shard_map/cond/branch_0_fun/dot_general | solution.py:354
  25.3 4.7 %collective-permute-start.2 = (f32[2,1024]{1,0:T(2,128)S(1)}, f32[2,1024]{1,0:T(2,128)S(1)}, u32[]{:S(2)}, u32[]{:S(2)}) collective-permute-start(f32[2,1024]{1,0:T(2,128)S(1)} %pad_maximum_fusion), channel_id=1, source_target_pairs={{0,3},{1,0},{2,1},{3,2},{4,7},{5,4},{6,5},{7,6},{8,11},{9,8},{10,9... | collective-permute-start | bytes 24584 | tf_op jit(solution)/shard_map/cond/branch_0_fun/ppermute | solution.py:23
  30.0 2.7 %collective-permute-start.1 = (f32[2,1024]{1,0:T(2,128)S(1)}, f32[2,1024]{1,0:T(2,128)S(1)}, u32[]{:S(2)}, u32[]{:S(2)}) collective-permute-start(f32[2,1024]{1,0:T(2,128)S(1)} %pad_maximum_fusion), channel_id=1, source_target_pairs={{0,2},{1,3},{2,0},{3,1},{4,6},{5,7},{6,4},{7,5},{8,10},{9,11},{10,... | collective-permute-start | bytes 24584 | tf_op jit(solution)/shard_map/cond/branch_0_fun/ppermute | solution.py:23
  32.7 2.8 %collective-permute-start = (f32[2,1024]{1,0:T(2,128)S(1)}, f32[2,1024]{1,0:T(2,128)S(1)}, u32[]{:S(2)}, u32[]{:S(2)}) collective-permute-start(f32[2,1024]{1,0:T(2,128)S(1)} %pad_maximum_fusion), channel_id=1, source_target_pairs={{0,1},{1,2},{2,3},{3,0},{4,5},{5,6},{6,7},{7,4},{8,9},{9,10},{10,1... | collective-permute-start | bytes 24584 | tf_op jit(solution)/shard_map/cond/branch_0_fun/ppermute | solution.py:23
  35.6 1.5 %collective-permute-done.1 = f32[2,1024]{1,0:T(2,128)S(1)} collective-permute-done((f32[2,1024]{1,0:T(2,128)S(1)}, f32[2,1024]{1,0:T(2,128)S(1)}, u32[]{:S(2)}, u32[]{:S(2)}) %collective-permute-start.1) | collective-permute-done | bytes 8224 | tf_op jit(solution)/shard_map/cond/branch_0_fun/ppermute | solution.py:23
  37.1 2.4 %collective-permute-done = f32[2,1024]{1,0:T(2,128)S(1)} collective-permute-done((f32[2,1024]{1,0:T(2,128)S(1)}, f32[2,1024]{1,0:T(2,128)S(1)}, u32[]{:S(2)}, u32[]{:S(2)}) %collective-permute-start) | collective-permute-done | bytes 8224 | tf_op jit(solution)/shard_map/cond/branch_0_fun/ppermute | solution.py:23
  39.5 1.1 %all-to-all-done = bf16[64,8,512]{2,1,0:T(8,128)(2,1)S(1)} async-done(((bf16[64,8,512]{2,1,0:T(8,128)(2,1)}), bf16[64,8,512]{2,1,0:T(8,128)(2,1)S(1)}, u32[]{:S(2)}, u32[]{:S(2)}) %all-to-all-start) | async-done | bytes 524320 | tf_op jit(solution)/shard_map/cond/branch_0_fun/all_to_all | solution.py:398
  40.6 2.0 %compact_pairs_5.1 = bf16[272,768]{1,0:T(8,128)(2,1)} custom-call(bf16[512,512]{1,0:T(8,128)(2,1)S(1)} %bitcast.48), custom_call_target="tpu_custom_call" | custom-call | tf_op jit(solution)/shard_map/cond/branch_0_fun/compact_pairs_5/pallas_call | solution.py:250
  42.5 3.4 %collective-permute-start.13 = (bf16[272,768]{1,0:T(8,128)(2,1)}, bf16[272,768]{1,0:T(8,128)(2,1)S(1)}, u32[]{:S(2)}, u32[]{:S(2)}) collective-permute-start(bf16[272,768]{1,0:T(8,128)(2,1)} %get-tuple-element.80), channel_id=1, source_target_pairs={{0,1},{1,2},{2,7},{3,4},{4,5},{5,6},{6,3},{7,0},{8,9},{9,10},{10,1... | collective-permute-start | bytes 1253384 | tf_op jit(solution)/shard_map/ppermute | solution.py:40
  45.9 3.2 %collective-permute-start.12 = (bf16[272,768]{1,0:T(8,128)(2,1)}, bf16[272,768]{1,0:T(8,128)(2,1)S(1)}, u32[]{:S(2)}, u32[]{:S(2)}) collective-permute-start(bf16[272,768]{1,0:T(8,128)(2,1)} %get-tuple-element.80), channel_id=1, source_target_pairs={{0,3},{1,0},{2,5},{3,6},{4,7},{5,4},{6,1},{7,2},{8,11},{9,8},{10,1... | collective-permute-start | bytes 1253384 | tf_op jit(solution)/shard_map/ppermute | solution.py:40
  49.1 2.2 %collective-permute-start.11 = (bf16[272,768]{1,0:T(8,128)(2,1)}, bf16[272,768]{1,0:T(8,128)(2,1)S(1)}, u32[]{:S(2)}, u32[]{:S(2)}) collective-permute-start(bf16[272,768]{1,0:T(8,128)(2,1)} %get-tuple-element.80), channel_id=1, source_target_pairs={{0,4},{1,5},{2,10},{3,11},{4,8},{5,9},{6,6},{7,7},{8,12},{9,13},{1... | collective-permute-start | bytes 1253384 | tf_op jit(solution)/shard_map/ppermute | solution.py:40
  51.4 1.7 %collective-permute-start.10 = (bf16[272,768]{1,0:T(8,128)(2,1)}, bf16[272,768]{1,0:T(8,128)(2,1)S(1)}, u32[]{:S(2)}, u32[]{:S(2)}) collective-permute-start(bf16[272,768]{1,0:T(8,128)(2,1)} %get-tuple-element.80), channel_id=1, source_target_pairs={{0,0},{1,1},{2,6},{3,7},{4,4},{5,5},{6,2},{7,3},{8,8},{9,9},{10,14... | collective-permute-start | bytes 1253384 | tf_op jit(solution)/shard_map/ppermute | solution.py:40
  53.0 2.3 %select_reduce_fusion.3 = s32[1024]{0:T(1024)S(1)} fusion(s32[4096]{0:T(1024)S(1)} %get-tuple-element.94, s32[1024]{0:T(1024)S(1)} %iota_add_fusion), kind=kLoop, calls=%fused_computation.30 | loop fusion | flops 12581888 | bytes 24576 | tf_op jit(solution)/shard_map/reduce_max | solution.py:434
  55.3 2.3 %collective-permute-done.13.left_ref = bf16[272,768]{1,0:T(8,128)(2,1)S(1)} collective-permute-done((bf16[272,768]{1,0:T(8,128)(2,1)}, bf16[272,768]{1,0:T(8,128)(2,1)S(1)}, u32[]{:S(2)}, u32[]{:S(2)}) %collective-permute-start.13) | collective-permute-done | bytes 417824 | tf_op jit(solution)/shard_map/ppermute | solution.py:40
  57.7 1.4 %collective-permute-done.12.right_ref = bf16[272,768]{1,0:T(8,128)(2,1)S(1)} collective-permute-done((bf16[272,768]{1,0:T(8,128)(2,1)}, bf16[272,768]{1,0:T(8,128)(2,1)S(1)}, u32[]{:S(2)}, u32[]{:S(2)}) %collective-permute-start.12) | collective-permute-done | bytes 417824 | tf_op jit(solution)/shard_map/ppermute | solution.py:40
  59.1 1.7 %collective-permute-done.11.previous_ref = bf16[272,768]{1,0:T(8,128)(2,1)S(1)} collective-permute-done((bf16[272,768]{1,0:T(8,128)(2,1)}, bf16[272,768]{1,0:T(8,128)(2,1)S(1)}, u32[]{:S(2)}, u32[]{:S(2)}) %collective-permute-start.11) | collective-permute-done | bytes 417824 | tf_op jit(solution)/shard_map/ppermute | solution.py:40
  60.8 1.9 %collective-permute-start.14 = (bf16[272,768]{1,0:T(8,128)(2,1)S(1)}, bf16[272,768]{1,0:T(8,128)(2,1)S(1)}, u32[]{:S(2)}, u32[]{:S(2)}) collective-permute-start(bf16[272,768]{1,0:T(8,128)(2,1)S(1)} %collective-permute-done.13.left_ref), channel_id=1, source_target_pairs={{0,4},{4,8},{8,12},{12,16},{16,20},{20,24},{24,28},{28,32},{32,36}... | collective-permute-start | bytes 1253384 | tf_op jit(solution)/shard_map/ppermute | solution.py:28
  62.7 2.4 %near.1 = (f32[1,1024]{1,0:T(1,128)S(1)}, f32[3,272]{1,0:T(4,128)S(1)}) custom-call(s32[1,1024]{1,0:T(1,128)S(1)} %bitcast.50, bf16[272,768]{1,0:T(8,128)(2,1)S(1)} %collective-permute-done.10.here_ref, bf16[272,768]{1,0:T(8,128)(2,1)S(1)} %collective-permute-done.13.left_ref, bf16[272,768]{1,0:T(8,128)(2,1)S(1)} %collective-permute-done.12.right_ref, ...), custom_call_target="tpu_custom_call" | custom-call | flops 455114752 | bytes 6692864 | tf_op jit(solution)/shard_map/near/pallas_call | solution.py:342
  65.1 7.1 %collective-permute-done.14.previous_left_ref = bf16[272,768]{1,0:T(8,128)(2,1)S(1)} collective-permute-done((bf16[272,768]{1,0:T(8,128)(2,1)S(1)}, bf16[272,768]{1,0:T(8,128)(2,1)S(1)}, u32[]{:S(2)}, u32[]{:S(2)}) %collective-permute-start.14) | collective-permute-done | bytes 417824 | tf_op jit(solution)/shard_map/ppermute | solution.py:28
  72.3 0.7 far.1
  73.0 8.7 %all_to_all.25 = f32[4,2,128]{2,1,0:T(2,128)S(1)} all-to-all(f32[4,2,128]{2,1,0:T(2,128)S(1)} %bitcast.49), channel_id=1, replica_groups=mesh['rows'=128,'cent'=4] {'cent'}, dimensions={0} | all-to-all | bytes 8192 | tf_op jit(solution)/shard_map/all_to_all | solution.py:464
  81.7 0.6 reduce_max.46
  (21 shorter events, 0.1 us)
Async XLA Ops:
  0.6 5.3 %copy-start = (bf16[1024,768]{1,0:T(8,128)(2,1)S(1)}, bf16[1024,768]{1,0:T(8,128)(2,1)}, u32[]{:S(2)}) copy-start(bf16[1024,768]{1,0:T(8,128)(2,1)} %refs_2_.1) | copy-start | bytes 4718596
  0.6 5.3 %copy-start.2 = (s32[1024]{0:T(1024)S(1)}, s32[1024]{0:T(1024)}, u32[]{:S(2)}) copy-start(s32[1024]{0:T(1024)} %param.9) | copy-start | bytes 12292
  0.7 4.0 %copy-start.1 = (s32[4096]{0:T(1024)S(1)}, s32[4096]{0:T(1024)}, u32[]{:S(2)}) copy-start(s32[4096]{0:T(1024)} %param.10) | copy-start | bytes 49156
  6.0 34.6 %all-to-all-start = ((bf16[64,8,512]{2,1,0:T(8,128)(2,1)}), bf16[64,8,512]{2,1,0:T(8,128)(2,1)S(1)}, u32[]{:S(2)}, u32[]{:S(2)}) async-start(bf16[64,8,512]{2,1,0:T(8,128)(2,1)} %bitcast), calls=%async_computation | async-start | bytes 1048576 | tf_op jit(solution)/shard_map/cond/branch_0_fun/all_to_all | solution.py:398
  21.8 1.4 %copy-start.4 = (bf16[1024,768]{1,0:T(8,128)(2,1)S(1)}, bf16[1024,768]{1,0:T(8,128)(2,1)}, u32[]{:S(2)}) copy-start(bf16[1024,768]{1,0:T(8,128)(2,1)} %get-tuple-element.40) | copy-start | bytes 4718596 | tf_op jit(solution)/shard_map/cond
  25.3 10.2 %collective-permute-start.2 = (f32[2,1024]{1,0:T(2,128)S(1)}, f32[2,1024]{1,0:T(2,128)S(1)}, u32[]{:S(2)}, u32[]{:S(2)}) collective-permute-start(f32[2,1024]{1,0:T(2,128)S(1)} %pad_maximum_fusion), channel_id=1, source_target_pairs={{0,3},{1,0},{2,1},{3,2},{4,7},{5,4},{6,5},{7,6},{8,11},{9,8},{10,9... | collective-permute-start | bytes 24584 | tf_op jit(solution)/shard_map/cond/branch_0_fun/ppermute | solution.py:23
  30.0 7.1 %collective-permute-start.1 = (f32[2,1024]{1,0:T(2,128)S(1)}, f32[2,1024]{1,0:T(2,128)S(1)}, u32[]{:S(2)}, u32[]{:S(2)}) collective-permute-start(f32[2,1024]{1,0:T(2,128)S(1)} %pad_maximum_fusion), channel_id=1, source_target_pairs={{0,2},{1,3},{2,0},{3,1},{4,6},{5,7},{6,4},{7,5},{8,10},{9,11},{10,... | collective-permute-start | bytes 24584 | tf_op jit(solution)/shard_map/cond/branch_0_fun/ppermute | solution.py:23
  32.7 6.8 %collective-permute-start = (f32[2,1024]{1,0:T(2,128)S(1)}, f32[2,1024]{1,0:T(2,128)S(1)}, u32[]{:S(2)}, u32[]{:S(2)}) collective-permute-start(f32[2,1024]{1,0:T(2,128)S(1)} %pad_maximum_fusion), channel_id=1, source_target_pairs={{0,1},{1,2},{2,3},{3,0},{4,5},{5,6},{6,7},{7,4},{8,9},{9,10},{10,1... | collective-permute-start | bytes 24584 | tf_op jit(solution)/shard_map/cond/branch_0_fun/ppermute | solution.py:23
  42.5 39.7 %copy-start.3 = (f32[1024]{0:T(1024)}, f32[1024]{0:T(1024)S(1)}, u32[]{:S(2)}) copy-start(f32[1024]{0:T(1024)S(1)} %get-tuple-element.72) | copy-start | bytes 12292
  42.5 15.1 %collective-permute-start.13 = (bf16[272,768]{1,0:T(8,128)(2,1)}, bf16[272,768]{1,0:T(8,128)(2,1)S(1)}, u32[]{:S(2)}, u32[]{:S(2)}) collective-permute-start(bf16[272,768]{1,0:T(8,128)(2,1)} %get-tuple-element.80), channel_id=1, source_target_pairs={{0,1},{1,2},{2,7},{3,4},{4,5},{5,6},{6,3},{7,0},{8,9},{9,10},{10,1... | collective-permute-start | bytes 1253384 | tf_op jit(solution)/shard_map/ppermute | solution.py:40
  45.9 13.1 %collective-permute-start.12 = (bf16[272,768]{1,0:T(8,128)(2,1)}, bf16[272,768]{1,0:T(8,128)(2,1)S(1)}, u32[]{:S(2)}, u32[]{:S(2)}) collective-permute-start(bf16[272,768]{1,0:T(8,128)(2,1)} %get-tuple-element.80), channel_id=1, source_target_pairs={{0,3},{1,0},{2,5},{3,6},{4,7},{5,4},{6,1},{7,2},{8,11},{9,8},{10,1... | collective-permute-start | bytes 1253384 | tf_op jit(solution)/shard_map/ppermute | solution.py:40
  49.1 11.7 %collective-permute-start.11 = (bf16[272,768]{1,0:T(8,128)(2,1)}, bf16[272,768]{1,0:T(8,128)(2,1)S(1)}, u32[]{:S(2)}, u32[]{:S(2)}) collective-permute-start(bf16[272,768]{1,0:T(8,128)(2,1)} %get-tuple-element.80), channel_id=1, source_target_pairs={{0,4},{1,5},{2,10},{3,11},{4,8},{5,9},{6,6},{7,7},{8,12},{9,13},{1... | collective-permute-start | bytes 1253384 | tf_op jit(solution)/shard_map/ppermute | solution.py:40
  51.4 9.5 %collective-permute-start.10 = (bf16[272,768]{1,0:T(8,128)(2,1)}, bf16[272,768]{1,0:T(8,128)(2,1)S(1)}, u32[]{:S(2)}, u32[]{:S(2)}) collective-permute-start(bf16[272,768]{1,0:T(8,128)(2,1)} %get-tuple-element.80), channel_id=1, source_target_pairs={{0,0},{1,1},{2,6},{3,7},{4,4},{5,5},{6,2},{7,3},{8,8},{9,9},{10,14... | collective-permute-start | bytes 1253384 | tf_op jit(solution)/shard_map/ppermute | solution.py:40
  60.8 11.5 %collective-permute-start.14 = (bf16[272,768]{1,0:T(8,128)(2,1)S(1)}, bf16[272,768]{1,0:T(8,128)(2,1)S(1)}, u32[]{:S(2)}, u32[]{:S(2)}) collective-permute-start(bf16[272,768]{1,0:T(8,128)(2,1)S(1)} %collective-permute-done.13.left_ref), channel_id=1, source_target_pairs={{0,4},{4,8},{8,12},{12,16},{16,20},{20,24},{24,28},{28,32},{32,36}... | collective-permute-start | bytes 1253384 | tf_op jit(solution)/shard_map/ppermute | solution.py:28

commit v6 on v5

--- a/solution.py
+++ b/solution.py
@@ -433,13 +433,12 @@
     started = jnp.where(cluster_starts[None, :] <= places[:, None], cluster_starts[None, :], 0)
     starts = (jnp.max(started, axis=1) - base_place)[None, :]
 
+    right = from_holders(held, 3, 0)
+    left = from_holders(held, 1, 0)
+    held, starts = lax.optimization_barrier((held, starts))
     here = from_holders(held, 0, 0)
     previous_here = from_holders(held, 0, 1)
-    right = from_holders(held, 3, 0)
-    left = from_holders(held, 1, 0)
-    here, previous_here, right, left, starts = lax.optimization_barrier(
-        (here, previous_here, right, left, starts)
-    )
+    right, left, starts = lax.optimization_barrier((right, left, starts))
     previous_left = to_next_owner(left)
     best_shape = pltpu.VMEM((1, block_rows), jnp.float32)
     best, right_lines = whole_call(

time: 82.7 us -> 82.3 us (level)
  waiting for transfers between devices: 17.6 us -> 15.9 us
  blocking collectives: 8.67 us -> 9.95 us
    ppermute x1, waiting for transfers between devices: 7.13 us -> 4.98 us  [to_next_owner(): lax.ppermute(shard, 'rows', [(row, row + 1) for row in range(row_count -...]
    all_to_all x1, blocking collectives: 8.67 us -> 9.95 us  [on_device(): lax.all_to_all(best.reshape(cent_count, 2, quarter // 2), 'cent', split_a...]
where the time goes in v6:
time: 82.3 us; the launch traced here: 81.8 us
  starting transfers between devices  38.3 us (47%)
  waiting for transfers between devices  15.9 us (19%)
  blocking collectives  9.95 us (12%)
  Pallas kernels  9.04 us (11%)
  other arithmetic  3.71 us (5%)
  matrix products  2.08 us (3%)
  between operations  1.48 us (2%)
  local copies, waits for them, and re-layouts  1.24 us (2%)
    all_to_all x1, starting transfers between devices, by_pairs(): lax.all_to_all(packed, 'rows', split_axis=0, concat_axis=0, tiled=True, a...  15.8 us
    ppermute x4, starting transfers between devices, from_holders(): return lax.ppermute(shard, ('rows', 'cent'), pairs)  10.4 us
    ppermute x3, starting transfers between devices, rotated(): lax.ppermute(shard, axis, [(i, (i + by) % peers) for i in range(peers)])  10.2 us
    all_to_all x1, blocking collectives, on_device(): lax.all_to_all(best.reshape(cent_count, 2, quarter // 2), 'cent', split_a...  9.95 us
    ppermute x4, waiting for transfers between devices, from_holders(): return lax.ppermute(shard, ('rows', 'cent'), pairs)  5.89 us
    ppermute x1, waiting for transfers between devices, to_next_owner(): lax.ppermute(shard, 'rows', [(row, row + 1) for row in range(row_count -...  4.98 us
    pallas_call x1, Pallas kernels, pack_pairs(): pl.pallas_call(lambda *refs: pack_pairs_kernel(*refs, owner_rows=owner_ro...  3.97 us
    ppermute x3, waiting for transfers between devices, rotated(): lax.ppermute(shard, axis, [(i, (i + by) % peers) for i in range(peers)])  3.92 us
  transfers between devices with their start and end apart: 9, of which 7 were waited for; matrix products, arithmetic and copies ran while one was open for 6% of the time, Pallas kernels for 3%

profile of v6, /device:TPU:64, one launch (start us, length us, event | category | flops | bytes accessed | tf_op | source)
XLA Modules:
  0.0 81.8 jit_solution(10862712628864069827)
XLA Ops:
  0.7 4.0 %pack_pairs_5.1 = (bf16[512,512]{1,0:T(8,128)(2,1)}, s32[1]{0:T(128)}) custom-call(s32[1]{0:T(128)} %bitcast.33.refs_0_, s32[1]{0:T(128)} %bitcast.34.refs_1_, bf16[1024,768]{1,0:T(8,128)(2,1)} %refs_2_.1, s32[1,1024]{1,0:T(1,128)} %bitcast.52), custom_call_target="tpu_custom_call" | custom-call | tf_op jit(solution)/shard_map/pack_pairs_5/pallas_call | solution.py:139
  4.7 0.3 reduce-window.9
  4.9 0.1 slice.81
  5.0 0.1 reduce-window.12
  5.1 0.1 slice_reduce_fusion
  5.2 0.1 fusion.18
  6.0 36.5 %conditional.1 = (bf16[272,768]{1,0:T(8,128)(2,1)}, f32[1024]{0:T(1024)S(1)}) conditional(s32[]{:T(128)} %bitcast.36, (bf16[512,512]{1,0:T(8,128)(2,1)}, bf16[1024,768]{1,0:T(8,128)(2,1)S(1)}, bf16[1024,768]{1,0:T(8,128)(2,1)}, s32[1024]{0:T(1024)S(1)}, s32[1024]{0:T(1024)S(1)}, /*index=5*/s32[1024]{0:T(1024)S(1)}) %tuple.49, ...), branch_computations={%region_2.6_spmd, %region_6.10_spmd, %region_10.14_spmd} | conditional | flops 1621629952 | bytes 19341548 | solution.py:421
  6.0 15.8 %all-to-all-start = ((bf16[64,8,512]{2,1,0:T(8,128)(2,1)}), bf16[64,8,512]{2,1,0:T(8,128)(2,1)S(1)}, u32[]{:S(2)}, u32[]{:S(2)}) async-start(bf16[64,8,512]{2,1,0:T(8,128)(2,1)} %bitcast), calls=%async_computation | async-start | bytes 1048576 | tf_op jit(solution)/shard_map/cond/branch_0_fun/all_to_all | solution.py:398
  21.8 0.4 fusion
  22.2 1.0 %copy-done.4 = bf16[1024,768]{1,0:T(8,128)(2,1)S(1)} copy-done((bf16[1024,768]{1,0:T(8,128)(2,1)S(1)}, bf16[1024,768]{1,0:T(8,128)(2,1)}, u32[]{:S(2)}) %copy-start.4) | copy-done | bytes 1572888 | tf_op jit(solution)/shard_map/cond
  23.2 2.1 %fusion.15 = (f32[1024]{0:T(1024)S(1)}, f32[1024]{0:T(1024)S(1)}) fusion(s32[1024]{0:T(1024)S(1)} %get-tuple-element.43, s32[1024]{0:T(1024)S(1)} %get-tuple-element.42, s32[1024]{0:T(1024)S(1)} %get-tuple-element.41, bf16[1024,768]{1,0:T(8,128)(2,1)S(1)} %copy-done.4, bf16[1024,768]{1,0:T(8,128)(2,1)S(1)} %get-tuple-element.39, f32[1024]{0:T(1024)S(1)} %add_rsqrt_fusion), kind=kOutput, calls=%fused_computation.35 | convolution fusion | flops 1619261440 | bytes 3170304 | tf_op jit(solution)/shard_map/cond/branch_0_fun/dot_general | solution.py:354
  25.3 4.7 %collective-permute-start.2 = (f32[2,1024]{1,0:T(2,128)S(1)}, f32[2,1024]{1,0:T(2,128)S(1)}, u32[]{:S(2)}, u32[]{:S(2)}) collective-permute-start(f32[2,1024]{1,0:T(2,128)S(1)} %pad_maximum_fusion), channel_id=1, source_target_pairs={{0,3},{1,0},{2,1},{3,2},{4,7},{5,4},{6,5},{7,6},{8,11},{9,8},{10,9... | collective-permute-start | bytes 24584 | tf_op jit(solution)/shard_map/cond/branch_0_fun/ppermute | solution.py:23
  30.0 2.7 %collective-permute-start.1 = (f32[2,1024]{1,0:T(2,128)S(1)}, f32[2,1024]{1,0:T(2,128)S(1)}, u32[]{:S(2)}, u32[]{:S(2)}) collective-permute-start(f32[2,1024]{1,0:T(2,128)S(1)} %pad_maximum_fusion), channel_id=1, source_target_pairs={{0,2},{1,3},{2,0},{3,1},{4,6},{5,7},{6,4},{7,5},{8,10},{9,11},{10,... | collective-permute-start | bytes 24584 | tf_op jit(solution)/shard_map/cond/branch_0_fun/ppermute | solution.py:23
  32.7 2.8 %collective-permute-start = (f32[2,1024]{1,0:T(2,128)S(1)}, f32[2,1024]{1,0:T(2,128)S(1)}, u32[]{:S(2)}, u32[]{:S(2)}) collective-permute-start(f32[2,1024]{1,0:T(2,128)S(1)} %pad_maximum_fusion), channel_id=1, source_target_pairs={{0,1},{1,2},{2,3},{3,0},{4,5},{5,6},{6,7},{7,4},{8,9},{9,10},{10,1... | collective-permute-start | bytes 24584 | tf_op jit(solution)/shard_map/cond/branch_0_fun/ppermute | solution.py:23
  35.6 1.5 %collective-permute-done.1 = f32[2,1024]{1,0:T(2,128)S(1)} collective-permute-done((f32[2,1024]{1,0:T(2,128)S(1)}, f32[2,1024]{1,0:T(2,128)S(1)}, u32[]{:S(2)}, u32[]{:S(2)}) %collective-permute-start.1) | collective-permute-done | bytes 8224 | tf_op jit(solution)/shard_map/cond/branch_0_fun/ppermute | solution.py:23
  37.1 2.4 %collective-permute-done = f32[2,1024]{1,0:T(2,128)S(1)} collective-permute-done((f32[2,1024]{1,0:T(2,128)S(1)}, f32[2,1024]{1,0:T(2,128)S(1)}, u32[]{:S(2)}, u32[]{:S(2)}) %collective-permute-start) | collective-permute-done | bytes 8224 | tf_op jit(solution)/shard_map/cond/branch_0_fun/ppermute | solution.py:23
  39.5 1.1 %all-to-all-done = bf16[64,8,512]{2,1,0:T(8,128)(2,1)S(1)} async-done(((bf16[64,8,512]{2,1,0:T(8,128)(2,1)}), bf16[64,8,512]{2,1,0:T(8,128)(2,1)S(1)}, u32[]{:S(2)}, u32[]{:S(2)}) %all-to-all-start) | async-done | bytes 524320 | tf_op jit(solution)/shard_map/cond/branch_0_fun/all_to_all | solution.py:398
  40.6 2.0 %compact_pairs_5.1 = bf16[272,768]{1,0:T(8,128)(2,1)} custom-call(bf16[512,512]{1,0:T(8,128)(2,1)S(1)} %bitcast.48), custom_call_target="tpu_custom_call" | custom-call | tf_op jit(solution)/shard_map/cond/branch_0_fun/compact_pairs_5/pallas_call | solution.py:250
  42.5 3.4 %collective-permute-start.11 = (bf16[272,768]{1,0:T(8,128)(2,1)}, bf16[272,768]{1,0:T(8,128)(2,1)S(1)}, u32[]{:S(2)}, u32[]{:S(2)}) collective-permute-start(bf16[272,768]{1,0:T(8,128)(2,1)} %get-tuple-element.83), channel_id=1, source_target_pairs={{0,1},{1,2},{2,7},{3,4},{4,5},{5,6},{6,3},{7,0},{8,9},{9,10},{10,1... | collective-permute-start | bytes 1253384 | tf_op jit(solution)/shard_map/ppermute | solution.py:40
  45.9 3.2 %collective-permute-start.10 = (bf16[272,768]{1,0:T(8,128)(2,1)}, bf16[272,768]{1,0:T(8,128)(2,1)S(1)}, u32[]{:S(2)}, u32[]{:S(2)}) collective-permute-start(bf16[272,768]{1,0:T(8,128)(2,1)} %get-tuple-element.83), channel_id=1, source_target_pairs={{0,3},{1,0},{2,5},{3,6},{4,7},{5,4},{6,1},{7,2},{8,11},{9,8},{10,1... | collective-permute-start | bytes 1253384 | tf_op jit(solution)/shard_map/ppermute | solution.py:40
  49.2 2.3 %select_reduce_fusion.3 = s32[1024]{0:T(1024)S(1)} fusion(s32[4096]{0:T(1024)S(1)} %get-tuple-element.94, s32[1024]{0:T(1024)S(1)} %iota_add_fusion), kind=kLoop, calls=%fused_computation.30 | loop fusion | flops 12581888 | bytes 24576 | tf_op jit(solution)/shard_map/reduce_max | solution.py:434
  51.5 2.2 %collective-permute-start.13 = (bf16[272,768]{1,0:T(8,128)(2,1)}, bf16[272,768]{1,0:T(8,128)(2,1)S(1)}, u32[]{:S(2)}, u32[]{:S(2)}) collective-permute-start(bf16[272,768]{1,0:T(8,128)(2,1)} %get-tuple-element.83), channel_id=1, source_target_pairs={{0,4},{1,5},{2,10},{3,11},{4,8},{5,9},{6,6},{7,7},{8,12},{9,13},{1... | collective-permute-start | bytes 1253384 | tf_op jit(solution)/shard_map/ppermute | solution.py:40
  53.7 1.7 %collective-permute-start.12 = (bf16[272,768]{1,0:T(8,128)(2,1)}, bf16[272,768]{1,0:T(8,128)(2,1)S(1)}, u32[]{:S(2)}, u32[]{:S(2)}) collective-permute-start(bf16[272,768]{1,0:T(8,128)(2,1)} %get-tuple-element.83), channel_id=1, source_target_pairs={{0,0},{1,1},{2,6},{3,7},{4,4},{5,5},{6,2},{7,3},{8,8},{9,9},{10,14... | collective-permute-start | bytes 1253384 | tf_op jit(solution)/shard_map/ppermute | solution.py:40
  55.4 2.3 %collective-permute-done.11.left_ref = bf16[272,768]{1,0:T(8,128)(2,1)S(1)} collective-permute-done((bf16[272,768]{1,0:T(8,128)(2,1)}, bf16[272,768]{1,0:T(8,128)(2,1)S(1)}, u32[]{:S(2)}, u32[]{:S(2)}) %collective-permute-start.11) | collective-permute-done | bytes 417824 | tf_op jit(solution)/shard_map/ppermute | solution.py:40
  57.7 1.4 %collective-permute-done.10.right_ref = bf16[272,768]{1,0:T(8,128)(2,1)S(1)} collective-permute-done((bf16[272,768]{1,0:T(8,128)(2,1)}, bf16[272,768]{1,0:T(8,128)(2,1)S(1)}, u32[]{:S(2)}, u32[]{:S(2)}) %collective-permute-start.10) | collective-permute-done | bytes 417824 | tf_op jit(solution)/shard_map/ppermute | solution.py:40
  59.1 1.9 %collective-permute-start.14 = (bf16[272,768]{1,0:T(8,128)(2,1)S(1)}, bf16[272,768]{1,0:T(8,128)(2,1)S(1)}, u32[]{:S(2)}, u32[]{:S(2)}) collective-permute-start(bf16[272,768]{1,0:T(8,128)(2,1)S(1)} %collective-permute-done.11.left_ref), channel_id=1, source_target_pairs={{0,4},{4,8},{8,12},{12,16},{16,20},{20,24},{24,28},{28,32},{32,36}... | collective-permute-start | bytes 1253384 | tf_op jit(solution)/shard_map/ppermute | solution.py:28
  61.0 2.2 %collective-permute-done.13.previous_ref = bf16[272,768]{1,0:T(8,128)(2,1)S(1)} collective-permute-done((bf16[272,768]{1,0:T(8,128)(2,1)}, bf16[272,768]{1,0:T(8,128)(2,1)S(1)}, u32[]{:S(2)}, u32[]{:S(2)}) %collective-permute-start.13) | collective-permute-done | bytes 417824 | tf_op jit(solution)/shard_map/ppermute | solution.py:40
  63.2 2.4 %near.1 = (f32[1,1024]{1,0:T(1,128)S(1)}, f32[3,272]{1,0:T(4,128)S(1)}) custom-call(s32[1,1024]{1,0:T(1,128)S(1)} %bitcast.50, bf16[272,768]{1,0:T(8,128)(2,1)S(1)} %collective-permute-done.12.here_ref, bf16[272,768]{1,0:T(8,128)(2,1)S(1)} %collective-permute-done.11.left_ref, bf16[272,768]{1,0:T(8,128)(2,1)S(1)} %collective-permute-done.10.right_ref, ...), custom_call_target="tpu_custom_call" | custom-call | flops 455114752 | bytes 6692864 | tf_op jit(solution)/shard_map/near/pallas_call | solution.py:342
  65.6 5.0 %collective-permute-done.14.previous_left_ref = bf16[272,768]{1,0:T(8,128)(2,1)S(1)} collective-permute-done((bf16[272,768]{1,0:T(8,128)(2,1)S(1)}, bf16[272,768]{1,0:T(8,128)(2,1)S(1)}, u32[]{:S(2)}, u32[]{:S(2)}) %collective-permute-start.14) | collective-permute-done | bytes 417824 | tf_op jit(solution)/shard_map/ppermute | solution.py:28
  70.5 0.7 far.1
  71.3 9.9 %all_to_all.25 = f32[4,2,128]{2,1,0:T(2,128)S(1)} all-to-all(f32[4,2,128]{2,1,0:T(2,128)S(1)} %bitcast.49), channel_id=1, replica_groups=mesh['rows'=128,'cent'=4] {'cent'}, dimensions={0} | all-to-all | bytes 8192 | tf_op jit(solution)/shard_map/all_to_all | solution.py:463
  81.2 0.6 reduce_max.46
  (21 shorter events, 0.1 us)
Async XLA Ops:
  0.6 5.3 %copy-start = (bf16[1024,768]{1,0:T(8,128)(2,1)S(1)}, bf16[1024,768]{1,0:T(8,128)(2,1)}, u32[]{:S(2)}) copy-start(bf16[1024,768]{1,0:T(8,128)(2,1)} %refs_2_.1) | copy-start | bytes 4718596
  0.6 5.3 %copy-start.2 = (s32[1024]{0:T(1024)S(1)}, s32[1024]{0:T(1024)}, u32[]{:S(2)}) copy-start(s32[1024]{0:T(1024)} %param.9) | copy-start | bytes 12292
  0.7 4.0 %copy-start.1 = (s32[4096]{0:T(1024)S(1)}, s32[4096]{0:T(1024)}, u32[]{:S(2)}) copy-start(s32[4096]{0:T(1024)} %param.10) | copy-start | bytes 49156
  6.0 34.6 %all-to-all-start = ((bf16[64,8,512]{2,1,0:T(8,128)(2,1)}), bf16[64,8,512]{2,1,0:T(8,128)(2,1)S(1)}, u32[]{:S(2)}, u32[]{:S(2)}) async-start(bf16[64,8,512]{2,1,0:T(8,128)(2,1)} %bitcast), calls=%async_computation | async-start | bytes 1048576 | tf_op jit(solution)/shard_map/cond/branch_0_fun/all_to_all | solution.py:398
  21.8 1.4 %copy-start.4 = (bf16[1024,768]{1,0:T(8,128)(2,1)S(1)}, bf16[1024,768]{1,0:T(8,128)(2,1)}, u32[]{:S(2)}) copy-start(bf16[1024,768]{1,0:T(8,128)(2,1)} %get-tuple-element.40) | copy-start | bytes 4718596 | tf_op jit(solution)/shard_map/cond
  25.3 10.2 %collective-permute-start.2 = (f32[2,1024]{1,0:T(2,128)S(1)}, f32[2,1024]{1,0:T(2,128)S(1)}, u32[]{:S(2)}, u32[]{:S(2)}) collective-permute-start(f32[2,1024]{1,0:T(2,128)S(1)} %pad_maximum_fusion), channel_id=1, source_target_pairs={{0,3},{1,0},{2,1},{3,2},{4,7},{5,4},{6,5},{7,6},{8,11},{9,8},{10,9... | collective-permute-start | bytes 24584 | tf_op jit(solution)/shard_map/cond/branch_0_fun/ppermute | solution.py:23
  30.0 7.1 %collective-permute-start.1 = (f32[2,1024]{1,0:T(2,128)S(1)}, f32[2,1024]{1,0:T(2,128)S(1)}, u32[]{:S(2)}, u32[]{:S(2)}) collective-permute-start(f32[2,1024]{1,0:T(2,128)S(1)} %pad_maximum_fusion), channel_id=1, source_target_pairs={{0,2},{1,3},{2,0},{3,1},{4,6},{5,7},{6,4},{7,5},{8,10},{9,11},{10,... | collective-permute-start | bytes 24584 | tf_op jit(solution)/shard_map/cond/branch_0_fun/ppermute | solution.py:23
  32.7 6.8 %collective-permute-start = (f32[2,1024]{1,0:T(2,128)S(1)}, f32[2,1024]{1,0:T(2,128)S(1)}, u32[]{:S(2)}, u32[]{:S(2)}) collective-permute-start(f32[2,1024]{1,0:T(2,128)S(1)} %pad_maximum_fusion), channel_id=1, source_target_pairs={{0,1},{1,2},{2,3},{3,0},{4,5},{5,6},{6,7},{7,4},{8,9},{9,10},{10,1... | collective-permute-start | bytes 24584 | tf_op jit(solution)/shard_map/cond/branch_0_fun/ppermute | solution.py:23
  42.5 39.2 %copy-start.3 = (f32[1024]{0:T(1024)}, f32[1024]{0:T(1024)S(1)}, u32[]{:S(2)}) copy-start(f32[1024]{0:T(1024)S(1)} %get-tuple-element.72) | copy-start | bytes 12292
  42.5 15.1 %collective-permute-start.11 = (bf16[272,768]{1,0:T(8,128)(2,1)}, bf16[272,768]{1,0:T(8,128)(2,1)S(1)}, u32[]{:S(2)}, u32[]{:S(2)}) collective-permute-start(bf16[272,768]{1,0:T(8,128)(2,1)} %get-tuple-element.83), channel_id=1, source_target_pairs={{0,1},{1,2},{2,7},{3,4},{4,5},{5,6},{6,3},{7,0},{8,9},{9,10},{10,1... | collective-permute-start | bytes 1253384 | tf_op jit(solution)/shard_map/ppermute | solution.py:40
  45.9 13.1 %collective-permute-start.10 = (bf16[272,768]{1,0:T(8,128)(2,1)}, bf16[272,768]{1,0:T(8,128)(2,1)S(1)}, u32[]{:S(2)}, u32[]{:S(2)}) collective-permute-start(bf16[272,768]{1,0:T(8,128)(2,1)} %get-tuple-element.83), channel_id=1, source_target_pairs={{0,3},{1,0},{2,5},{3,6},{4,7},{5,4},{6,1},{7,2},{8,11},{9,8},{10,1... | collective-permute-start | bytes 1253384 | tf_op jit(solution)/shard_map/ppermute | solution.py:40
  51.5 11.7 %collective-permute-start.13 = (bf16[272,768]{1,0:T(8,128)(2,1)}, bf16[272,768]{1,0:T(8,128)(2,1)S(1)}, u32[]{:S(2)}, u32[]{:S(2)}) collective-permute-start(bf16[272,768]{1,0:T(8,128)(2,1)} %get-tuple-element.83), channel_id=1, source_target_pairs={{0,4},{1,5},{2,10},{3,11},{4,8},{5,9},{6,6},{7,7},{8,12},{9,13},{1... | collective-permute-start | bytes 1253384 | tf_op jit(solution)/shard_map/ppermute | solution.py:40
  53.7 9.5 %collective-permute-start.12 = (bf16[272,768]{1,0:T(8,128)(2,1)}, bf16[272,768]{1,0:T(8,128)(2,1)S(1)}, u32[]{:S(2)}, u32[]{:S(2)}) collective-permute-start(bf16[272,768]{1,0:T(8,128)(2,1)} %get-tuple-element.83), channel_id=1, source_target_pairs={{0,0},{1,1},{2,6},{3,7},{4,4},{5,5},{6,2},{7,3},{8,8},{9,9},{10,14... | collective-permute-start | bytes 1253384 | tf_op jit(solution)/shard_map/ppermute | solution.py:40
  59.1 11.5 %collective-permute-start.14 = (bf16[272,768]{1,0:T(8,128)(2,1)S(1)}, bf16[272,768]{1,0:T(8,128)(2,1)S(1)}, u32[]{:S(2)}, u32[]{:S(2)}) collective-permute-start(bf16[272,768]{1,0:T(8,128)(2,1)S(1)} %collective-permute-done.11.left_ref), channel_id=1, source_target_pairs={{0,4},{4,8},{8,12},{12,16},{16,20},{20,24},{24,28},{28,32},{32,36}... | collective-permute-start | bytes 1253384 | tf_op jit(solution)/shard_map/ppermute | solution.py:28

commit v7 on v6

--- a/solution.py
+++ b/solution.py
@@ -301,31 +301,56 @@
     return jnp.maximum(best, jnp.max(placed, axis=0, keepdims=True))
 
 
-def near_kernel(starts_ref, here_ref, left_ref, right_ref, previous_ref, best_ref, right_lines_ref):
+def lines_of_starts(starts_ref):
     owner_rows = starts_ref.shape[1]
     starts = starts_ref[...] + owner_rows
     line = iota((16, owner_rows), 0)
-    start_lines = jnp.where(line == 0, starts // 64, jnp.where(line == 1, starts % 64, 0))
-    start_lines = start_lines.astype(jnp.float32).astype(jnp.bfloat16)
+    lines = jnp.where(line == 0, starts // 64, jnp.where(line == 1, starts % 64, 0))
+    return lines.astype(jnp.float32).astype(jnp.bfloat16)
+
+
+def store_lines(lines_ref, first, best, places, starts):
+    lines_ref[first : first + 1, :] = best
+    lines_ref[first + 1 : first + 2, :] = places.astype(jnp.float32)
+    lines_ref[first + 2 : first + 3, :] = starts.astype(jnp.float32)
+
+
+def early_kernel(starts_ref, here_ref, left_ref, previous_ref, lines_ref):
+    owner_rows = starts_ref.shape[1]
+    start_lines = lines_of_starts(starts_ref)
     here = (here_ref, place_column(here_ref))
     left = (left_ref, place_column(left_ref))
-    right = (right_ref, place_column(right_ref))
     previous = (previous_ref, place_column(previous_ref) - owner_rows)
-    placed = jnp.full((1, owner_rows), -1.0, jnp.float32)
-    for queries_ref, keys in (
-        (here_ref, (here, left, right, previous)),
-        (left_ref, (right, previous)),
-        (right_ref, (previous,)),
+    least = jnp.full((1, PART), -1.0, jnp.float32)
+    for first, queries_ref, keys in (
+        (0, here_ref, (here, left, previous)),
+        (3, left_ref, (previous,)),
     ):
         places = place_row(queries_ref)
         starts = start_row(places, start_lines)
-        best = compared(jnp.full((1, PART), -1.0, jnp.float32), queries_ref, places, starts, keys)
-        if queries_ref is not right_ref:
-            placed = at_places(placed, places, best)
+        best = compared(least, queries_ref, places, starts, keys)
+        store_lines(lines_ref, first, best, places, starts)
+
+
+def near_kernel(
+    starts_ref, early_ref, here_ref, left_ref, right_ref, previous_ref, best_ref, right_lines_ref
+):
+    owner_rows = starts_ref.shape[1]
+    right = (right_ref, place_column(right_ref))
+    placed = jnp.full((1, owner_rows), -1.0, jnp.float32)
+    for first, queries_ref in ((0, here_ref), (3, left_ref)):
+        places = early_ref[first + 1 : first + 2, :].astype(jnp.int32)
+        starts = early_ref[first + 2 : first + 3, :].astype(jnp.int32)
+        best = early_ref[first : first + 1, :]
+        best = compared(best, queries_ref, places, starts, (right,))
+        placed = at_places(placed, places, best)
     best_ref[...] = placed
-    right_lines_ref[0:1, :] = best
-    right_lines_ref[1:2, :] = places.astype(jnp.float32)
-    right_lines_ref[2:3, :] = starts.astype(jnp.float32)
+    places = place_row(right_ref)
+    starts = start_row(places, lines_of_starts(starts_ref))
+    previous = (previous_ref, place_column(previous_ref) - owner_rows)
+    least = jnp.full((1, PART), -1.0, jnp.float32)
+    best = compared(least, right_ref, places, starts, (previous,))
+    store_lines(right_lines_ref, 0, best, places, starts)
 
 
 def far_kernel(best_ref, right_lines_ref, right_ref, previous_left_ref, out_ref):
@@ -430,22 +455,36 @@
     )
     base_place = row_index * block_rows
     places = base_place + jnp.arange(block_rows, dtype=jnp.int32)
-    started = jnp.where(cluster_starts[None, :] <= places[:, None], cluster_starts[None, :], 0)
-    starts = (jnp.max(started, axis=1) - base_place)[None, :]
-
+    def starts_of(some):
+        started = jnp.where(cluster_starts[None, :] <= some[:, None], cluster_starts[None, :], 0)
+        return (jnp.max(started, axis=1) - base_place)[None, :]
+
+    first_starts, other_starts = starts_of(places[:LANES]), starts_of(places[LANES:])
+    left = from_holders(held, 1, 0)
+    held, first_starts = lax.optimization_barrier((held, first_starts))
     right = from_holders(held, 3, 0)
-    left = from_holders(held, 1, 0)
-    held, starts = lax.optimization_barrier((held, starts))
+    held, other_starts = lax.optimization_barrier((held, other_starts))
     here = from_holders(held, 0, 0)
     previous_here = from_holders(held, 0, 1)
-    right, left, starts = lax.optimization_barrier((right, left, starts))
+    starts = jnp.concatenate([first_starts, other_starts], axis=1)
+    left, starts = lax.optimization_barrier((left, starts))
     previous_left = to_next_owner(left)
     best_shape = pltpu.VMEM((1, block_rows), jnp.float32)
+    early = whole_call(
+        early_kernel,
+        pltpu.VMEM((6, PART), jnp.float32),
+        "early",
+        starts,
+        here,
+        left,
+        previous_here,
+    )
     best, right_lines = whole_call(
         near_kernel,
         (best_shape, pltpu.VMEM((3, PART), jnp.float32)),
         "near",
         starts,
+        early,
         here,
         left,
         right,

time: 82.3 us -> 80.8 us (0.982)
  the two profiles are of different devices: /device:TPU:64 before, /device:TPU:8 now
where the time goes in v7:
time: 80.8 us; the launch traced here: 80.3 us
  starting transfers between devices  40.2 us (50%)
  waiting for transfers between devices  12.2 us (15%)
  blocking collectives  9.81 us (12%)
  Pallas kernels  9.3 us (12%)
  other arithmetic  3.86 us (5%)
  matrix products  2.08 us (3%)
  between operations  1.47 us (2%)
  local copies, waits for them, and re-layouts  1.25 us (2%)
    all_to_all x1, starting transfers between devices, by_pairs(): lax.all_to_all(packed, 'rows', split_axis=0, concat_axis=0, tiled=True, a...  16.6 us
    ppermute x4, starting transfers between devices, from_holders(): return lax.ppermute(shard, ('rows', 'cent'), pairs)  11.4 us
    ppermute x3, starting transfers between devices, rotated(): lax.ppermute(shard, axis, [(i, (i + by) % peers) for i in range(peers)])  10.2 us
    all_to_all x1, blocking collectives, on_device(): lax.all_to_all(best.reshape(cent_count, 2, quarter // 2), 'cent', split_a...  9.81 us
    ppermute x4, waiting for transfers between devices, from_holders(): return lax.ppermute(shard, ('rows', 'cent'), pairs)  6.58 us
    pallas_call x1, Pallas kernels, pack_pairs(): pl.pallas_call(lambda *refs: pack_pairs_kernel(*refs, owner_rows=owner_ro...  3.99 us
    ppermute x3, waiting for transfers between devices, rotated(): lax.ppermute(shard, axis, [(i, (i + by) % peers) for i in range(peers)])  3.92 us
    pallas_call x3, Pallas kernels, whole_call(): pl.pallas_call(kernel, in_specs=[pl.BlockSpec(memory_space=pltpu.VMEM)] *...  3.36 us
  transfers between devices with their start and end apart: 9, of which 5 were waited for; matrix products, arithmetic and copies ran while one was open for 6% of the time, Pallas kernels for 3%

profile of v7, /device:TPU:8, one launch (start us, length us, event | category | flops | bytes accessed | tf_op | source)
XLA Modules:
  0.0 80.3 jit_solution(9938773146152517954)
XLA Ops:
  0.7 4.0 %pack_pairs_5.1 = (bf16[512,512]{1,0:T(8,128)(2,1)}, s32[1]{0:T(128)}) custom-call(s32[1]{0:T(128)} %bitcast.33.refs_0_, s32[1]{0:T(128)} %bitcast.34.refs_1_, bf16[1024,768]{1,0:T(8,128)(2,1)} %refs_2_.1, s32[1,1024]{1,0:T(1,128)} %bitcast.52), custom_call_target="tpu_custom_call" | custom-call | tf_op jit(solution)/shard_map/pack_pairs_5/pallas_call | solution.py:139
  4.7 0.3 reduce-window.9
  5.0 0.1 slice.89
  5.0 0.1 reduce-window.12
  5.1 0.1 slice_reduce_fusion
  5.2 0.1 fusion.18
  5.9 38.0 %conditional.1 = (bf16[272,768]{1,0:T(8,128)(2,1)}, f32[1024]{0:T(1024)S(1)}) conditional(s32[]{:T(128)} %bitcast.36, (bf16[512,512]{1,0:T(8,128)(2,1)}, bf16[1024,768]{1,0:T(8,128)(2,1)S(1)}, bf16[1024,768]{1,0:T(8,128)(2,1)}, s32[1024]{0:T(1024)S(1)}, s32[1024]{0:T(1024)S(1)}, /*index=5*/s32[1024]{0:T(1024)S(1)}) %tuple.51, ...), branch_computations={%region_2.6_spmd, %region_6.10_spmd, %region_10.14_spmd} | conditional | flops 1621629952 | bytes 19341548 | solution.py:446
  5.9 16.6 %all-to-all-start = ((bf16[64,8,512]{2,1,0:T(8,128)(2,1)}), bf16[64,8,512]{2,1,0:T(8,128)(2,1)S(1)}, u32[]{:S(2)}, u32[]{:S(2)}) async-start(bf16[64,8,512]{2,1,0:T(8,128)(2,1)} %bitcast), calls=%async_computation | async-start | bytes 1048576 | tf_op jit(solution)/shard_map/cond/branch_0_fun/all_to_all | solution.py:423
  22.6 0.4 fusion
  22.9 1.0 %copy-done.4 = bf16[1024,768]{1,0:T(8,128)(2,1)S(1)} copy-done((bf16[1024,768]{1,0:T(8,128)(2,1)S(1)}, bf16[1024,768]{1,0:T(8,128)(2,1)}, u32[]{:S(2)}) %copy-start.4) | copy-done | bytes 1572888 | tf_op jit(solution)/shard_map/cond
  24.0 2.1 %fusion.15 = (f32[1024]{0:T(1024)S(1)}, f32[1024]{0:T(1024)S(1)}) fusion(s32[1024]{0:T(1024)S(1)} %get-tuple-element.43, s32[1024]{0:T(1024)S(1)} %get-tuple-element.42, s32[1024]{0:T(1024)S(1)} %get-tuple-element.41, bf16[1024,768]{1,0:T(8,128)(2,1)S(1)} %copy-done.4, bf16[1024,768]{1,0:T(8,128)(2,1)S(1)} %get-tuple-element.39, f32[1024]{0:T(1024)S(1)} %add_rsqrt_fusion), kind=kOutput, calls=%fused_computation.38 | convolution fusion | flops 1619261440 | bytes 3170304 | tf_op jit(solution)/shard_map/cond/branch_0_fun/dot_general | solution.py:379
  26.1 4.7 %collective-permute-start.2 = (f32[2,1024]{1,0:T(2,128)S(1)}, f32[2,1024]{1,0:T(2,128)S(1)}, u32[]{:S(2)}, u32[]{:S(2)}) collective-permute-start(f32[2,1024]{1,0:T(2,128)S(1)} %pad_maximum_fusion), channel_id=1, source_target_pairs={{0,3},{1,0},{2,1},{3,2},{4,7},{5,4},{6,5},{7,6},{8,11},{9,8},{10,9... | collective-permute-start | bytes 24584 | tf_op jit(solution)/shard_map/cond/branch_0_fun/ppermute | solution.py:23
  30.7 2.7 %collective-permute-start.1 = (f32[2,1024]{1,0:T(2,128)S(1)}, f32[2,1024]{1,0:T(2,128)S(1)}, u32[]{:S(2)}, u32[]{:S(2)}) collective-permute-start(f32[2,1024]{1,0:T(2,128)S(1)} %pad_maximum_fusion), channel_id=1, source_target_pairs={{0,2},{1,3},{2,0},{3,1},{4,6},{5,7},{6,4},{7,5},{8,10},{9,11},{10,... | collective-permute-start | bytes 24584 | tf_op jit(solution)/shard_map/cond/branch_0_fun/ppermute | solution.py:23
  33.5 2.8 %collective-permute-start = (f32[2,1024]{1,0:T(2,128)S(1)}, f32[2,1024]{1,0:T(2,128)S(1)}, u32[]{:S(2)}, u32[]{:S(2)}) collective-permute-start(f32[2,1024]{1,0:T(2,128)S(1)} %pad_maximum_fusion), channel_id=1, source_target_pairs={{0,1},{1,2},{2,3},{3,0},{4,5},{5,6},{6,7},{7,4},{8,9},{9,10},{10,1... | collective-permute-start | bytes 24584 | tf_op jit(solution)/shard_map/cond/branch_0_fun/ppermute | solution.py:23
  36.3 1.5 %collective-permute-done.1 = f32[2,1024]{1,0:T(2,128)S(1)} collective-permute-done((f32[2,1024]{1,0:T(2,128)S(1)}, f32[2,1024]{1,0:T(2,128)S(1)}, u32[]{:S(2)}, u32[]{:S(2)}) %collective-permute-start.1) | collective-permute-done | bytes 8224 | tf_op jit(solution)/shard_map/cond/branch_0_fun/ppermute | solution.py:23
  37.8 2.4 %collective-permute-done = f32[2,1024]{1,0:T(2,128)S(1)} collective-permute-done((f32[2,1024]{1,0:T(2,128)S(1)}, f32[2,1024]{1,0:T(2,128)S(1)}, u32[]{:S(2)}, u32[]{:S(2)}) %collective-permute-start) | collective-permute-done | bytes 8224 | tf_op jit(solution)/shard_map/cond/branch_0_fun/ppermute | solution.py:23
  40.2 1.7 %all-to-all-done = bf16[64,8,512]{2,1,0:T(8,128)(2,1)S(1)} async-done(((bf16[64,8,512]{2,1,0:T(8,128)(2,1)}), bf16[64,8,512]{2,1,0:T(8,128)(2,1)S(1)}, u32[]{:S(2)}, u32[]{:S(2)}) %all-to-all-start) | async-done | bytes 524320 | tf_op jit(solution)/shard_map/cond/branch_0_fun/all_to_all | solution.py:423
  41.9 2.0 %compact_pairs_5.1 = bf16[272,768]{1,0:T(8,128)(2,1)} custom-call(bf16[512,512]{1,0:T(8,128)(2,1)S(1)} %bitcast.49), custom_call_target="tpu_custom_call" | custom-call | tf_op jit(solution)/shard_map/cond/branch_0_fun/compact_pairs_5/pallas_call | solution.py:250
  43.9 3.4 %collective-permute-start.10 = (bf16[272,768]{1,0:T(8,128)(2,1)}, bf16[272,768]{1,0:T(8,128)(2,1)S(1)}, u32[]{:S(2)}, u32[]{:S(2)}) collective-permute-start(bf16[272,768]{1,0:T(8,128)(2,1)} %get-tuple-element.86), channel_id=1, source_target_pairs={{0,1},{1,2},{2,7},{3,4},{4,5},{5,6},{6,3},{7,0},{8,9},{9,10},{10,1... | collective-permute-start | bytes 1253384 | tf_op jit(solution)/shard_map/ppermute | solution.py:40
  47.3 2.0 %select_reduce_fusion.3 = s32[896]{0:T(1024)S(1)} fusion(s32[4096]{0:T(1024)S(1)} %get-tuple-element.96, s32[896]{0:T(1024)S(1)} %slice.70), kind=kLoop, calls=%fused_computation.30 | loop fusion | flops 11009152 | bytes 23552 | tf_op jit(solution)/shard_map/reduce_max | solution.py:460
  49.4 0.4 select_reduce_fusion.4
  49.8 1.9 %collective-permute-start.12 = (bf16[272,768]{1,0:T(8,128)(2,1)}, bf16[272,768]{1,0:T(8,128)(2,1)S(1)}, u32[]{:S(2)}, u32[]{:S(2)}) collective-permute-start(bf16[272,768]{1,0:T(8,128)(2,1)} %get-tuple-element.86), channel_id=1, source_target_pairs={{0,4},{1,5},{2,10},{3,11},{4,8},{5,9},{6,6},{7,7},{8,12},{9,13},{1... | collective-permute-start | bytes 1253384 | tf_op jit(solution)/shard_map/ppermute | solution.py:40
  51.8 1.7 %collective-permute-start.11 = (bf16[272,768]{1,0:T(8,128)(2,1)}, bf16[272,768]{1,0:T(8,128)(2,1)S(1)}, u32[]{:S(2)}, u32[]{:S(2)}) collective-permute-start(bf16[272,768]{1,0:T(8,128)(2,1)} %get-tuple-element.86), channel_id=1, source_target_pairs={{0,0},{1,1},{2,6},{3,7},{4,4},{5,5},{6,2},{7,3},{8,8},{9,9},{10,14... | collective-permute-start | bytes 1253384 | tf_op jit(solution)/shard_map/ppermute | solution.py:40
  53.4 4.5 %collective-permute-start.13 = (bf16[272,768]{1,0:T(8,128)(2,1)}, bf16[272,768]{1,0:T(8,128)(2,1)S(1)}, u32[]{:S(2)}, u32[]{:S(2)}) collective-permute-start(bf16[272,768]{1,0:T(8,128)(2,1)} %get-tuple-element.86), channel_id=1, source_target_pairs={{0,3},{1,0},{2,5},{3,6},{4,7},{5,4},{6,1},{7,2},{8,11},{9,8},{10,1... | collective-permute-start | bytes 1253384 | tf_op jit(solution)/shard_map/ppermute | solution.py:40
  57.9 1.1 %collective-permute-done.10.left_ref = bf16[272,768]{1,0:T(8,128)(2,1)S(1)} collective-permute-done((bf16[272,768]{1,0:T(8,128)(2,1)}, bf16[272,768]{1,0:T(8,128)(2,1)S(1)}, u32[]{:S(2)}, u32[]{:S(2)}) %collective-permute-start.10) | collective-permute-done | bytes 417824 | tf_op jit(solution)/shard_map/ppermute | solution.py:40
  59.0 2.0 %collective-permute-start.14 = (bf16[272,768]{1,0:T(8,128)(2,1)S(1)}, bf16[272,768]{1,0:T(8,128)(2,1)S(1)}, u32[]{:S(2)}, u32[]{:S(2)}) collective-permute-start(bf16[272,768]{1,0:T(8,128)(2,1)S(1)} %collective-permute-done.10.left_ref), channel_id=1, source_target_pairs={{0,4},{4,8},{8,12},{12,16},{16,20},{20,24},{24,28},{28,32},{32,36}... | collective-permute-start | bytes 1253384 | tf_op jit(solution)/shard_map/ppermute | solution.py:28
  61.1 1.4 %early.1.early_ref = f32[6,272]{1,0:T(8,128)S(1)} custom-call(s32[1,1024]{1,0:T(1,128)S(1)} %pad_add_fusion.starts_ref, bf16[272,768]{1,0:T(8,128)(2,1)S(1)} %collective-permute-done.11.here_ref, bf16[272,768]{1,0:T(8,128)(2,1)S(1)} %collective-permute-done.10.left_ref, bf16[272,768]{1,0:T(8,128)(2,1)S(1)} %collective-permute-done.12.previous_ref), custom_call_target="tpu_custom_call" | custom-call | flops 341475328 | bytes 5021696 | tf_op jit(solution)/shard_map/early/pallas_call | solution.py:367
  62.4 5.4 %collective-permute-done.13.right_ref = bf16[272,768]{1,0:T(8,128)(2,1)S(1)} collective-permute-done((bf16[272,768]{1,0:T(8,128)(2,1)}, bf16[272,768]{1,0:T(8,128)(2,1)S(1)}, u32[]{:S(2)}, u32[]{:S(2)}) %collective-permute-start.13) | collective-permute-done | bytes 417824 | tf_op jit(solution)/shard_map/ppermute | solution.py:40
  67.9 1.3 %near.1 = (f32[1,1024]{1,0:T(1,128)S(1)}, f32[3,272]{1,0:T(4,128)S(1)}) custom-call(s32[1,1024]{1,0:T(1,128)S(1)} %pad_add_fusion.starts_ref, f32[6,272]{1,0:T(8,128)S(1)} %early.1.early_ref, bf16[272,768]{1,0:T(8,128)(2,1)S(1)} %collective-permute-done.11.here_ref, bf16[272,768]{1,0:T(8,128)(2,1)S(1)} %collective-permute-done.10.left_ref, ...), custom_call_target="tpu_custom_call" | custom-call | flops 456002560 | bytes 6705920 | tf_op jit(solution)/shard_map/near/pallas_call | solution.py:367
  69.2 0.7 far.1
  69.9 9.8 %all_to_all.25 = f32[4,2,128]{2,1,0:T(2,128)S(1)} all-to-all(f32[4,2,128]{2,1,0:T(2,128)S(1)} %bitcast.50), channel_id=1, replica_groups=mesh['rows'=128,'cent'=4] {'cent'}, dimensions={0} | all-to-all | bytes 8192 | tf_op jit(solution)/shard_map/all_to_all | solution.py:502
  79.7 0.6 reduce_max.56
  (28 shorter events, 0.1 us)
Async XLA Ops:
  0.6 5.3 %copy-start = (bf16[1024,768]{1,0:T(8,128)(2,1)S(1)}, bf16[1024,768]{1,0:T(8,128)(2,1)}, u32[]{:S(2)}) copy-start(bf16[1024,768]{1,0:T(8,128)(2,1)} %refs_2_.1) | copy-start | bytes 4718596
  0.6 5.3 %copy-start.2 = (s32[1024]{0:T(1024)S(1)}, s32[1024]{0:T(1024)}, u32[]{:S(2)}) copy-start(s32[1024]{0:T(1024)} %param.9) | copy-start | bytes 12292
  0.7 4.0 %copy-start.1 = (s32[4096]{0:T(1024)S(1)}, s32[4096]{0:T(1024)}, u32[]{:S(2)}) copy-start(s32[4096]{0:T(1024)} %param.10) | copy-start | bytes 49156
  5.9 36.0 %all-to-all-start = ((bf16[64,8,512]{2,1,0:T(8,128)(2,1)}), bf16[64,8,512]{2,1,0:T(8,128)(2,1)S(1)}, u32[]{:S(2)}, u32[]{:S(2)}) async-start(bf16[64,8,512]{2,1,0:T(8,128)(2,1)} %bitcast), calls=%async_computation | async-start | bytes 1048576 | tf_op jit(solution)/shard_map/cond/branch_0_fun/all_to_all | solution.py:423
  22.5 1.4 %copy-start.4 = (bf16[1024,768]{1,0:T(8,128)(2,1)S(1)}, bf16[1024,768]{1,0:T(8,128)(2,1)}, u32[]{:S(2)}) copy-start(bf16[1024,768]{1,0:T(8,128)(2,1)} %get-tuple-element.40) | copy-start | bytes 4718596 | tf_op jit(solution)/shard_map/cond
  26.1 10.2 %collective-permute-start.2 = (f32[2,1024]{1,0:T(2,128)S(1)}, f32[2,1024]{1,0:T(2,128)S(1)}, u32[]{:S(2)}, u32[]{:S(2)}) collective-permute-start(f32[2,1024]{1,0:T(2,128)S(1)} %pad_maximum_fusion), channel_id=1, source_target_pairs={{0,3},{1,0},{2,1},{3,2},{4,7},{5,4},{6,5},{7,6},{8,11},{9,8},{10,9... | collective-permute-start | bytes 24584 | tf_op jit(solution)/shard_map/cond/branch_0_fun/ppermute | solution.py:23
  30.7 7.1 %collective-permute-start.1 = (f32[2,1024]{1,0:T(2,128)S(1)}, f32[2,1024]{1,0:T(2,128)S(1)}, u32[]{:S(2)}, u32[]{:S(2)}) collective-permute-start(f32[2,1024]{1,0:T(2,128)S(1)} %pad_maximum_fusion), channel_id=1, source_target_pairs={{0,2},{1,3},{2,0},{3,1},{4,6},{5,7},{6,4},{7,5},{8,10},{9,11},{10,... | collective-permute-start | bytes 24584 | tf_op jit(solution)/shard_map/cond/branch_0_fun/ppermute | solution.py:23
  33.5 6.8 %collective-permute-start = (f32[2,1024]{1,0:T(2,128)S(1)}, f32[2,1024]{1,0:T(2,128)S(1)}, u32[]{:S(2)}, u32[]{:S(2)}) collective-permute-start(f32[2,1024]{1,0:T(2,128)S(1)} %pad_maximum_fusion), channel_id=1, source_target_pairs={{0,1},{1,2},{2,3},{3,0},{4,5},{5,6},{6,7},{7,4},{8,9},{9,10},{10,1... | collective-permute-start | bytes 24584 | tf_op jit(solution)/shard_map/cond/branch_0_fun/ppermute | solution.py:23
  43.9 26.0 %copy-start.3 = (f32[1024]{0:T(1024)}, f32[1024]{0:T(1024)S(1)}, u32[]{:S(2)}) copy-start(f32[1024]{0:T(1024)S(1)} %get-tuple-element.73) | copy-start | bytes 12292
  43.9 15.1 %collective-permute-start.10 = (bf16[272,768]{1,0:T(8,128)(2,1)}, bf16[272,768]{1,0:T(8,128)(2,1)S(1)}, u32[]{:S(2)}, u32[]{:S(2)}) collective-permute-start(bf16[272,768]{1,0:T(8,128)(2,1)} %get-tuple-element.86), channel_id=1, source_target_pairs={{0,1},{1,2},{2,7},{3,4},{4,5},{5,6},{6,3},{7,0},{8,9},{9,10},{10,1... | collective-permute-start | bytes 1253384 | tf_op jit(solution)/shard_map/ppermute | solution.py:40
  49.8 11.2 %collective-permute-start.12 = (bf16[272,768]{1,0:T(8,128)(2,1)}, bf16[272,768]{1,0:T(8,128)(2,1)S(1)}, u32[]{:S(2)}, u32[]{:S(2)}) collective-permute-start(bf16[272,768]{1,0:T(8,128)(2,1)} %get-tuple-element.86), channel_id=1, source_target_pairs={{0,4},{1,5},{2,10},{3,11},{4,8},{5,9},{6,6},{7,7},{8,12},{9,13},{1... | collective-permute-start | bytes 1253384 | tf_op jit(solution)/shard_map/ppermute | solution.py:40
  51.8 9.3 %collective-permute-start.11 = (bf16[272,768]{1,0:T(8,128)(2,1)}, bf16[272,768]{1,0:T(8,128)(2,1)S(1)}, u32[]{:S(2)}, u32[]{:S(2)}) collective-permute-start(bf16[272,768]{1,0:T(8,128)(2,1)} %get-tuple-element.86), channel_id=1, source_target_pairs={{0,0},{1,1},{2,6},{3,7},{4,4},{5,5},{6,2},{7,3},{8,8},{9,9},{10,14... | collective-permute-start | bytes 1253384 | tf_op jit(solution)/shard_map/ppermute | solution.py:40
  53.4 14.5 %collective-permute-start.13 = (bf16[272,768]{1,0:T(8,128)(2,1)}, bf16[272,768]{1,0:T(8,128)(2,1)S(1)}, u32[]{:S(2)}, u32[]{:S(2)}) collective-permute-start(bf16[272,768]{1,0:T(8,128)(2,1)} %get-tuple-element.86), channel_id=1, source_target_pairs={{0,3},{1,0},{2,5},{3,6},{4,7},{5,4},{6,1},{7,2},{8,11},{9,8},{10,1... | collective-permute-start | bytes 1253384 | tf_op jit(solution)/shard_map/ppermute | solution.py:40
  59.0 10.1 %collective-permute-start.14 = (bf16[272,768]{1,0:T(8,128)(2,1)S(1)}, bf16[272,768]{1,0:T(8,128)(2,1)S(1)}, u32[]{:S(2)}, u32[]{:S(2)}) collective-permute-start(bf16[272,768]{1,0:T(8,128)(2,1)S(1)} %collective-permute-done.10.left_ref), channel_id=1, source_target_pairs={{0,4},{4,8},{8,12},{12,16},{16,20},{20,24},{24,28},{28,32},{32,36}... | collective-permute-start | bytes 1253384 | tf_op jit(solution)/shard_map/ppermute | solution.py:28
